TPU v7x, 32 devices: a whole 2x2x4 slice. The times are simulated.
32 devices in a mesh: kx: 4 (over y, x), ky: 4 (over z), kz: 2 (over core).
Axes of the slice: x: 2, y: 2, z: 4, core: 2. Of those that a mesh axis runs over, the one named last changes fastest.
Arguments:
- orbitals: bfloat16 [16, 16, 2, 1024, 128], P('kx', 'ky', 'kz'), may hold values from -6 to 6
- kernel: bfloat16 [32, 2, 1024, 1024], P(('kx', 'ky', 'kz')), may hold values from -0.00015258789 to 0.00015258789
- plan: int32 [2, 2, 32], replicated, may hold values from 0 to 15, as said below
- occupation: int32 [16, 16, 2, 64], replicated, may hold values 0 or 1
Outputs:
- exchange_blocks: float32 [16, 16, 2, 64, 128], P('kx', 'ky', 'kz')
Inputs may be any that keep to these rules, and one draw needn't show every extreme that they name: `plan`: entry [r, 0, e] is the slot, in device e's block of 4 x 4 x 1 k-points, of the k-point that e sends as k in round r, and [r, 1, e] the slot of the one it sends as p. For every owner, k minus p is the same momentum transfer on the periodic k-mesh in every round.
All inputs are finite; a program needn't handle non-finite values.
Results may differ from a plain program's by a relative error of at most 0.004.
Values may be sent and summed in bfloat16 or wider, within the bound.
No kernel may reach another device: no remote copies, remote signals or barrier semaphores. Data moves between devices by JAX's collectives and lax.ppermute only.
A program may use at most 128 MiB of HBM per device.

v0:
```python
import jax
import jax.numpy as jnp
from jax import lax
from jax.sharding import PartitionSpec as P


def shifted(block, axis, distance):
    devices = range(lax.axis_size(axis))
    route = [((i - distance) % len(devices), i) for i in devices]
    return lax.ppermute(block, axis, route)


def hop_shifts(turn_number, mesh_counts):
    forward = (
        (turn_number + 1) % mesh_counts[0],
        (2 * turn_number + 1) % mesh_counts[1],
        (3 * turn_number + 1) % mesh_counts[2],
    )
    partner = (forward[0], forward[1], (forward[2] - mesh_counts[2] // 2) % mesh_counts[2])
    return (forward, partner)


def negated(shift, mesh_counts):
    return (-shift[0] % mesh_counts[0], -shift[1] % mesh_counts[1], -shift[2] % mesh_counts[2])


def global_points(plan, turn_number, column, shift, owner_coords, mesh_counts, cell_counts):
    sender_first = (owner_coords[0] - shift[0]) % mesh_counts[0]
    sender_second = (owner_coords[1] - shift[1]) % mesh_counts[1]
    sender_third = (owner_coords[2] - shift[2]) % mesh_counts[2]
    linear = (sender_first * mesh_counts[1] + sender_second) * mesh_counts[2] + sender_third
    slot_index = plan[turn_number, column, linear]
    cell_first = slot_index // (cell_counts[1] * cell_counts[2])
    cell_second = slot_index // cell_counts[2] % cell_counts[1]
    cell_third = slot_index % cell_counts[2]
    return (
        sender_first * cell_counts[0] + cell_first,
        sender_second * cell_counts[1] + cell_second,
        sender_third * cell_counts[2] + cell_third,
    )


def density_product(orbital, occupied):
    bands = orbital.shape[1] // 2
    weights = jnp.concatenate([occupied, occupied]).astype(orbital.dtype)
    masked = orbital * weights[None, :]
    swapped = jnp.concatenate([-orbital[:, bands:], orbital[:, :bands]], axis=1)
    density_real = jnp.dot(masked, orbital.T, preferred_element_type=jnp.float32)
    density_imag = jnp.dot(masked, swapped.T, preferred_element_type=jnp.float32)
    return (density_real, density_imag)


def kernel_hadamard(kernel_real, kernel_imag, density_real, density_imag, conjugate_sign):
    weight_real = kernel_real.astype(jnp.float32)
    weight_imag = kernel_imag.astype(jnp.float32) * conjugate_sign
    hadamard_real = weight_real * density_real - weight_imag * density_imag
    hadamard_imag = weight_real * density_imag + weight_imag * density_real
    return jnp.concatenate([hadamard_real, hadamard_imag], axis=1).astype(jnp.bfloat16)


def exchange_block(stacked, orbital):
    bands = orbital.shape[1] // 2
    real_part = orbital[:, :bands]
    imag_part = orbital[:, bands:]
    blocked = jnp.concatenate([orbital, jnp.concatenate([-imag_part, real_part], axis=1)], axis=0)
    mixture = jnp.dot(stacked, blocked, preferred_element_type=jnp.float32).astype(jnp.bfloat16)
    gram_matrix = lax.dot_general(
        orbital, mixture, (((0,), (0,)), ((), ())), preferred_element_type=jnp.float32
    )
    result_real = -(gram_matrix[:bands, :bands] + gram_matrix[bands:, bands:])
    result_imag = -(gram_matrix[:bands, bands:] - gram_matrix[bands:, :bands])
    return jnp.concatenate([result_real, result_imag], axis=1)


def pair_blocks(
    kernel_real, kernel_imag, orbital_first, occupied_first, orbital_second, occupied_second
):
    second_real, second_imag = density_product(orbital_second, occupied_second)
    first_block = exchange_block(
        kernel_hadamard(kernel_real, kernel_imag, second_real, second_imag, 1.0), orbital_first
    )
    first_real, first_imag = density_product(orbital_first, occupied_first)
    second_block = exchange_block(
        kernel_hadamard(kernel_real, kernel_imag, first_real, first_imag, -1.0), orbital_second
    )
    return (first_block, second_block)


def orbit_hops(payload, amounts):
    payload = shifted(payload, "kx", amounts[0])
    payload = shifted(payload, "ky", amounts[1])
    if amounts[2]:
        payload = shifted(payload, "kz", amounts[2])
    return payload


def return_hops(payload, amounts):
    payload = shifted(payload, "kx", amounts[0])
    payload = shifted(payload, "ky", amounts[1])
    if amounts[2]:
        payload = shifted(payload, "kz", amounts[2])
    return payload


def on_device(orbitals, kernel, plan, occupation):
    mesh_counts = (lax.axis_size("kx"), lax.axis_size("ky"), lax.axis_size("kz"))
    places = (lax.axis_index("kx"), lax.axis_index("ky"), lax.axis_index("kz"))
    own_linear = (places[0] * mesh_counts[1] + places[1]) * mesh_counts[2] + places[2]
    cell_counts = orbitals.shape[:3]
    point_total = cell_counts[0] * cell_counts[1] * cell_counts[2]
    local_orbitals = orbitals.reshape(point_total, orbitals.shape[3], orbitals.shape[4])
    bands = orbitals.shape[4] // 2
    kernel_real = kernel[0, 0]
    kernel_imag = kernel[0, 1]
    slot_numbers = jnp.arange(point_total, dtype=jnp.int32)
    totals = jnp.zeros((point_total, bands, 2 * bands), jnp.float32)
    for turn_number in range(plan.shape[0]):
        forward, partner = hop_shifts(turn_number, mesh_counts)
        first_slot = plan[turn_number, 0, own_linear]
        second_slot = plan[turn_number, 1, own_linear]
        first_send = lax.dynamic_index_in_dim(local_orbitals, first_slot, 0, keepdims=False)
        second_send = lax.dynamic_index_in_dim(local_orbitals, second_slot, 0, keepdims=False)
        sectioned = shifted(second_send, "kz", mesh_counts[2] // 2)
        arrived = orbit_hops(jnp.stack([first_send, sectioned]), forward)
        first_orbital = arrived[0]
        second_orbital = arrived[1]
        first_point = global_points(plan, turn_number, 0, forward, places, mesh_counts, cell_counts)
        second_point = global_points(
            plan, turn_number, 1, partner, places, mesh_counts, cell_counts
        )
        first_occupied = occupation[first_point[0], first_point[1], first_point[2]]
        second_occupied = occupation[second_point[0], second_point[1], second_point[2]]
        first_block, second_block = pair_blocks(
            kernel_real, kernel_imag, first_orbital, first_occupied, second_orbital, second_occupied
        )
        returned_first = return_hops(first_block, negated(forward, mesh_counts))
        returned_second = return_hops(second_block, negated(partner, mesh_counts))
        first_pick = (slot_numbers == first_slot).astype(jnp.float32)[:, None, None]
        second_pick = (slot_numbers == second_slot).astype(jnp.float32)[:, None, None]
        totals = totals + first_pick * returned_first[None] + second_pick * returned_second[None]
    return totals.reshape(cell_counts[0], cell_counts[1], cell_counts[2], bands, 2 * bands)


def solution(mesh):
    placed = (P("kx", "ky", "kz", None, None), P(("kx", "ky", "kz"), None, None, None), P(), P())
    return jax.shard_map(
        on_device,
        mesh=mesh,
        in_specs=placed,
        out_specs=P("kx", "ky", "kz", None, None),
        check_vma=False,
    )
```

profile of v0, /device:TPU:0, one launch (start us, length us, event | category | flops | bytes accessed | tf_op | source)
XLA Modules:
  0.0 126.5 jit_solution(7851860119670819292)
XLA Ops:
  0.0 1.5 %constant_dynamic-slice_fusion.8 = (s32[1,1,1]{2,1,0:T(1,128)}, s32[1,1,1]{2,1,0:T(1,128)}, s32[1,1,1]{2,1,0:T(1,128)}, s32[1,1,1]{2,1,0:T(1,128)}, s32[1,1,1]{2...) fusion(s32[2,2,32]{2,1,0:T(2,128)} %param.6, s32[]{:T(128)S(6)} %select_n.149, ...), kind=kLoop, calls=%fused_computation.162 | loop fusion | bytes 84 | tf_op jit(solution)/shard_map/dynamic_slice | solution.py:32
  9.0 1.3 %constant_dynamic-slice_fusion.10 = (bf16[1,1024,128]{2,1,0:T(8,128)(2,1)S(1)}, bf16[1024,128]{1,0:T(8,128)(2,1)S(1)}, bf16[1,1024,128]{2,1,0:T(8,128)(2,1)S(1)}, bf16[1024,128]{1,0:T(8,128)(2,1)S(1)}) fusion(bf16[16,1024,128]{2,1,0:T(8,128)(2,1)} %bitcast.85, s32[]{:T(128)S(6)} %select_n.144, s32[]{:T(128)S(6)} %select_n.163, s32[]{:T(128)S(6)} %select_n.162, ...), kind=kLoop, calls=%fused_computation.164 | loop fusion | bytes 2097168 | tf_op jit(solution)/shard_map/jit(dynamic_index_in_dim)/dynamic_slice | solution.py:121
  10.3 0.6 collective-permute-start.9
  10.8 1.2 collective-permute-done.9
  12.1 3.0 %collective-permute-start.10 = (bf16[2,1024,128]{2,1,0:T(8,128)(2,1)S(1)}, bf16[2,1024,128]{2,1,0:T(8,128)(2,1)}, u32[]{:S(2)}, u32[]{:S(2)}) collective-permute-start(bf16[2,1024,128]{2,1,0:T(8,128)(2,1)S(1)} %pad_maximum_fusion.1), channel_id=1, source_target_pairs={{16,0},{24,8},{0,16},{8,24},{17,1},{25,9},{1,17},{9,25},{18,2},{26... | collective-permute-start | bytes 1572872 | tf_op jit(solution)/shard_map/ppermute | solution.py:10
  25.1 1.5 %collective-permute-start.1 = (bf16[2,1024,128]{2,1,0:T(8,128)(2,1)S(1)}, bf16[2,1024,128]{2,1,0:T(8,128)(2,1)}, u32[]{:S(2)}, u32[]{:S(2)}) collective-permute-start(bf16[2,1024,128]{2,1,0:T(8,128)(2,1)S(1)} %pad_maximum_fusion), channel_id=1, source_target_pairs={{24,0},{0,8},{8,16},{16,24},{25,1},{1,9},{9,17},{17,25},{26,2},{2,... | collective-permute-start | bytes 1572872 | tf_op jit(solution)/shard_map/ppermute | solution.py:10
  26.6 0.7 fusion.161
  27.4 3.8 %collective-permute-start.11 = (bf16[2,1024,128]{2,1,0:T(8,128)(2,1)}, bf16[2,1024,128]{2,1,0:T(8,128)(2,1)S(1)}, u32[]{:S(2)}, u32[]{:S(2)}) collective-permute-start(bf16[2,1024,128]{2,1,0:T(8,128)(2,1)} %collective-permute-done.10), channel_id=1, source_target_pairs={{2,0},{4,2},{6,4},{0,6},{3,1},{5,3},{7,5},{1,7},{10,8},{12,10},{14... | collective-permute-start | bytes 1572872 | tf_op jit(solution)/shard_map/ppermute | solution.py:10
  31.2 0.1 pad_maximum_fusion.8
  31.2 4.7 %fusion.180 = (bf16[1,1,1024,1024]{3,2,1,0:T(8,128)(2,1)}, bf16[1,1,1024,1024]{3,2,1,0:T(8,128)(2,1)}) fusion(bf16[1,2,1024,1024]{3,2,1,0:T(8,128)(2,1)} %param.5), kind=kLoop, calls=%fused_computation.197 | loop fusion | bytes 8388608 | tf_op jit(solution)/shard_map/slice | solution.py:113
  35.9 4.6 %collective-permute-done.1 = bf16[2,1024,128]{2,1,0:T(8,128)(2,1)} collective-permute-done((bf16[2,1024,128]{2,1,0:T(8,128)(2,1)S(1)}, bf16[2,1024,128]{2,1,0:T(8,128)(2,1)}, u32[]{:S(2)}, u32[]{:S(2)}) %collective-permute-start.1) | collective-permute-done | bytes 524320 | tf_op jit(solution)/shard_map/ppermute | solution.py:10
  40.5 1.5 %collective-permute-start.2 = (bf16[2,1024,128]{2,1,0:T(8,128)(2,1)}, bf16[2,1024,128]{2,1,0:T(8,128)(2,1)}, u32[]{:S(2)}, u32[]{:S(2)}) collective-permute-start(bf16[2,1024,128]{2,1,0:T(8,128)(2,1)} %collective-permute-done.1), channel_id=1, source_target_pairs={{6,0},{0,2},{2,4},{4,6},{7,1},{1,3},{3,5},{5,7},{14,8},{8,10},{10,... | collective-permute-start | bytes 1572872 | tf_op jit(solution)/shard_map/ppermute | solution.py:10
  42.1 2.9 %copy.7 = bf16[1,1,1024,1024]{2,3,1,0:T(8,128)(2,1)S(1)} copy(bf16[1,1,1024,1024]{3,2,1,0:T(8,128)(2,1)} %get-tuple-element.23) | data formatting | bytes 4194304
  45.0 4.0 %copy.8 = bf16[1,1,1024,1024]{2,3,1,0:T(8,128)(2,1)} copy(bf16[1,1,1024,1024]{3,2,1,0:T(8,128)(2,1)} %get-tuple-element.24) | data formatting | bytes 4194304
  49.0 0.2 slice_negate_fusion
  49.3 0.5 copy-done
  49.7 6.4 %collective-permute-done.2 = bf16[2,1024,128]{2,1,0:T(8,128)(2,1)} collective-permute-done((bf16[2,1024,128]{2,1,0:T(8,128)(2,1)}, bf16[2,1024,128]{2,1,0:T(8,128)(2,1)}, u32[]{:S(2)}, u32[]{:S(2)}) %collective-permute-start.2) | collective-permute-done | bytes 524320 | tf_op jit(solution)/shard_map/ppermute | solution.py:10
  56.1 2.8 %fusion.116 = f32[1024,1024]{0,1:T(8,128)} fusion(bf16[2,1024,128]{2,1,0:T(8,128)(2,1)S(1)} %collective-permute-done.11, bf16[128]{0:T(256)(128)(2,1)S(1)} %get-tuple-element.62), kind=kOutput, calls=%fused_computation.100 | convolution fusion | flops 268566528 | bytes 4718848 | tf_op jit(solution)/shard_map/dot_general | solution.py:48
  58.9 2.7 %fusion.112 = f32[1024,1024]{0,1:T(8,128)} fusion(bf16[1024,64]{1,0:T(8,128)(2,1)S(1)} %get-tuple-element.40, bf16[1024,64]{1,0:T(8,128)(2,1)S(1)} %get-tuple-element.39, bf16[128]{0:T(256)(128)(2,1)S(1)} %get-tuple-element.62, bf16[2,1024,128]{2,1,0:T(8,128)(2,1)S(1)} %collective-permute-done.11), kind=kOutput, calls=%fused_computation.96 | convolution fusion | flops 269090816 | bytes 4981248 | tf_op jit(solution)/shard_map/dot_general | solution.py:49
  61.6 2.8 %fusion.108 = f32[1024,1024]{0,1:T(8,128)} fusion(bf16[1024,64]{1,0:T(8,128)(2,1)S(1)} %get-tuple-element.57, bf16[1024,64]{1,0:T(8,128)(2,1)S(1)} %get-tuple-element.58, bf16[128]{0:T(256)(128)(2,1)S(1)} %get-tuple-element.61, bf16[2,1024,128]{2,1,0:T(8,128)(2,1)S(1)} %collective-permute-done.11), kind=kOutput, calls=%fused_computation.92 | convolution fusion | flops 269090816 | bytes 4981248 | tf_op jit(solution)/shard_map/dot_general | solution.py:49
  64.4 2.7 %fusion.118 = f32[1024,1024]{0,1:T(8,128)} fusion(bf16[2,1024,128]{2,1,0:T(8,128)(2,1)S(1)} %collective-permute-done.11, bf16[128]{0:T(256)(128)(2,1)S(1)} %get-tuple-element.61), kind=kOutput, calls=%fused_computation.102 | convolution fusion | flops 268566528 | bytes 4718848 | tf_op jit(solution)/shard_map/dot_general | solution.py:48
  67.1 0.1 slice_negate_fusion.2
  67.3 0.9 slice_negate_fusion.3
  68.2 2.7 %fusion.120 = f32[1024,1024]{0,1:T(8,128)} fusion(bf16[2,1024,128]{2,1,0:T(8,128)(2,1)S(1)} %collective-permute-done.3, bf16[128]{0:T(256)(128)(2,1)S(1)} %get-tuple-element.60), kind=kOutput, calls=%fused_computation.104 | convolution fusion | flops 268566528 | bytes 4718848 | tf_op jit(solution)/shard_map/dot_general | solution.py:48
  71.0 2.7 %fusion.122 = f32[1024,1024]{0,1:T(8,128)} fusion(bf16[2,1024,128]{2,1,0:T(8,128)(2,1)S(1)} %collective-permute-done.3, bf16[128]{0:T(256)(128)(2,1)S(1)} %get-tuple-element.59), kind=kOutput, calls=%fused_computation.106 | convolution fusion | flops 268566528 | bytes 4718848 | tf_op jit(solution)/shard_map/dot_general | solution.py:48
  73.6 2.8 %fusion.104 = f32[1024,1024]{0,1:T(8,128)} fusion(bf16[1024,64]{1,0:T(8,128)(2,1)S(1)} %get-tuple-element.36, bf16[1024,64]{1,0:T(8,128)(2,1)S(1)} %get-tuple-element.35, bf16[128]{0:T(256)(128)(2,1)S(1)} %get-tuple-element.60, bf16[2,1024,128]{2,1,0:T(8,128)(2,1)S(1)} %collective-permute-done.3), kind=kOutput, calls=%fused_computation.88 | convolution fusion | flops 269090816 | bytes 4981248 | tf_op jit(solution)/shard_map/dot_general | solution.py:49
  76.4 16.2 %fusion.13 = (bf16[1024,1024]{0,1:T(8,128)(2,1)}, bf16[1024,1024]{0,1:T(8,128)(2,1)}, bf16[1024,1024]{0,1:T(8,128)(2,1)}, bf16[1024,1024]{0,1:T(8,128)(2,1)}, bf...) fusion(f32[1024,1024]{0,1:T(8,128)} %fusion.122, ...), kind=kOutput, calls=%fused_computation.26 | convolution fusion | flops 305790976 | bytes 50856448 | tf_op jit(solution)/shard_map/dot_general | solution.py:49
  92.7 4.0 %fusion.49 = f32[128,128]{1,0:T(8,128)S(1)} fusion(bf16[1024,128]{1,0:T(8,128)(2,1)S(1)} %get-tuple-element.25, bf16[1024,1024]{0,1:T(8,128)(2,1)} %get-tuple-element.6, bf16[1024,1024]{0,1:T(8,128)(2,1)} %get-tuple-element.5, bf16[1024,64]{1,0:T(8,128)(2,1)} %copy-done.6, bf16[1024,64]{1,0:T(8,128)(2,1)} %copy-done.5), kind=kOutput, calls=%fused_computation.53 | convolution fusion | flops 580517888 | bytes 4784128 | tf_op jit(solution)/shard_map/dot_general | solution.py:67
  96.7 0.1 fusion.151
  96.8 0.1 pad_maximum_fusion.2
  96.8 0.7 collective-permute-start.4
  97.6 3.2 %fusion.52 = f32[128,128]{1,0:T(8,128)S(1)} fusion(bf16[1024,128]{1,0:T(8,128)(2,1)S(1)} %get-tuple-element.26, bf16[1024,1024]{0,1:T(8,128)(2,1)S(1)} %copy-done.3, bf16[1024,1024]{0,1:T(8,128)(2,1)} %get-tuple-element.16, bf16[1024,64]{1,0:T(8,128)(2,1)} %get-tuple-element.34, bf16[1024,64]{1,0:T(8,128)(2,1)S(1)} %copy-done.4), kind=kOutput, calls=%fused_computation.54 | convolution fusion | flops 580517888 | bytes 4784128 | tf_op jit(solution)/shard_map/dot_general | solution.py:67
  100.8 0.1 fusion.149
  101.0 1.4 %collective-permute-start.7 = (f32[64,128]{1,0:T(8,128)S(1)}, f32[64,128]{1,0:T(8,128)S(1)}, u32[]{:S(2)}, u32[]{:S(2)}) collective-permute-start(f32[64,128]{1,0:T(8,128)S(1)} %pad_maximum_fusion.3), channel_id=1, source_target_pairs={{8,0},{16,8},{24,16},{0,24},{9,1},{17,9},{25,17},{1,25},{10,2},{18... | collective-permute-start | bytes 98312 | tf_op jit(solution)/shard_map/ppermute | solution.py:10
  102.4 4.0 %fusion.55 = f32[128,128]{1,0:T(8,128)S(1)} fusion(bf16[1024,128]{1,0:T(8,128)(2,1)S(1)} %copy-done.1, bf16[1024,1024]{0,1:T(8,128)(2,1)} %get-tuple-element.13, bf16[1024,1024]{0,1:T(8,128)(2,1)} %get-tuple-element.14, bf16[1024,64]{1,0:T(8,128)(2,1)} %copy-done.12, bf16[1024,64]{1,0:T(8,128)(2,1)} %copy-done.11), kind=kOutput, calls=%fused_computation.55 | convolution fusion | flops 580517888 | bytes 4784128 | tf_op jit(solution)/shard_map/dot_general | solution.py:67
  106.4 0.1 fusion.147
  106.5 3.2 %fusion.58 = f32[128,128]{1,0:T(8,128)S(1)} fusion(bf16[1024,128]{1,0:T(8,128)(2,1)S(1)} %get-tuple-element.28, bf16[1024,1024]{0,1:T(8,128)(2,1)S(1)} %copy-done.2, bf16[1024,1024]{0,1:T(8,128)(2,1)} %get-tuple-element.18, bf16[1024,64]{1,0:T(8,128)(2,1)S(1)} %copy-done.8, bf16[1024,64]{1,0:T(8,128)(2,1)S(1)} %copy-done.10), kind=kOutput, calls=%fused_computation.56 | convolution fusion | flops 580517888 | bytes 4784128 | tf_op jit(solution)/shard_map/dot_general | solution.py:67
  109.7 0.1 fusion.145
  109.9 1.5 %collective-permute-start.14 = (f32[64,128]{1,0:T(8,128)S(1)}, f32[64,128]{1,0:T(8,128)S(1)}, u32[]{:S(2)}, u32[]{:S(2)}) collective-permute-start(f32[64,128]{1,0:T(8,128)S(1)} %pad_maximum_fusion.5), channel_id=1, source_target_pairs={{16,0},{24,8},{0,16},{8,24},{17,1},{25,9},{1,17},{9,25},{18,2},{26... | collective-permute-start | bytes 98312 | tf_op jit(solution)/shard_map/ppermute | solution.py:10
  111.5 0.5 collective-permute-start.12
  112.0 2.6 %collective-permute-start.5 = (f32[64,128]{1,0:T(8,128)S(1)}, f32[64,128]{1,0:T(8,128)S(1)}, u32[]{:S(2)}, u32[]{:S(2)}) collective-permute-start(f32[64,128]{1,0:T(8,128)S(1)} %collective-permute-done.4), channel_id=1, source_target_pairs={{2,0},{4,2},{6,4},{0,6},{3,1},{5,3},{7,5},{1,7},{10,8},{12,10},{14... | collective-permute-start | bytes 98312 | tf_op jit(solution)/shard_map/ppermute | solution.py:10
  114.6 0.1 collective-permute-start.15
  114.8 1.3 fusion.156
  116.0 3.7 %collective-permute-start.8 = (f32[64,128]{1,0:T(8,128)S(1)}, f32[64,128]{1,0:T(8,128)S(1)}, u32[]{:S(2)}, u32[]{:S(2)}) collective-permute-start(f32[64,128]{1,0:T(8,128)S(1)} %collective-permute-done.7), channel_id=1, source_target_pairs={{2,0},{4,2},{6,4},{0,6},{3,1},{5,3},{7,5},{1,7},{10,8},{12,10},{14... | collective-permute-start | bytes 98312 | tf_op jit(solution)/shard_map/ppermute | solution.py:10
  119.9 0.5 collective-permute-done.15
  120.4 1.2 fusion.158
  121.6 3.9 %collective-permute-done.13 = f32[64,128]{1,0:T(8,128)S(1)} collective-permute-done((f32[64,128]{1,0:T(8,128)S(1)}, f32[64,128]{1,0:T(8,128)S(1)}, u32[]{:S(2)}, u32[]{:S(2)}) %collective-permute-start.13) | collective-permute-done | bytes 32800 | tf_op jit(solution)/shard_map/ppermute | solution.py:10
  125.5 1.0 multiply_add_fusion
  (50 shorter events, 0.7 us)
Async XLA Ops:
  10.3 1.7 %collective-permute-start.9 = (bf16[1024,128]{1,0:T(8,128)(2,1)S(1)}, bf16[1024,128]{1,0:T(8,128)(2,1)S(1)}, u32[]{:S(2)}, u32[]{:S(2)}) collective-permute-start(bf16[1024,128]{1,0:T(8,128)(2,1)S(1)} %get-tuple-element.20), channel_id=1, source_target_pairs={{1,0},{0,1},{3,2},{2,3},{5,4},{4,5},{7,6},{6,7},{9,8},{8,9},{11,10... | collective-permute-start | bytes 786440 | tf_op jit(solution)/shard_map/ppermute | solution.py:10
  12.1 15.3 %collective-permute-start.10 = (bf16[2,1024,128]{2,1,0:T(8,128)(2,1)S(1)}, bf16[2,1024,128]{2,1,0:T(8,128)(2,1)}, u32[]{:S(2)}, u32[]{:S(2)}) collective-permute-start(bf16[2,1024,128]{2,1,0:T(8,128)(2,1)S(1)} %pad_maximum_fusion.1), channel_id=1, source_target_pairs={{16,0},{24,8},{0,16},{8,24},{17,1},{25,9},{1,17},{9,25},{18,2},{26... | collective-permute-start | bytes 1572872 | tf_op jit(solution)/shard_map/ppermute | solution.py:10
  15.0 10.0 %collective-permute-start = (bf16[1024,128]{1,0:T(8,128)(2,1)S(1)}, bf16[1024,128]{1,0:T(8,128)(2,1)S(1)}, u32[]{:S(2)}, u32[]{:S(2)}) collective-permute-start(bf16[1024,128]{1,0:T(8,128)(2,1)S(1)} %get-tuple-element.22), channel_id=1, source_target_pairs={{1,0},{0,1},{3,2},{2,3},{5,4},{4,5},{7,6},{6,7},{9,8},{8,9},{11,10... | collective-permute-start | bytes 786440 | tf_op jit(solution)/shard_map/ppermute | solution.py:10
  25.1 15.4 %collective-permute-start.1 = (bf16[2,1024,128]{2,1,0:T(8,128)(2,1)S(1)}, bf16[2,1024,128]{2,1,0:T(8,128)(2,1)}, u32[]{:S(2)}, u32[]{:S(2)}) collective-permute-start(bf16[2,1024,128]{2,1,0:T(8,128)(2,1)S(1)} %pad_maximum_fusion), channel_id=1, source_target_pairs={{24,0},{0,8},{8,16},{16,24},{25,1},{1,9},{9,17},{17,25},{26,2},{2,... | collective-permute-start | bytes 1572872 | tf_op jit(solution)/shard_map/ppermute | solution.py:10
  27.4 21.6 %collective-permute-start.11 = (bf16[2,1024,128]{2,1,0:T(8,128)(2,1)}, bf16[2,1024,128]{2,1,0:T(8,128)(2,1)S(1)}, u32[]{:S(2)}, u32[]{:S(2)}) collective-permute-start(bf16[2,1024,128]{2,1,0:T(8,128)(2,1)} %collective-permute-done.10), channel_id=1, source_target_pairs={{2,0},{4,2},{6,4},{0,6},{3,1},{5,3},{7,5},{1,7},{10,8},{12,10},{14... | collective-permute-start | bytes 1572872 | tf_op jit(solution)/shard_map/ppermute | solution.py:10
  40.5 15.6 %collective-permute-start.2 = (bf16[2,1024,128]{2,1,0:T(8,128)(2,1)}, bf16[2,1024,128]{2,1,0:T(8,128)(2,1)}, u32[]{:S(2)}, u32[]{:S(2)}) collective-permute-start(bf16[2,1024,128]{2,1,0:T(8,128)(2,1)} %collective-permute-done.1), channel_id=1, source_target_pairs={{6,0},{0,2},{2,4},{4,6},{7,1},{1,3},{3,5},{5,7},{14,8},{8,10},{10,... | collective-permute-start | bytes 1572872 | tf_op jit(solution)/shard_map/ppermute | solution.py:10
  49.0 0.7 copy-start
  49.7 11.8 %copy-start.11 = (bf16[1024,64]{1,0:T(8,128)(2,1)}, bf16[1024,64]{1,0:T(8,128)(2,1)S(1)}, u32[]{:S(2)}) copy-start(bf16[1024,64]{1,0:T(8,128)(2,1)S(1)} %get-tuple-element.39) | copy-start | bytes 393220
  49.7 11.8 %copy-start.12 = (bf16[1024,64]{1,0:T(8,128)(2,1)}, bf16[1024,64]{1,0:T(8,128)(2,1)S(1)}, u32[]{:S(2)}) copy-start(bf16[1024,64]{1,0:T(8,128)(2,1)S(1)} %get-tuple-element.40) | copy-start | bytes 393220
  49.7 11.8 %copy-start.7 = (bf16[1024,64]{1,0:T(8,128)(2,1)}, bf16[1024,64]{1,0:T(8,128)(2,1)S(1)}, u32[]{:S(2)}) copy-start(bf16[1024,64]{1,0:T(8,128)(2,1)S(1)} %get-tuple-element.57) | copy-start | bytes 393220
  49.7 11.8 %copy-start.9 = (bf16[1024,64]{1,0:T(8,128)(2,1)}, bf16[1024,64]{1,0:T(8,128)(2,1)S(1)}, u32[]{:S(2)}) copy-start(bf16[1024,64]{1,0:T(8,128)(2,1)S(1)} %get-tuple-element.58) | copy-start | bytes 393220
  56.1 10.9 %collective-permute-start.3 = (bf16[2,1024,128]{2,1,0:T(8,128)(2,1)}, bf16[2,1024,128]{2,1,0:T(8,128)(2,1)S(1)}, u32[]{:S(2)}, u32[]{:S(2)}) collective-permute-start(bf16[2,1024,128]{2,1,0:T(8,128)(2,1)} %collective-permute-done.2), channel_id=1, source_target_pairs={{1,0},{0,1},{3,2},{2,3},{5,4},{4,5},{7,6},{6,7},{9,8},{8,9},{11,10... | collective-permute-start | bytes 1572872 | tf_op jit(solution)/shard_map/ppermute | solution.py:10
  67.3 6.4 %copy-start.5 = (bf16[1024,64]{1,0:T(8,128)(2,1)}, bf16[1024,64]{1,0:T(8,128)(2,1)S(1)}, u32[]{:S(2)}) copy-start(bf16[1024,64]{1,0:T(8,128)(2,1)S(1)} %get-tuple-element.35) | copy-start | bytes 393220
  67.3 6.4 %copy-start.6 = (bf16[1024,64]{1,0:T(8,128)(2,1)}, bf16[1024,64]{1,0:T(8,128)(2,1)S(1)}, u32[]{:S(2)}) copy-start(bf16[1024,64]{1,0:T(8,128)(2,1)S(1)} %get-tuple-element.36) | copy-start | bytes 393220
  92.6 5.0 %copy-start.3 = (bf16[1024,1024]{0,1:T(8,128)(2,1)S(1)}, bf16[1024,1024]{0,1:T(8,128)(2,1)}, u32[]{:S(2)}) copy-start(bf16[1024,1024]{0,1:T(8,128)(2,1)} %get-tuple-element.15) | copy-start | bytes 6291460
  92.6 5.0 %copy-start.4 = (bf16[1024,64]{1,0:T(8,128)(2,1)S(1)}, bf16[1024,64]{1,0:T(8,128)(2,1)}, u32[]{:S(2)}) copy-start(bf16[1024,64]{1,0:T(8,128)(2,1)} %get-tuple-element.33) | copy-start | bytes 393220
  96.8 15.1 %collective-permute-start.4 = (f32[64,128]{1,0:T(8,128)S(1)}, f32[64,128]{1,0:T(8,128)S(1)}, u32[]{:S(2)}, u32[]{:S(2)}) collective-permute-start(f32[64,128]{1,0:T(8,128)S(1)} %pad_maximum_fusion.2), channel_id=1, source_target_pairs={{8,0},{16,8},{24,16},{0,24},{9,1},{17,9},{25,17},{1,25},{10,2},{18... | collective-permute-start | bytes 98312 | tf_op jit(solution)/shard_map/ppermute | solution.py:10
  97.6 4.8 %copy-start.1 = (bf16[1024,128]{1,0:T(8,128)(2,1)S(1)}, bf16[1024,128]{1,0:T(8,128)(2,1)}, u32[]{:S(2)}) copy-start(bf16[1024,128]{1,0:T(8,128)(2,1)} %copy-done) | copy-start | bytes 786436
  101.0 15.0 %collective-permute-start.7 = (f32[64,128]{1,0:T(8,128)S(1)}, f32[64,128]{1,0:T(8,128)S(1)}, u32[]{:S(2)}, u32[]{:S(2)}) collective-permute-start(f32[64,128]{1,0:T(8,128)S(1)} %pad_maximum_fusion.3), channel_id=1, source_target_pairs={{8,0},{16,8},{24,16},{0,24},{9,1},{17,9},{25,17},{1,25},{10,2},{18... | collective-permute-start | bytes 98312 | tf_op jit(solution)/shard_map/ppermute | solution.py:10
  102.4 4.1 %copy-start.2 = (bf16[1024,1024]{0,1:T(8,128)(2,1)S(1)}, bf16[1024,1024]{0,1:T(8,128)(2,1)}, u32[]{:S(2)}) copy-start(bf16[1024,1024]{0,1:T(8,128)(2,1)} %get-tuple-element.17) | copy-start | bytes 6291460
  102.4 4.1 %copy-start.8 = (bf16[1024,64]{1,0:T(8,128)(2,1)S(1)}, bf16[1024,64]{1,0:T(8,128)(2,1)}, u32[]{:S(2)}) copy-start(bf16[1024,64]{1,0:T(8,128)(2,1)} %copy-done.7) | copy-start | bytes 393220
  102.4 4.1 %copy-start.10 = (bf16[1024,64]{1,0:T(8,128)(2,1)S(1)}, bf16[1024,64]{1,0:T(8,128)(2,1)}, u32[]{:S(2)}) copy-start(bf16[1024,64]{1,0:T(8,128)(2,1)} %copy-done.9) | copy-start | bytes 393220
  109.9 4.8 %collective-permute-start.14 = (f32[64,128]{1,0:T(8,128)S(1)}, f32[64,128]{1,0:T(8,128)S(1)}, u32[]{:S(2)}, u32[]{:S(2)}) collective-permute-start(f32[64,128]{1,0:T(8,128)S(1)} %pad_maximum_fusion.5), channel_id=1, source_target_pairs={{16,0},{24,8},{0,16},{8,24},{17,1},{25,9},{1,17},{9,25},{18,2},{26... | collective-permute-start | bytes 98312 | tf_op jit(solution)/shard_map/ppermute | solution.py:10
  111.5 8.3 %collective-permute-start.12 = (f32[64,128]{1,0:T(8,128)S(1)}, f32[64,128]{1,0:T(8,128)S(1)}, u32[]{:S(2)}, u32[]{:S(2)}) collective-permute-start(f32[64,128]{1,0:T(8,128)S(1)} %pad_maximum_fusion.4), channel_id=1, source_target_pairs={{16,0},{24,8},{0,16},{8,24},{17,1},{25,9},{1,17},{9,25},{18,2},{26... | collective-permute-start | bytes 98312 | tf_op jit(solution)/shard_map/ppermute | solution.py:10
  112.0 7.8 %collective-permute-start.5 = (f32[64,128]{1,0:T(8,128)S(1)}, f32[64,128]{1,0:T(8,128)S(1)}, u32[]{:S(2)}, u32[]{:S(2)}) collective-permute-start(f32[64,128]{1,0:T(8,128)S(1)} %collective-permute-done.4), channel_id=1, source_target_pairs={{2,0},{4,2},{6,4},{0,6},{3,1},{5,3},{7,5},{1,7},{10,8},{12,10},{14... | collective-permute-start | bytes 98312 | tf_op jit(solution)/shard_map/ppermute | solution.py:10
  114.6 5.7 %collective-permute-start.15 = (f32[64,128]{1,0:T(8,128)S(1)}, f32[64,128]{1,0:T(8,128)S(1)}, u32[]{:S(2)}, u32[]{:S(2)}) collective-permute-start(f32[64,128]{1,0:T(8,128)S(1)} %collective-permute-done.14), channel_id=1, source_target_pairs={{6,0},{0,2},{2,4},{4,6},{7,1},{1,3},{3,5},{5,7},{14,8},{8,10},{10,... | collective-permute-start | bytes 98312 | tf_op jit(solution)/shard_map/ppermute | solution.py:10
  116.0 5.6 %collective-permute-start.8 = (f32[64,128]{1,0:T(8,128)S(1)}, f32[64,128]{1,0:T(8,128)S(1)}, u32[]{:S(2)}, u32[]{:S(2)}) collective-permute-start(f32[64,128]{1,0:T(8,128)S(1)} %collective-permute-done.7), channel_id=1, source_target_pairs={{2,0},{4,2},{6,4},{0,6},{3,1},{5,3},{7,5},{1,7},{10,8},{12,10},{14... | collective-permute-start | bytes 98312 | tf_op jit(solution)/shard_map/ppermute | solution.py:10
  119.8 5.7 %collective-permute-start.13 = (f32[64,128]{1,0:T(8,128)S(1)}, f32[64,128]{1,0:T(8,128)S(1)}, u32[]{:S(2)}, u32[]{:S(2)}) collective-permute-start(f32[64,128]{1,0:T(8,128)S(1)} %collective-permute-done.12), channel_id=1, source_target_pairs={{6,0},{0,2},{2,4},{4,6},{7,1},{1,3},{3,5},{5,7},{14,8},{8,10},{10,... | collective-permute-start | bytes 98312 | tf_op jit(solution)/shard_map/ppermute | solution.py:10
  119.8 5.7 %collective-permute-start.6 = (f32[64,128]{1,0:T(8,128)S(1)}, f32[64,128]{1,0:T(8,128)S(1)}, u32[]{:S(2)}, u32[]{:S(2)}) collective-permute-start(f32[64,128]{1,0:T(8,128)S(1)} %collective-permute-done.5), channel_id=1, source_target_pairs={{1,0},{0,1},{3,2},{2,3},{5,4},{4,5},{7,6},{6,7},{9,8},{8,9},{11,10... | collective-permute-start | bytes 98312 | tf_op jit(solution)/shard_map/ppermute | solution.py:10
  120.4 5.1 %collective-permute-start.16 = (f32[64,128]{1,0:T(8,128)S(1)}, f32[64,128]{1,0:T(8,128)S(1)}, u32[]{:S(2)}, u32[]{:S(2)}) collective-permute-start(f32[64,128]{1,0:T(8,128)S(1)} %collective-permute-done.15), channel_id=1, source_target_pairs={{1,0},{0,1},{3,2},{2,3},{5,4},{4,5},{7,6},{6,7},{9,8},{8,9},{11,10... | collective-permute-start | bytes 98312 | tf_op jit(solution)/shard_map/ppermute | solution.py:10
where the time goes:
time: 127 us
  matrix products  49.7 us (39%)
  starting transfers between devices  21.2 us (17%)
  between operations  17.7 us (14%)
  waiting for transfers between devices  16.5 us (13%)
  local copies, waits for them, and re-layouts  15 us (12%)
  other arithmetic  6.44 us (5%)
    dot_general x4, matrix products, density_product(): jnp.dot(masked, swapped.T, preferred_element_type=jnp.float32)  24.5 us
    ppermute x17, starting transfers between devices, shifted(): return lax.ppermute(block, axis, route)  21.2 us
    ppermute x17, waiting for transfers between devices, shifted(): return lax.ppermute(block, axis, route)  16.5 us
    dot_general x4, matrix products, exchange_block(): lax.dot_general(orbital, mixture, (((0,), (0,)), ((), ())), preferred_ele...  14.4 us
    dot_general x4, matrix products, density_product(): jnp.dot(masked, orbital.T, preferred_element_type=jnp.float32)  10.9 us
    unnamed x28, local copies, waits for them, and re-layouts  7.37 us
    slice x1, local copies, waits for them, and re-layouts, on_device(): kernel_real = kernel[0, 0]  4.69 us
  transfers between devices with their start and end apart: 17, of which 5 were waited for; matrix products, arithmetic and copies ran while one was open for 29% of the time, Pallas kernels for 0%

commit v1 on v0

v1 whole, which is shorter than its diff:
```python
import functools

import jax
import jax.numpy as jnp
from jax import lax
from jax.experimental import pallas as pl
from jax.experimental.pallas import tpu as pltpu
from jax.sharding import PartitionSpec as P

AXES = ("kx", "ky", "kz")
SMALL_GRANT = 4 << 20
PICK_GRANT = 61 << 20
PAIR_GRANT = 24 << 20
CONTRACT_LAST = (((1,), (1,)), ((), ()))
CONTRACT_FIRST = (((0,), (0,)), ((), ()))


def mesh_sizes():
    return tuple(lax.axis_size(axis) for axis in AXES)


def hop_shifts(turn_number, mesh_counts):
    forward = (
        (turn_number + 1) % mesh_counts[0],
        (2 * turn_number + 1) % mesh_counts[1],
        (3 * turn_number + 1) % mesh_counts[2],
    )
    partner = (forward[0], forward[1], (forward[2] - mesh_counts[2] // 2) % mesh_counts[2])
    return (forward, partner)


def linear_of(places, mesh_counts):
    return (places[0] * mesh_counts[1] + places[1]) * mesh_counts[2] + places[2]


def moved(block, shift, mesh_counts):
    route = []
    for first in range(mesh_counts[0]):
        for second in range(mesh_counts[1]):
            for third in range(mesh_counts[2]):
                target = tuple(
                    (place + step) % count
                    for place, step, count in zip((first, second, third), shift, mesh_counts)
                )
                route.append(
                    (linear_of((first, second, third), mesh_counts), linear_of(target, mesh_counts))
                )
    return lax.ppermute(block, AXES, route)


def negated(shift):
    return tuple(-step for step in shift)


def cell_of(slot, cell_counts):
    return (
        slot // (cell_counts[1] * cell_counts[2]),
        slot // cell_counts[2] % cell_counts[1],
        slot % cell_counts[2],
    )


def own_places():
    return tuple(lax.axis_index(axis) for axis in AXES)


def wrapped(value, count):
    return jnp.where(value < 0, value + count, value)


def whole(space):
    return pl.BlockSpec(memory_space=space)


def pick_kernel(turn_number, mesh_counts, plan_ref, orbitals_ref, first_ref, second_ref, sems):
    own = linear_of(own_places(), mesh_counts)
    copies = []
    for column, out_ref in ((1, second_ref), (0, first_ref)):
        cell = cell_of(plan_ref[turn_number, column, own], orbitals_ref.shape[:3])
        copy = pltpu.make_async_copy(
            orbitals_ref.at[cell[0], cell[1], cell[2]], out_ref, sems.at[column]
        )
        copy.start()
        copies.append(copy)
    for copy in copies:
        copy.wait()


def picked(turn_number, mesh_counts, plan, orbitals):
    block = jax.ShapeDtypeStruct(orbitals.shape[3:], orbitals.dtype)
    return pl.pallas_call(
        functools.partial(pick_kernel, turn_number, mesh_counts),
        out_shape=(block, block),
        in_specs=[whole(pltpu.SMEM), whole(pl.ANY)],
        out_specs=(whole(pltpu.VMEM), whole(pltpu.VMEM)),
        scratch_shapes=[pltpu.SemaphoreType.DMA((2,))],
        compiler_params=pltpu.CompilerParams(vmem_limit_bytes=PICK_GRANT),
        name=f"pick_{turn_number}",
    )(plan, orbitals)


def mask_kernel(mesh_counts, cell_counts, plan_ref, occupation_ref, out_ref, rows, sem):
    places = own_places()
    copies = []
    turns = plan_ref.shape[0]
    for turn_number in range(turns):
        for column, shift in enumerate(hop_shifts(turn_number, mesh_counts)):
            sender = tuple(
                wrapped(place - step, count)
                for place, step, count in zip(places, shift, mesh_counts)
            )
            cell = cell_of(plan_ref[turn_number, column, linear_of(sender, mesh_counts)], cell_counts)
            point = tuple(
                place * count + inner for place, count, inner in zip(sender, cell_counts, cell)
            )
            entry = 2 * turn_number + column
            copy = pltpu.make_async_copy(
                occupation_ref.at[point[0], point[1], pl.ds(point[2], 1)],
                rows.at[pl.ds(entry, 1)],
                sem.at[entry],
            )
            copy.start()
            copies.append(copy)
    for copy in copies:
        copy.wait()
    held = rows[...].astype(jnp.float32)
    out_ref[...] = jnp.concatenate([held, held], axis=1)


def masks_of(mesh_counts, cell_counts, plan, occupation):
    entries = plan.shape[0] * 2
    bands = occupation.shape[3]
    return pl.pallas_call(
        functools.partial(mask_kernel, mesh_counts, cell_counts),
        out_shape=jax.ShapeDtypeStruct((entries, 2 * bands), jnp.float32),
        in_specs=[whole(pltpu.SMEM), whole(pl.ANY)],
        out_specs=whole(pltpu.VMEM),
        scratch_shapes=[
            pltpu.VMEM((entries, bands), occupation.dtype),
            pltpu.SemaphoreType.DMA((entries,)),
        ],
        compiler_params=pltpu.CompilerParams(vmem_limit_bytes=SMALL_GRANT),
        name="masks",
    )(plan, occupation)


def quarter_turn(block):
    bands = block.shape[1] // 2
    return jnp.concatenate([-block[:, bands:], block[:, :bands]], axis=1)


def folded(gram):
    bands = gram.shape[0] // 2
    top, bottom = gram[:bands], gram[bands:]
    return -(top + jnp.concatenate([bottom[:, bands:], -bottom[:, :bands]], axis=1))


def dot32(left, right, dims):
    return lax.dot_general(left, right, dims, preferred_element_type=jnp.float32)


def pair_kernel(
    turn_number,
    chunk,
    mask_ref,
    kernel_ref,
    first_ref,
    second_ref,
    first_out,
    second_out,
    first_wide,
    second_wide,
    first_mix,
    second_mix,
):
    tile = kernel_ref.shape[2]
    points, width = first_ref.shape
    step = pl.program_id(0)

    @pl.when(step == 0)
    def _():
        for source, wide in ((first_ref, first_wide), (second_ref, second_wide)):
            block = source[...]
            wide[:points] = block
            wide[points:] = quarter_turn(block)

    rows = pl.ds(pl.multiple_of(step * tile, tile), tile)
    entry = 2 * turn_number
    first_masked = first_ref[rows, :] * mask_ref[entry : entry + 1, :].astype(first_ref.dtype)
    second_masked = second_ref[rows, :] * mask_ref[entry + 1 : entry + 2, :].astype(second_ref.dtype)
    first_total = jnp.zeros((tile, width), jnp.float32)
    second_total = first_total
    plain = (((1,), (0,)), ((), ()))
    for start in range(0, points, chunk):
        real = slice(start, start + chunk)
        imag = slice(points + start, points + start + chunk)
        weight_real = kernel_ref[0, 0, :, real].astype(jnp.float32)
        weight_imag = kernel_ref[0, 1, :, real].astype(jnp.float32)
        density_real = dot32(second_masked, second_wide[real], CONTRACT_LAST)
        density_imag = dot32(second_masked, second_wide[imag], CONTRACT_LAST)
        part_real = weight_real * density_real - weight_imag * density_imag
        part_imag = weight_real * density_imag + weight_imag * density_real
        first_total += dot32(part_real.astype(jnp.bfloat16), first_wide[real], plain)
        first_total += dot32(part_imag.astype(jnp.bfloat16), first_wide[imag], plain)
        density_real = dot32(first_masked, first_wide[real], CONTRACT_LAST)
        density_imag = dot32(first_masked, first_wide[imag], CONTRACT_LAST)
        part_real = weight_real * density_real + weight_imag * density_imag
        part_imag = weight_real * density_imag - weight_imag * density_real
        second_total += dot32(part_real.astype(jnp.bfloat16), second_wide[real], plain)
        second_total += dot32(part_imag.astype(jnp.bfloat16), second_wide[imag], plain)
    first_mix[rows, :] = first_total.astype(jnp.bfloat16)
    second_mix[rows, :] = second_total.astype(jnp.bfloat16)

    @pl.when(step == pl.num_programs(0) - 1)
    def _():
        for source, mix, out in (
            (first_ref, first_mix, first_out),
            (second_ref, second_mix, second_out),
        ):
            out[...] = folded(dot32(source[...], mix[...], CONTRACT_FIRST)).astype(out.dtype)


def pair_blocks(turn_number, masks, kernel, first, second):
    points, width = first.shape
    tile = points // 2
    fixed = lambda shape: pl.BlockSpec(shape, lambda step: (0,) * len(shape))
    block = jax.ShapeDtypeStruct((width // 2, width), jnp.bfloat16)
    return pl.pallas_call(
        functools.partial(pair_kernel, turn_number, points // 4),
        grid=(points // tile,),
        out_shape=(block, block),
        in_specs=[
            fixed(masks.shape),
            pl.BlockSpec((1, 2, tile, points), lambda step: (0, 0, step, 0)),
            fixed(first.shape),
            fixed(second.shape),
        ],
        out_specs=(fixed(block.shape), fixed(block.shape)),
        scratch_shapes=[pltpu.VMEM((2 * points, width), jnp.bfloat16)] * 2
        + [pltpu.VMEM((points, width), jnp.bfloat16)] * 2,
        cost_estimate=pl.CostEstimate(
            flops=24 * points * points * width, bytes_accessed=6 * points * points, transcendentals=0
        ),
        compiler_params=pltpu.CompilerParams(vmem_limit_bytes=PAIR_GRANT),
        name=f"pair_{turn_number}",
    )(masks, kernel, first, second)


def total_kernel(mesh_counts, plan_ref, *refs):
    out_ref = refs[-1]
    own = linear_of(own_places(), mesh_counts)
    out_ref[...] = jnp.zeros_like(out_ref)
    for number, block_ref in enumerate(refs[:-1]):
        cell = cell_of(plan_ref[number // 2, number % 2, own], out_ref.shape[:3])
        held = out_ref[cell[0], cell[1], cell[2]]
        out_ref[cell[0], cell[1], cell[2]] = held + block_ref[...].astype(out_ref.dtype)


def totalled(mesh_counts, cell_counts, plan, blocks):
    return pl.pallas_call(
        functools.partial(total_kernel, mesh_counts),
        out_shape=jax.ShapeDtypeStruct((*cell_counts, *blocks[0].shape), jnp.float32),
        in_specs=[whole(pltpu.SMEM)] + [whole(pltpu.VMEM)] * len(blocks),
        out_specs=whole(pltpu.VMEM),
        compiler_params=pltpu.CompilerParams(vmem_limit_bytes=SMALL_GRANT),
        name="totals",
    )(plan, *blocks)


def on_device(orbitals, kernel, plan, occupation):
    mesh_counts = mesh_sizes()
    cell_counts = orbitals.shape[:3]
    arrived = []
    for turn_number in range(plan.shape[0]):
        forward, partner = hop_shifts(turn_number, mesh_counts)
        first_send, second_send = picked(turn_number, mesh_counts, plan, orbitals)
        second = moved(second_send, partner, mesh_counts)
        first = moved(first_send, forward, mesh_counts)
        arrived.append((first, second))
    masks = masks_of(mesh_counts, cell_counts, plan, occupation)
    returned = []
    for turn_number, (first, second) in enumerate(arrived):
        forward, partner = hop_shifts(turn_number, mesh_counts)
        first_block, second_block = pair_blocks(turn_number, masks, kernel, first, second)
        returned.append(moved(first_block, negated(forward), mesh_counts))
        returned.append(moved(second_block, negated(partner), mesh_counts))
    return totalled(mesh_counts, cell_counts, plan, returned)


def solution(mesh):
    placed = (P("kx", "ky", "kz", None, None), P(("kx", "ky", "kz"), None, None, None), P(), P())
    return jax.shard_map(
        on_device,
        mesh=mesh,
        in_specs=placed,
        out_specs=P("kx", "ky", "kz", None, None),
        check_vma=False,
    )
```

time: 127 us -> 49 us (0.39)
  matrix products: 49.7 us -> 0 us
  Pallas kernels: 0 us -> 20.3 us
  between operations: 17.7 us -> 0.06 us
  local copies, waits for them, and re-layouts: 15 us -> 2.19 us
  waiting for transfers between devices: 16.5 us -> 9.81 us
  other arithmetic: 6.44 us -> 0 us
  starting transfers between devices: 21.2 us -> 16.3 us
    dot_general x12 -> x0, matrix products: 49.7 us -> none  [the longest x4 24.5 us: density_product(): jnp.dot(masked, swapped.T, preferred_element_type=jnp.float32)]
    pallas_call x0 -> x6, Pallas kernels: none -> 20.3 us  [the longest x2 12.9 us: pair_blocks(): pl.pallas_call(functools.partial(pair_kernel, turn_number, points // 4),...]
    ppermute x17 -> x8, waiting for transfers between devices: 16.5 us -> 9.81 us  [moved(): return lax.ppermute(block, AXES, route)]
    unnamed x28 -> x6, local copies, waits for them, and re-layouts: 7.37 us -> 2.19 us
    ppermute x17 -> x8, starting transfers between devices: 21.2 us -> 16.3 us  [moved(): return lax.ppermute(block, AXES, route)]
    slice x1 -> x0, local copies, waits for them, and re-layouts: 4.69 us -> none  [on_device(): kernel_real = kernel[0, 0]]
    dynamic_slice x2 -> x0, local copies, waits for them, and re-layouts: 2.82 us -> none  [the longest x1 1.55 us: global_points(): slot_index = plan[turn_number, column, linear]]
    convert_element_type x2 -> x0, other arithmetic: 2.49 us -> none  [on_device(): first_pick = (slot_numbers == first_slot).astype(jnp.float32)[:, None, None]]
  transfers between devices with their start and end apart: 17 -> 8, of which waited for: 5 -> 4; matrix products, arithmetic and copies ran while one was open for 29% -> 0% of each run, Pallas kernels for 0% -> 33%
where the time goes in v1:
time: 49 us; the launch traced here: 48.7 us
  Pallas kernels  20.3 us (41%)
  starting transfers between devices  16.3 us (33%)
  waiting for transfers between devices  9.81 us (20%)
  local copies, waits for them, and re-layouts  2.19 us (4%)
    ppermute x8, starting transfers between devices, moved(): return lax.ppermute(block, AXES, route)  16.3 us
    pallas_call x2, Pallas kernels, pair_blocks(): pl.pallas_call(functools.partial(pair_kernel, turn_number, points // 4),...  12.9 us
    ppermute x8, waiting for transfers between devices, moved(): return lax.ppermute(block, AXES, route)  9.81 us
    pallas_call x2, Pallas kernels, picked(): pl.pallas_call(functools.partial(pick_kernel, turn_number, mesh_counts),...  5.27 us
    unnamed x6, local copies, waits for them, and re-layouts  2.19 us
    pallas_call x1, Pallas kernels, totalled(): pl.pallas_call(functools.partial(total_kernel, mesh_counts), out_shape=ja...  1.42 us
  transfers between devices with their start and end apart: 8, of which 4 were waited for; matrix products, arithmetic and copies ran while one was open for 0% of the time, Pallas kernels for 33%

profile of v1, /device:TPU:0, one launch (start us, length us, event | category | flops | bytes accessed | tf_op | source)
XLA Modules:
  0.0 48.7 jit_solution(245727584510710319)
XLA Ops:
  0.0 0.0 copy-start.1
  0.0 0.0 copy-start
  0.0 2.7 %pick_1.1 = (bf16[1024,128]{1,0:T(8,128)(2,1)}, bf16[1024,128]{1,0:T(8,128)(2,1)}) custom-call(s32[2,2,32]{2,1,0:T(2,128)} %plan_ref.7, bf16[4,4,1,1024,128]{4,3,2,1,0:T(8,128)(2,1)} %orbitals_ref.3), custom_call_target="tpu_custom_call" | custom-call | tf_op jit(solution)/shard_map/pick_1/pallas_call | solution.py:91
  2.7 6.1 %collective-permute-start.4 = (bf16[1024,128]{1,0:T(8,128)(2,1)}, bf16[1024,128]{1,0:T(8,128)(2,1)S(1)}, u32[]{:S(2)}, u32[]{:S(2)}) collective-permute-start(bf16[1024,128]{1,0:T(8,128)(2,1)} %get-tuple-element.17), channel_id=1, source_target_pairs={{0,22},{1,23},{2,16},{3,17},{4,18},{5,19},{6,20},{7,21},{8,30},{9,... | collective-permute-start | bytes 786440 | tf_op jit(solution)/shard_map/ppermute | solution.py:48
  8.8 0.0 collective-permute-start.5
  8.8 2.6 %pick_0.1 = (bf16[1024,128]{1,0:T(8,128)(2,1)}, bf16[1024,128]{1,0:T(8,128)(2,1)}) custom-call(s32[2,2,32]{2,1,0:T(2,128)} %plan_ref.7, bf16[4,4,1,1024,128]{4,3,2,1,0:T(8,128)(2,1)} %orbitals_ref.3), custom_call_target="tpu_custom_call" | custom-call | tf_op jit(solution)/shard_map/pick_0/pallas_call | solution.py:91
  11.4 2.7 %collective-permute-start = (bf16[1024,128]{1,0:T(8,128)(2,1)}, bf16[1024,128]{1,0:T(8,128)(2,1)S(1)}, u32[]{:S(2)}, u32[]{:S(2)}) collective-permute-start(bf16[1024,128]{1,0:T(8,128)(2,1)} %get-tuple-element.13), channel_id=1, source_target_pairs={{0,11},{1,10},{2,13},{3,12},{4,15},{5,14},{6,9},{7,8},{8,19},{9,18... | collective-permute-start | bytes 786440 | tf_op jit(solution)/shard_map/ppermute | solution.py:48
  14.0 0.0 collective-permute-start.1
  14.0 0.0 copy-done.1
  14.0 0.0 copy-done
  14.1 0.8 %masks.1.mask_ref = f32[4,128]{1,0:T(4,128)S(1)} custom-call(s32[2,2,32]{2,1,0:T(2,128)S(1)} %copy-done.1, s32[16,16,2,64]{3,2,1,0:T(2,128)S(1)} %copy-done), custom_call_target="tpu_custom_call" | custom-call | tf_op jit(solution)/shard_map/masks/pallas_call | solution.py:133
  14.8 1.0 %collective-permute-done.4.first_ref = bf16[1024,128]{1,0:T(8,128)(2,1)S(1)} collective-permute-done((bf16[1024,128]{1,0:T(8,128)(2,1)}, bf16[1024,128]{1,0:T(8,128)(2,1)S(1)}, u32[]{:S(2)}, u32[]{:S(2)}) %collective-permute-start.4) | collective-permute-done | bytes 262176 | tf_op jit(solution)/shard_map/ppermute | solution.py:48
  15.9 5.6 %collective-permute-done.5.second_ref = bf16[1024,128]{1,0:T(8,128)(2,1)S(1)} collective-permute-done((bf16[1024,128]{1,0:T(8,128)(2,1)}, bf16[1024,128]{1,0:T(8,128)(2,1)S(1)}, u32[]{:S(2)}, u32[]{:S(2)}) %collective-permute-start.5) | collective-permute-done | bytes 262176 | tf_op jit(solution)/shard_map/ppermute | solution.py:48
  21.5 0.0 copy-start.2
  21.5 2.2 %copy-done.2 = bf16[1,2,1024,1024]{3,2,1,0:T(8,128)(2,1)S(1)} copy-done((bf16[1,2,1024,1024]{3,2,1,0:T(8,128)(2,1)S(1)}, bf16[1,2,1024,1024]{3,2,1,0:T(8,128)(2,1)}, u32[]{:S(2)}) %copy-start.2) | copy-done | bytes 4194328
  23.7 6.5 %pair_1.1 = (bf16[64,128]{1,0:T(8,128)(2,1)S(1)}, bf16[64,128]{1,0:T(8,128)(2,1)S(1)}) custom-call(f32[4,128]{1,0:T(4,128)S(1)} %masks.1.mask_ref, bf16[1,2,1024,1024]{3,2,1,0:T(8,128)(2,1)S(1)} %copy-done.2, bf16[1024,128]{1,0:T(8,128)(2,1)S(1)} %collective-permute-done.4.first_ref, bf16[1024,128]{1,0:T(8,128)(2,1)S(1)} %collective-permute-done.5.second_ref), custom_call_target="tpu_custom_call" | custom-call | flops 3221225472 | bytes 6291456 | tf_op jit(solution)/shard_map/pair_1/pallas_call | solution.py:228
  30.1 0.1 collective-permute-start.6
  30.2 1.9 %collective-permute-start.7 = (bf16[64,128]{1,0:T(8,128)(2,1)S(1)}, bf16[64,128]{1,0:T(8,128)(2,1)S(1)}, u32[]{:S(2)}, u32[]{:S(2)}) collective-permute-start(bf16[64,128]{1,0:T(8,128)(2,1)S(1)} %get-tuple-element.20), channel_id=1, source_target_pairs={{0,19},{1,18},{2,21},{3,20},{4,23},{5,22},{6,17},{7,16},{8,27},{9,... | collective-permute-start | bytes 49160 | tf_op jit(solution)/shard_map/ppermute | solution.py:48
  32.1 0.0 collective-permute-done.first_ref
  32.1 1.1 %collective-permute-done.1.second_ref = bf16[1024,128]{1,0:T(8,128)(2,1)S(1)} collective-permute-done((bf16[1024,128]{1,0:T(8,128)(2,1)}, bf16[1024,128]{1,0:T(8,128)(2,1)S(1)}, u32[]{:S(2)}, u32[]{:S(2)}) %collective-permute-start.1) | collective-permute-done | bytes 262176 | tf_op jit(solution)/shard_map/ppermute | solution.py:48
  33.2 6.4 %pair_0.1 = (bf16[64,128]{1,0:T(8,128)(2,1)S(1)}, bf16[64,128]{1,0:T(8,128)(2,1)S(1)}) custom-call(f32[4,128]{1,0:T(4,128)S(1)} %masks.1.mask_ref, bf16[1,2,1024,1024]{3,2,1,0:T(8,128)(2,1)S(1)} %copy-done.2, bf16[1024,128]{1,0:T(8,128)(2,1)S(1)} %collective-permute-done.first_ref, bf16[1024,128]{1,0:T(8,128)(2,1)S(1)} %collective-permute-done.1.second_ref), custom_call_target="tpu_custom_call" | custom-call | flops 3221225472 | bytes 6291456 | tf_op jit(solution)/shard_map/pair_0/pallas_call | solution.py:228
  39.7 3.0 %collective-permute-start.2 = (bf16[64,128]{1,0:T(8,128)(2,1)S(1)}, bf16[64,128]{1,0:T(8,128)(2,1)S(1)}, u32[]{:S(2)}, u32[]{:S(2)}) collective-permute-start(bf16[64,128]{1,0:T(8,128)(2,1)S(1)} %get-tuple-element.15), channel_id=1, source_target_pairs={{0,31},{1,30},{2,25},{3,24},{4,27},{5,26},{6,29},{7,28},{8,7},{9,6... | collective-permute-start | bytes 49160 | tf_op jit(solution)/shard_map/ppermute | solution.py:48
  42.7 2.6 %collective-permute-start.3 = (bf16[64,128]{1,0:T(8,128)(2,1)S(1)}, bf16[64,128]{1,0:T(8,128)(2,1)S(1)}, u32[]{:S(2)}, u32[]{:S(2)}) collective-permute-start(bf16[64,128]{1,0:T(8,128)(2,1)S(1)} %get-tuple-element.16), channel_id=1, source_target_pairs={{0,30},{1,31},{2,24},{3,25},{4,26},{5,27},{6,28},{7,29},{8,6},{9,7... | collective-permute-start | bytes 49160 | tf_op jit(solution)/shard_map/ppermute | solution.py:48
  45.3 0.0 collective-permute-done.6.refs_2_
  45.3 0.0 collective-permute-done.7.refs_3_
  45.3 0.0 collective-permute-done.2.refs_0_
  45.3 2.0 %collective-permute-done.3.refs_1_ = bf16[64,128]{1,0:T(8,128)(2,1)S(1)} collective-permute-done((bf16[64,128]{1,0:T(8,128)(2,1)S(1)}, bf16[64,128]{1,0:T(8,128)(2,1)S(1)}, u32[]{:S(2)}, u32[]{:S(2)}) %collective-permute-start.3) | collective-permute-done | bytes 16416 | tf_op jit(solution)/shard_map/ppermute | solution.py:48
  47.3 1.4 %totals.1 = f32[4,4,1,64,128]{4,3,2,1,0:T(8,128)} custom-call(s32[2,2,32]{2,1,0:T(2,128)S(1)} %copy-done.1, bf16[64,128]{1,0:T(8,128)(2,1)S(1)} %collective-permute-done.2.refs_0_, bf16[64,128]{1,0:T(8,128)(2,1)S(1)} %collective-permute-done.3.refs_1_, bf16[64,128]{1,0:T(8,128)(2,1)S(1)} %collective-permute-done.6.refs_2_, ...), custom_call_target="tpu_custom_call" | custom-call | tf_op jit(solution)/shard_map/totals/pallas_call | solution.py:260
Async XLA Ops:
  0.0 14.0 %copy-start.1 = (s32[2,2,32]{2,1,0:T(2,128)S(1)}, s32[2,2,32]{2,1,0:T(2,128)}, u32[]{:S(2)}) copy-start(s32[2,2,32]{2,1,0:T(2,128)} %plan_ref.7) | copy-start | bytes 1540
  0.0 14.0 %copy-start = (s32[16,16,2,64]{3,2,1,0:T(2,128)S(1)}, s32[16,16,2,64]{3,2,1,0:T(2,128)}, u32[]{:S(2)}) copy-start(s32[16,16,2,64]{3,2,1,0:T(2,128)} %occupation_ref.1) | copy-start | bytes 393220
  2.7 13.1 %collective-permute-start.4 = (bf16[1024,128]{1,0:T(8,128)(2,1)}, bf16[1024,128]{1,0:T(8,128)(2,1)S(1)}, u32[]{:S(2)}, u32[]{:S(2)}) collective-permute-start(bf16[1024,128]{1,0:T(8,128)(2,1)} %get-tuple-element.17), channel_id=1, source_target_pairs={{0,22},{1,23},{2,16},{3,17},{4,18},{5,19},{6,20},{7,21},{8,30},{9,... | collective-permute-start | bytes 786440 | tf_op jit(solution)/shard_map/ppermute | solution.py:48
  8.8 12.7 %collective-permute-start.5 = (bf16[1024,128]{1,0:T(8,128)(2,1)}, bf16[1024,128]{1,0:T(8,128)(2,1)S(1)}, u32[]{:S(2)}, u32[]{:S(2)}) collective-permute-start(bf16[1024,128]{1,0:T(8,128)(2,1)} %get-tuple-element.18), channel_id=1, source_target_pairs={{0,23},{1,22},{2,17},{3,16},{4,19},{5,18},{6,21},{7,20},{8,31},{9,... | collective-permute-start | bytes 786440 | tf_op jit(solution)/shard_map/ppermute | solution.py:48
  11.4 20.7 %collective-permute-start = (bf16[1024,128]{1,0:T(8,128)(2,1)}, bf16[1024,128]{1,0:T(8,128)(2,1)S(1)}, u32[]{:S(2)}, u32[]{:S(2)}) collective-permute-start(bf16[1024,128]{1,0:T(8,128)(2,1)} %get-tuple-element.13), channel_id=1, source_target_pairs={{0,11},{1,10},{2,13},{3,12},{4,15},{5,14},{6,9},{7,8},{8,19},{9,18... | collective-permute-start | bytes 786440 | tf_op jit(solution)/shard_map/ppermute | solution.py:48
  14.0 19.2 %collective-permute-start.1 = (bf16[1024,128]{1,0:T(8,128)(2,1)}, bf16[1024,128]{1,0:T(8,128)(2,1)S(1)}, u32[]{:S(2)}, u32[]{:S(2)}) collective-permute-start(bf16[1024,128]{1,0:T(8,128)(2,1)} %get-tuple-element.14), channel_id=1, source_target_pairs={{0,10},{1,11},{2,12},{3,13},{4,14},{5,15},{6,8},{7,9},{8,18},{9,19... | collective-permute-start | bytes 786440 | tf_op jit(solution)/shard_map/ppermute | solution.py:48
  21.5 2.2 %copy-start.2 = (bf16[1,2,1024,1024]{3,2,1,0:T(8,128)(2,1)S(1)}, bf16[1,2,1024,1024]{3,2,1,0:T(8,128)(2,1)}, u32[]{:S(2)}) copy-start(bf16[1,2,1024,1024]{3,2,1,0:T(8,128)(2,1)} %kernel_ref.3) | copy-start | bytes 12582916
  30.1 15.2 %collective-permute-start.6 = (bf16[64,128]{1,0:T(8,128)(2,1)S(1)}, bf16[64,128]{1,0:T(8,128)(2,1)S(1)}, u32[]{:S(2)}, u32[]{:S(2)}) collective-permute-start(bf16[64,128]{1,0:T(8,128)(2,1)S(1)} %get-tuple-element.19), channel_id=1, source_target_pairs={{0,18},{1,19},{2,20},{3,21},{4,22},{5,23},{6,16},{7,17},{8,26},{9,... | collective-permute-start | bytes 49160 | tf_op jit(solution)/shard_map/ppermute | solution.py:48
  30.2 15.1 %collective-permute-start.7 = (bf16[64,128]{1,0:T(8,128)(2,1)S(1)}, bf16[64,128]{1,0:T(8,128)(2,1)S(1)}, u32[]{:S(2)}, u32[]{:S(2)}) collective-permute-start(bf16[64,128]{1,0:T(8,128)(2,1)S(1)} %get-tuple-element.20), channel_id=1, source_target_pairs={{0,19},{1,18},{2,21},{3,20},{4,23},{5,22},{6,17},{7,16},{8,27},{9,... | collective-permute-start | bytes 49160 | tf_op jit(solution)/shard_map/ppermute | solution.py:48
  39.7 5.6 %collective-permute-start.2 = (bf16[64,128]{1,0:T(8,128)(2,1)S(1)}, bf16[64,128]{1,0:T(8,128)(2,1)S(1)}, u32[]{:S(2)}, u32[]{:S(2)}) collective-permute-start(bf16[64,128]{1,0:T(8,128)(2,1)S(1)} %get-tuple-element.15), channel_id=1, source_target_pairs={{0,31},{1,30},{2,25},{3,24},{4,27},{5,26},{6,29},{7,28},{8,7},{9,6... | collective-permute-start | bytes 49160 | tf_op jit(solution)/shard_map/ppermute | solution.py:48
  42.7 4.6 %collective-permute-start.3 = (bf16[64,128]{1,0:T(8,128)(2,1)S(1)}, bf16[64,128]{1,0:T(8,128)(2,1)S(1)}, u32[]{:S(2)}, u32[]{:S(2)}) collective-permute-start(bf16[64,128]{1,0:T(8,128)(2,1)S(1)} %get-tuple-element.16), channel_id=1, source_target_pairs={{0,30},{1,31},{2,24},{3,25},{4,26},{5,27},{6,28},{7,29},{8,6},{9,7... | collective-permute-start | bytes 49160 | tf_op jit(solution)/shard_map/ppermute | solution.py:48

commit v2 on v1

v2 whole, which is shorter than its diff:
```python
import functools

import jax
import jax.numpy as jnp
from jax import lax
from jax.experimental import pallas as pl
from jax.experimental.pallas import tpu as pltpu
from jax.sharding import PartitionSpec as P


AXES = ("kx", "ky", "kz")
SMALL_GRANT = 4 << 20
PICK_GRANT = 52 << 20
PAIR_GRANT = 24 << 20
CONTRACT_LAST = (((1,), (1,)), ((), ()))
CONTRACT_FIRST = (((0,), (0,)), ((), ()))


def mesh_sizes():
    return tuple(lax.axis_size(axis) for axis in AXES)


def hop_shifts(turn_number, mesh_counts):
    forward = (
        (turn_number + 1) % mesh_counts[0],
        (2 * turn_number + 1) % mesh_counts[1],
        (3 * turn_number + 1) % mesh_counts[2],
    )
    partner = (forward[0], forward[1], (forward[2] - mesh_counts[2] // 2) % mesh_counts[2])
    return (forward, partner)


def linear_of(places, mesh_counts):
    return (places[0] * mesh_counts[1] + places[1]) * mesh_counts[2] + places[2]


def moved(block, shift, mesh_counts):
    route = []
    for first in range(mesh_counts[0]):
        for second in range(mesh_counts[1]):
            for third in range(mesh_counts[2]):
                target = tuple(
                    (place + step) % count
                    for place, step, count in zip((first, second, third), shift, mesh_counts)
                )
                route.append(
                    (linear_of((first, second, third), mesh_counts), linear_of(target, mesh_counts))
                )
    return lax.ppermute(block, AXES, route)


def after(block, *earlier):
    return lax.optimization_barrier((block, *earlier))[0] if earlier else block


def negated(shift):
    return tuple(-step for step in shift)


def cell_of(slot, cell_counts):
    return (
        slot // (cell_counts[1] * cell_counts[2]),
        slot // cell_counts[2] % cell_counts[1],
        slot % cell_counts[2],
    )


def own_places():
    return tuple(lax.axis_index(axis) for axis in AXES)


def wrapped(value, count):
    return jnp.where(value < 0, value + count, value)


def whole(space):
    return pl.BlockSpec(memory_space=space)


def pick_kernel(turn_number, mesh_counts, bounds, plan_ref, orbitals_ref, *refs):
    sems = refs[-1]
    own = linear_of(own_places(), mesh_counts)
    copies = []
    for number, out_ref in enumerate(refs[:-1]):
        column = 1 if number == 0 else 0
        cell = cell_of(plan_ref[turn_number, column, own], orbitals_ref.shape[:3])
        low = 0 if number == 0 else bounds[number - 1]
        copy = pltpu.make_async_copy(
            orbitals_ref.at[cell[0], cell[1], cell[2], pl.ds(low, out_ref.shape[0])],
            out_ref,
            sems.at[number],
        )
        copy.start()
        copies.append(copy)
    for copy in copies:
        copy.wait()


def picked(turn_number, mesh_counts, bounds, plan, orbitals):
    points, width = orbitals.shape[3:]
    lengths = [points] + [high - low for low, high in zip(bounds, bounds[1:])]
    return pl.pallas_call(
        functools.partial(pick_kernel, turn_number, mesh_counts, bounds),
        out_shape=tuple(jax.ShapeDtypeStruct((rows, width), orbitals.dtype) for rows in lengths),
        in_specs=[whole(pltpu.SMEM), whole(pl.ANY)],
        out_specs=(whole(pltpu.VMEM),) * len(lengths),
        scratch_shapes=[pltpu.SemaphoreType.DMA((len(lengths),))],
        compiler_params=pltpu.CompilerParams(vmem_limit_bytes=PICK_GRANT),
    )(plan, orbitals)


def mask_kernel(mesh_counts, cell_counts, plan_ref, occupation_ref, out_ref, rows, sem):
    places = own_places()
    copies = []
    turns = plan_ref.shape[0]
    for turn_number in range(turns):
        for column, shift in enumerate(hop_shifts(turn_number, mesh_counts)):
            sender = tuple(
                wrapped(place - step, count)
                for place, step, count in zip(places, shift, mesh_counts)
            )
            cell = cell_of(plan_ref[turn_number, column, linear_of(sender, mesh_counts)], cell_counts)
            point = tuple(
                place * count + inner for place, count, inner in zip(sender, cell_counts, cell)
            )
            entry = 2 * turn_number + column
            copy = pltpu.make_async_copy(
                occupation_ref.at[point[0], point[1], pl.ds(point[2], 1)],
                rows.at[pl.ds(entry, 1)],
                sem.at[entry],
            )
            copy.start()
            copies.append(copy)
    for copy in copies:
        copy.wait()
    held = rows[...].astype(jnp.float32)
    out_ref[...] = jnp.concatenate([held, held], axis=1)


def masks_of(mesh_counts, cell_counts, plan, occupation):
    entries = plan.shape[0] * 2
    bands = occupation.shape[3]
    return pl.pallas_call(
        functools.partial(mask_kernel, mesh_counts, cell_counts),
        out_shape=jax.ShapeDtypeStruct((entries, 2 * bands), jnp.float32),
        in_specs=[whole(pltpu.SMEM), whole(pl.ANY)],
        out_specs=whole(pltpu.VMEM),
        scratch_shapes=[
            pltpu.VMEM((entries, bands), occupation.dtype),
            pltpu.SemaphoreType.DMA((entries,)),
        ],
        compiler_params=pltpu.CompilerParams(vmem_limit_bytes=SMALL_GRANT),
        name="masks",
    )(plan, occupation)


def quarter_turn(block):
    bands = block.shape[1] // 2
    return jnp.concatenate([-block[:, bands:], block[:, :bands]], axis=1)


def folded(gram):
    bands = gram.shape[0] // 2
    top, bottom = gram[:bands], gram[bands:]
    return -(top + jnp.concatenate([bottom[:, bands:], -bottom[:, :bands]], axis=1))


def dot32(left, right, dims):
    return lax.dot_general(left, right, dims, preferred_element_type=jnp.float32)


def unturned(block):
    bands = block.shape[1] // 2
    return jnp.concatenate([block[:, bands:], -block[:, :bands]], axis=1)


def both_parts(rows_of, mask):
    masked = rows_of * mask
    return jnp.concatenate([masked, unturned(masked)], axis=0)


def steps(low, high, size):
    return [(start, min(start + size, high)) for start in range(low, high, size)]


def weigh_kernel(turn_number, mask_ref, kernel_ref, second_ref, weighed_ref, wide_ref):
    points = second_ref.shape[0]
    size = points // 4
    wide_ref[:points] = second_ref[...]
    wide_ref[points:] = quarter_turn(second_ref[...])
    entry = 2 * turn_number + 1
    mask = mask_ref[entry : entry + 1, :].astype(second_ref.dtype)
    for low, high in steps(0, points, size):
        left = both_parts(second_ref[low:high], mask)
        for start, stop in steps(0, points, size):
            density = dot32(left, second_ref[start:stop], CONTRACT_LAST)
            real, imag = density[: high - low], density[high - low :]
            weight_real = kernel_ref[0, 0, low:high, start:stop].astype(jnp.float32)
            weight_imag = kernel_ref[0, 1, low:high, start:stop].astype(jnp.float32)
            weighed_ref[low:high, start:stop] = (weight_real * real - weight_imag * imag).astype(
                jnp.bfloat16
            )
            weighed_ref[low:high, points + start : points + stop] = (
                weight_real * imag + weight_imag * real
            ).astype(jnp.bfloat16)


def pair_call(body, out_shape, scratch, flops, operands, aliases=None):
    return pl.pallas_call(
        body,
        out_shape=out_shape,
        in_specs=[whole(pltpu.VMEM)] * len(operands),
        out_specs=jax.tree.map(lambda _: whole(pltpu.VMEM), out_shape),
        scratch_shapes=scratch,
        input_output_aliases=aliases or {},
        cost_estimate=pl.CostEstimate(flops=flops, bytes_accessed=0, transcendentals=0),
        compiler_params=pltpu.CompilerParams(vmem_limit_bytes=PAIR_GRANT),
    )(*operands)


def weighed_by(turn_number, masks, kernel, second):
    points, width = second.shape
    return pair_call(
        functools.partial(weigh_kernel, turn_number),
        (
            jax.ShapeDtypeStruct((points, 2 * points), jnp.bfloat16),
            jax.ShapeDtypeStruct((2 * points, width), second.dtype),
        ),
        [],
        4 * points * points * width,
        (masks, kernel, second),
    )


def first_kernel(bounds, stage, *refs):
    low, high = bounds[stage : stage + 2]
    last = stage == len(bounds) - 2
    weighed_ref, refs = refs[0], refs[1:]
    pieces, refs = refs[: stage + 1] if last else refs[:1], refs[stage + 1 :] if last else refs[1:]
    earlier_ref = refs[0] if stage else None
    out_ref, mixed_ref = (refs[-2], refs[-1]) if last else (refs[-1], refs[-1])
    points = weighed_ref.shape[0]
    piece = pieces[-1][...]
    right = jnp.concatenate([piece, quarter_turn(piece)], axis=0)
    plain = (((1,), (0,)), ((), ()))
    for start, stop in steps(0, points, points // 4):
        left = jnp.concatenate(
            [weighed_ref[start:stop, low:high], weighed_ref[start:stop, points + low : points + high]],
            axis=1,
        )
        part = dot32(left, right, plain)
        if stage:
            part = part + earlier_ref[start:stop]
        mixed_ref[start:stop] = part.astype(mixed_ref.dtype)
    if last:
        gram = None
        for number, block_ref in enumerate(pieces):
            rows = slice(bounds[number], bounds[number + 1])
            part = dot32(block_ref[...], mixed_ref[rows], CONTRACT_FIRST)
            gram = part if gram is None else gram + part
        out_ref[...] = folded(gram).astype(out_ref.dtype)


def first_mixed(bounds, stage, weighed, pieces, earlier):
    points = weighed.shape[0]
    width = pieces[0].shape[1]
    last = stage == len(bounds) - 2
    operands = (weighed, *(pieces if last else pieces[-1:]))
    aliases = {}
    if stage:
        operands += (earlier,)
        aliases = {} if last else {len(operands) - 1: 0}
    shape = (width // 2, width) if last else (points, width)
    out = jax.ShapeDtypeStruct(shape, jnp.bfloat16 if last else jnp.float32)
    return pair_call(
        functools.partial(first_kernel, bounds, stage),
        out,
        [pltpu.VMEM((points, width), jnp.bfloat16)] if last else [],
        8 * points * (bounds[stage + 1] - bounds[stage]) * width,
        operands,
        aliases,
    )


def second_kernel(turn_number, bounds, stage, mask_ref, kernel_ref, wide_ref, *refs):
    pieces, refs = refs[: stage + 1], refs[stage + 1 :]
    last = stage == len(bounds) - 2
    _, high = bounds[stage : stage + 2]
    earlier_ref = refs[0] if stage else None
    held_ref, out_ref = refs[-1], refs[-3] if last else refs[-2]
    mixed_ref = refs[-2] if last else out_ref
    points = wide_ref.shape[0] // 2
    size = points // 4
    plain = (((1,), (0,)), ((), ()))
    entry = 2 * turn_number
    mask = mask_ref[entry : entry + 1, :].astype(wide_ref.dtype)
    slot = 0
    for number, rows_ref in enumerate(pieces):
        column_pieces = range(stage + 1) if number == stage else range(stage, stage + 1)
        column_low = bounds[column_pieces[0]]
        span = high - column_low
        for start, stop in steps(0, rows_ref.shape[0], size):
            row_low, row_high = bounds[number] + start, bounds[number] + stop
            count = stop - start
            left = both_parts(rows_ref[start:stop], mask)
            for column in column_pieces:
                for begin, end in steps(0, pieces[column].shape[0], size):
                    density = dot32(left, pieces[column][begin:end], CONTRACT_LAST)
                    real, imag = density[:count], density[count:]
                    columns = slice(bounds[column] + begin, bounds[column] + end)
                    at = bounds[column] + begin - column_low
                    weight_real = kernel_ref[0, 0, row_low:row_high, columns].astype(jnp.float32)
                    weight_imag = kernel_ref[0, 1, row_low:row_high, columns].astype(jnp.float32)
                    held_ref[slot, :count, at : at + end - begin] = (
                        weight_real * real + weight_imag * imag
                    ).astype(jnp.bfloat16)
                    held_ref[slot, :count, span + at : span + at + end - begin] = (
                        weight_real * imag - weight_imag * real
                    ).astype(jnp.bfloat16)
            if column_low:
                right = jnp.concatenate(
                    [wide_ref[column_low:high], wide_ref[points + column_low : points + high]], axis=0
                )
                part = dot32(held_ref[slot, :count, : 2 * span], right, plain)
            elif high == points:
                part = dot32(held_ref[slot, :count], wide_ref[...], plain)
            else:
                right = jnp.concatenate([wide_ref[:high], wide_ref[points : points + high]], axis=0)
                part = dot32(held_ref[slot, :count, : 2 * span], right, plain)
            if number < stage:
                part = part + earlier_ref[row_low:row_high]
            mixed_ref[row_low:row_high] = part.astype(mixed_ref.dtype)
            slot = 1 - slot
    if last:
        out_ref[...] = folded(dot32(wide_ref[:points], mixed_ref[...], CONTRACT_FIRST)).astype(
            out_ref.dtype
        )


def second_mixed(turn_number, bounds, stage, masks, kernel, wide, pieces, earlier):
    points, width = wide.shape[0] // 2, wide.shape[1]
    last = stage == len(bounds) - 2
    high, low = bounds[stage + 1], bounds[stage]
    operands = (masks, kernel, wide, *pieces)
    aliases = {}
    if stage:
        operands += (earlier,)
    shape = (width // 2, width) if last else (high, width)
    out = jax.ShapeDtypeStruct(shape, jnp.bfloat16 if last else jnp.float32)
    scratch = [pltpu.VMEM((2, points // 4, 2 * high), jnp.bfloat16)]
    if last:
        scratch = [pltpu.VMEM((points, width), jnp.bfloat16)] + scratch
    return pair_call(
        functools.partial(second_kernel, turn_number, bounds, stage),
        out,
        scratch,
        12 * (high * high - low * low) * width,
        operands,
        aliases,
    )


def total_kernel(mesh_counts, plan_ref, *refs):
    out_ref = refs[-1]
    own = linear_of(own_places(), mesh_counts)
    out_ref[...] = jnp.zeros_like(out_ref)
    for number, pair_ref in enumerate(refs[:-1]):
        turn_number = plan_ref.shape[0] - 1 - number
        for column in range(2):
            cell = cell_of(plan_ref[turn_number, 1 - column, own], out_ref.shape[:3])
            held = out_ref[cell[0], cell[1], cell[2]]
            out_ref[cell[0], cell[1], cell[2]] = held + pair_ref[column].astype(out_ref.dtype)


def totalled(mesh_counts, cell_counts, plan, pairs):
    return pl.pallas_call(
        functools.partial(total_kernel, mesh_counts),
        out_shape=jax.ShapeDtypeStruct((*cell_counts, *pairs[0].shape[1:]), jnp.float32),
        in_specs=[whole(pltpu.SMEM)] + [whole(pltpu.VMEM)] * len(pairs),
        out_specs=whole(pltpu.VMEM),
        compiler_params=pltpu.CompilerParams(vmem_limit_bytes=SMALL_GRANT),
        name="totals",
    )(plan, *pairs)


def on_device(orbitals, kernel, plan, occupation):
    mesh_counts = mesh_sizes()
    cell_counts = orbitals.shape[:3]
    turns = plan.shape[0]
    points = orbitals.shape[3]
    half = (0, 0, mesh_counts[2] // 2)
    order = tuple(reversed(range(turns)))
    bounds_of = {turn_number: (0, points) for turn_number in order}
    bounds_of[order[-1]] = (0, points // 2, points)
    sends = {
        turn_number: picked(turn_number, mesh_counts, bounds_of[turn_number], plan, orbitals)
        for turn_number in order
    }
    masks = masks_of(mesh_counts, cell_counts, plan, occupation)
    returned = {}
    done_before = ()
    for turn_number in order:
        bounds = bounds_of[turn_number]
        forward, partner = hop_shifts(turn_number, mesh_counts)
        second = moved(sends[turn_number][0], partner, mesh_counts)
        arrived = []
        for send in sends[turn_number][1:]:
            arrived.append(moved(send, forward, mesh_counts))
        weighed, wide = weighed_by(
            turn_number, after(masks, *done_before), kernel, second
        )
        first_block = second_block = None
        for stage in range(len(bounds) - 1):
            pieces = arrived[: stage + 1]
            if stage:
                weighed = after(weighed, second_block)
            first_block = first_mixed(bounds, stage, weighed, pieces, first_block)
            if stage == len(bounds) - 2:
                crossed = moved(first_block, half, mesh_counts)
            second_block = second_mixed(
                turn_number, bounds, stage, masks, kernel, wide, pieces, second_block
            )
        done_before = (second_block,)
        returned[turn_number] = moved(
            jnp.stack([second_block, crossed]), negated(partner), mesh_counts
        )
    blocks = [returned[turn_number] for turn_number in reversed(range(turns))]
    return totalled(mesh_counts, cell_counts, plan, blocks)


def solution(mesh):
    placed = (P("kx", "ky", "kz", None, None), P(("kx", "ky", "kz"), None, None, None), P(), P())

    return jax.shard_map(
        on_device,
        mesh=mesh,
        in_specs=placed,
        out_specs=P("kx", "ky", "kz", None, None),
        check_vma=False,
    )
```

time: 49 us -> 51.4 us (1.049)
  waiting for transfers between devices: 9.81 us -> 13.1 us
  Pallas kernels: 20.3 us -> 21.9 us
  local copies, waits for them, and re-layouts: 2.19 us -> 0.73 us
  starting transfers between devices: 16.3 us -> 15.3 us
    ppermute x8 -> x9, waiting for transfers between devices: 9.81 us -> 13.1 us  [moved(): return lax.ppermute(block, AXES, route)]
    pallas_call x4 -> x10, Pallas kernels: 18.2 us -> 19.8 us  [the longest x8 16.2 us: pair_call(): pl.pallas_call(body, out_shape=out_shape, in_specs=[whole(pltpu.VMEM)] *...]
    unnamed x6, local copies, waits for them, and re-layouts: 2.19 us -> 0.73 us
    ppermute x8 -> x9, starting transfers between devices: 16.3 us -> 15.3 us  [moved(): return lax.ppermute(block, AXES, route)]
  transfers between devices with their start and end apart: 8 -> 9, of which waited for: 4 -> 4; matrix products, arithmetic and copies ran while one was open for 0% -> 0% of each run, Pallas kernels for 33% -> 36%
where the time goes in v2:
time: 51.4 us; the launch traced here: 51.2 us
  Pallas kernels  21.9 us (43%)
  starting transfers between devices  15.3 us (30%)
  waiting for transfers between devices  13.1 us (25%)
  local copies, waits for them, and re-layouts  0.73 us (1%)
    pallas_call x8, Pallas kernels, pair_call(): pl.pallas_call(body, out_shape=out_shape, in_specs=[whole(pltpu.VMEM)] *...  16.2 us
    ppermute x9, starting transfers between devices, moved(): return lax.ppermute(block, AXES, route)  15.3 us
    ppermute x9, waiting for transfers between devices, moved(): return lax.ppermute(block, AXES, route)  13.1 us
    pallas_call x2, Pallas kernels, picked(): pl.pallas_call(functools.partial(pick_kernel, turn_number, mesh_counts, b...  3.59 us
    pallas_call x1, Pallas kernels, totalled(): pl.pallas_call(functools.partial(total_kernel, mesh_counts), out_shape=ja...  1.41 us
  transfers between devices with their start and end apart: 9, of which 4 were waited for; matrix products, arithmetic and copies ran while one was open for 0% of the time, Pallas kernels for 36%

profile of v2, /device:TPU:0, one launch (start us, length us, event | category | flops | bytes accessed | tf_op | source)
XLA Modules:
  0.0 51.2 jit_solution(15229461745091821126)
XLA Ops:
  0.0 0.0 copy-start.1
  0.0 0.0 copy-start.2
  0.0 0.7 %copy-done.2 = s32[2,2,32]{2,1,0:T(2,128)S(1)} copy-done((s32[2,2,32]{2,1,0:T(2,128)S(1)}, s32[2,2,32]{2,1,0:T(2,128)}, u32[]{:S(2)}) %copy-start.2) | copy-done | bytes 536
  0.7 0.0 copy-start
  0.7 1.9 %shard_map.46 = (bf16[1024,128]{1,0:T(8,128)(2,1)S(1)}, bf16[1024,128]{1,0:T(8,128)(2,1)S(1)}) custom-call(s32[2,2,32]{2,1,0:T(2,128)S(1)} %copy-done.2, bf16[4,4,1,1024,128]{4,3,2,1,0:T(8,128)(2,1)} %orbitals_ref.3), custom_call_target="tpu_custom_call" | custom-call | tf_op jit(solution)/shard_map/pallas_call | solution.py:102
  2.7 5.5 %collective-permute-start = (bf16[1024,128]{1,0:T(8,128)(2,1)S(1)}, bf16[1024,128]{1,0:T(8,128)(2,1)S(1)}, u32[]{:S(2)}, u32[]{:S(2)}) collective-permute-start(bf16[1024,128]{1,0:T(8,128)(2,1)S(1)} %get-tuple-element.16), channel_id=1, source_target_pairs={{0,23},{1,22},{2,17},{3,16},{4,19},{5,18},{6,21},{7,20},{8,31},{9,... | collective-permute-start | bytes 786440 | tf_op jit(solution)/shard_map/ppermute | solution.py:49
  8.2 0.6 %collective-permute-start.1 = (bf16[1024,128]{1,0:T(8,128)(2,1)S(1)}, bf16[1024,128]{1,0:T(8,128)(2,1)S(1)}, u32[]{:S(2)}, u32[]{:S(2)}) collective-permute-start(bf16[1024,128]{1,0:T(8,128)(2,1)S(1)} %get-tuple-element.18), channel_id=1, source_target_pairs={{0,22},{1,23},{2,16},{3,17},{4,18},{5,19},{6,20},{7,21},{8,30},{9,... | collective-permute-start | bytes 786440 | tf_op jit(solution)/shard_map/ppermute | solution.py:49
  8.8 1.7 %shard_map.50 = (bf16[1024,128]{1,0:T(8,128)(2,1)S(1)}, bf16[512,128]{1,0:T(8,128)(2,1)S(1)}, bf16[512,128]{1,0:T(8,128)(2,1)S(1)}) custom-call(s32[2,2,32]{2,1,0:T(2,128)S(1)} %copy-done.2, bf16[4,4,1,1024,128]{4,3,2,1,0:T(8,128)(2,1)} %orbitals_ref.3), custom_call_target="tpu_custom_call" | custom-call | tf_op jit(solution)/shard_map/pallas_call | solution.py:102
  10.5 2.3 %collective-permute-start.5 = (bf16[512,128]{1,0:T(8,128)(2,1)S(1)}, bf16[512,128]{1,0:T(8,128)(2,1)S(1)}, u32[]{:S(2)}, u32[]{:S(2)}) collective-permute-start(bf16[512,128]{1,0:T(8,128)(2,1)S(1)} %get-tuple-element.23), channel_id=1, source_target_pairs={{0,11},{1,10},{2,13},{3,12},{4,15},{5,14},{6,9},{7,8},{8,19},{9,18... | collective-permute-start | bytes 393224 | tf_op jit(solution)/shard_map/ppermute | solution.py:49
  12.8 0.1 collective-permute-start.6
  12.9 1.5 %collective-permute-start.4 = (bf16[1024,128]{1,0:T(8,128)(2,1)S(1)}, bf16[1024,128]{1,0:T(8,128)(2,1)S(1)}, u32[]{:S(2)}, u32[]{:S(2)}) collective-permute-start(bf16[1024,128]{1,0:T(8,128)(2,1)S(1)} %get-tuple-element.21), channel_id=1, source_target_pairs={{0,10},{1,11},{2,12},{3,13},{4,14},{5,15},{6,8},{7,9},{8,18},{9,19... | collective-permute-start | bytes 786440 | tf_op jit(solution)/shard_map/ppermute | solution.py:49
  14.4 0.0 copy-done.1
  14.4 0.8 %masks.1.mask_ref = f32[4,128]{1,0:T(4,128)S(1)} custom-call(s32[2,2,32]{2,1,0:T(2,128)S(1)} %copy-done.2, s32[16,16,2,64]{3,2,1,0:T(2,128)S(1)} %copy-done.1), custom_call_target="tpu_custom_call" | custom-call | tf_op jit(solution)/shard_map/masks/pallas_call | solution.py:143
  15.2 0.0 collective-permute-done.second_ref
  15.2 0.0 copy-done
  15.2 2.4 %shard_map.47 = (bf16[1024,2048]{1,0:T(8,128)(2,1)S(1)}, bf16[2048,128]{1,0:T(8,128)(2,1)S(1)}) custom-call(f32[4,128]{1,0:T(4,128)S(1)} %masks.1.mask_ref, bf16[1,2,1024,1024]{3,2,1,0:T(8,128)(2,1)S(1)} %copy-done, bf16[1024,128]{1,0:T(8,128)(2,1)S(1)} %collective-permute-done.second_ref), custom_call_target="tpu_custom_call" | custom-call | flops 536870912 | tf_op jit(solution)/shard_map/pallas_call | solution.py:209
  17.6 3.0 %collective-permute-done.1.refs_0_.refs_1_ = bf16[1024,128]{1,0:T(8,128)(2,1)S(1)} collective-permute-done((bf16[1024,128]{1,0:T(8,128)(2,1)S(1)}, bf16[1024,128]{1,0:T(8,128)(2,1)S(1)}, u32[]{:S(2)}, u32[]{:S(2)}) %collective-permute-start.1) | collective-permute-done | bytes 262176 | tf_op jit(solution)/shard_map/ppermute | solution.py:49
  20.5 3.7 %shard_map.48 = bf16[64,128]{1,0:T(8,128)(2,1)S(1)} custom-call(f32[4,128]{1,0:T(4,128)S(1)} %masks.1.mask_ref, bf16[1,2,1024,1024]{3,2,1,0:T(8,128)(2,1)S(1)} %copy-done, bf16[2048,128]{1,0:T(8,128)(2,1)S(1)} %get-tuple-element.17.wide_ref, bf16[1024,128]{1,0:T(8,128)(2,1)S(1)} %collective-permute-done.1.refs_0_.refs_1_), custom_call_target="tpu_custom_call" | custom-call | flops 1610612736 | tf_op jit(solution)/shard_map/pallas_call | solution.py:209
  24.3 1.5 %shard_map.49 = bf16[64,128]{1,0:T(8,128)(2,1)S(1)} custom-call(bf16[1024,2048]{1,0:T(8,128)(2,1)S(1)} %get-tuple-element.19.refs_0_, bf16[1024,128]{1,0:T(8,128)(2,1)S(1)} %collective-permute-done.1.refs_0_.refs_1_), custom_call_target="tpu_custom_call" | custom-call | flops 1073741824 | tf_op jit(solution)/shard_map/pallas_call | solution.py:209
  25.8 0.1 collective-permute-start.2
  26.0 7.5 %collective-permute-done.4.second_ref = bf16[1024,128]{1,0:T(8,128)(2,1)S(1)} collective-permute-done((bf16[1024,128]{1,0:T(8,128)(2,1)S(1)}, bf16[1024,128]{1,0:T(8,128)(2,1)S(1)}, u32[]{:S(2)}, u32[]{:S(2)}) %collective-permute-start.4) | collective-permute-done | bytes 262176 | tf_op jit(solution)/shard_map/ppermute | solution.py:49
  33.5 2.4 %shard_map.51 = (bf16[1024,2048]{1,0:T(8,128)(2,1)S(1)}, bf16[2048,128]{1,0:T(8,128)(2,1)S(1)}) custom-call(f32[4,128]{1,0:T(4,128)S(1)} %masks.1.mask_ref, bf16[1,2,1024,1024]{3,2,1,0:T(8,128)(2,1)S(1)} %copy-done, bf16[1024,128]{1,0:T(8,128)(2,1)S(1)} %collective-permute-done.4.second_ref), custom_call_target="tpu_custom_call" | custom-call | flops 536870912 | tf_op jit(solution)/shard_map/pallas_call | solution.py:209
  35.9 0.0 collective-permute-done.5.refs_0_.refs_1_
  35.9 1.1 %shard_map.52.refs_2_ = f32[512,128]{1,0:T(8,128)S(1)} custom-call(f32[4,128]{1,0:T(4,128)S(1)} %masks.1.mask_ref, bf16[1,2,1024,1024]{3,2,1,0:T(8,128)(2,1)S(1)} %copy-done, bf16[2048,128]{1,0:T(8,128)(2,1)S(1)} %get-tuple-element.22.wide_ref, bf16[512,128]{1,0:T(8,128)(2,1)S(1)} %collective-permute-done.5.refs_0_.refs_1_), custom_call_target="tpu_custom_call" | custom-call | flops 402653184 | tf_op jit(solution)/shard_map/pallas_call | solution.py:209
  37.0 0.8 %shard_map.54.refs_3_ = f32[1024,128]{1,0:T(8,128)S(1)} custom-call(bf16[1024,2048]{1,0:T(8,128)(2,1)S(1)} %get-tuple-element.26.refs_0_, bf16[512,128]{1,0:T(8,128)(2,1)S(1)} %collective-permute-done.5.refs_0_.refs_1_), custom_call_target="tpu_custom_call" | custom-call | flops 536870912 | tf_op jit(solution)/shard_map/pallas_call | solution.py:209
  37.8 0.0 collective-permute-done.6.refs_1_.refs_2_
  37.8 1.3 %shard_map.55 = bf16[64,128]{1,0:T(8,128)(2,1)S(1)} custom-call(bf16[1024,2048]{1,0:T(8,128)(2,1)S(1)} %get-tuple-element.26.refs_0_, bf16[512,128]{1,0:T(8,128)(2,1)S(1)} %collective-permute-done.5.refs_0_.refs_1_, bf16[512,128]{1,0:T(8,128)(2,1)S(1)} %collective-permute-done.6.refs_1_.refs_2_, f32[1024,128]{1,0:T(8,128)S(1)} %shard_map.54.refs_3_), custom_call_target="tpu_custom_call" | custom-call | flops 536870912 | tf_op jit(solution)/shard_map/pallas_call | solution.py:209
  39.1 0.1 collective-permute-start.7
  39.2 3.0 %shard_map.53 = bf16[64,128]{1,0:T(8,128)(2,1)S(1)} custom-call(f32[4,128]{1,0:T(4,128)S(1)} %masks.1.mask_ref, bf16[1,2,1024,1024]{3,2,1,0:T(8,128)(2,1)S(1)} %copy-done, bf16[2048,128]{1,0:T(8,128)(2,1)S(1)} %get-tuple-element.22.wide_ref, bf16[512,128]{1,0:T(8,128)(2,1)S(1)} %collective-permute-done.5.refs_0_.refs_1_, ...), custom_call_target="tpu_custom_call" | custom-call | flops 1207959552 | tf_op jit(solution)/shard_map/pallas_call | solution.py:209
  42.2 0.0 collective-permute-done.2
  42.2 2.7 %collective-permute-start.3 = (bf16[2,64,128]{2,1,0:T(8,128)(2,1)S(1)}, bf16[2,64,128]{2,1,0:T(8,128)(2,1)S(1)}, u32[]{:S(2)}, u32[]{:S(2)}) collective-permute-start(bf16[2,64,128]{2,1,0:T(8,128)(2,1)S(1)} %pad_maximum_fusion), channel_id=1, source_target_pairs={{0,19},{1,18},{2,21},{3,20},{4,23},{5,22},{6,17},{7,16},{8,27},{9,... | collective-permute-start | bytes 98312 | tf_op jit(solution)/shard_map/ppermute | solution.py:49
  44.9 0.0 collective-permute-done.7
  44.9 2.3 %collective-permute-start.8 = (bf16[2,64,128]{2,1,0:T(8,128)(2,1)S(1)}, bf16[2,64,128]{2,1,0:T(8,128)(2,1)S(1)}, u32[]{:S(2)}, u32[]{:S(2)}) collective-permute-start(bf16[2,64,128]{2,1,0:T(8,128)(2,1)S(1)} %pad_maximum_fusion.1), channel_id=1, source_target_pairs={{0,30},{1,31},{2,24},{3,25},{4,26},{5,27},{6,28},{7,29},{8,6},{9,7... | collective-permute-start | bytes 98312 | tf_op jit(solution)/shard_map/ppermute | solution.py:49
  47.2 1.1 %collective-permute-done.3.refs_0_ = bf16[2,64,128]{2,1,0:T(8,128)(2,1)S(1)} collective-permute-done((bf16[2,64,128]{2,1,0:T(8,128)(2,1)S(1)}, bf16[2,64,128]{2,1,0:T(8,128)(2,1)S(1)}, u32[]{:S(2)}, u32[]{:S(2)}) %collective-permute-start.3) | collective-permute-done | bytes 32800 | tf_op jit(solution)/shard_map/ppermute | solution.py:49
  48.3 1.5 %collective-permute-done.8.refs_1_ = bf16[2,64,128]{2,1,0:T(8,128)(2,1)S(1)} collective-permute-done((bf16[2,64,128]{2,1,0:T(8,128)(2,1)S(1)}, bf16[2,64,128]{2,1,0:T(8,128)(2,1)S(1)}, u32[]{:S(2)}, u32[]{:S(2)}) %collective-permute-start.8) | collective-permute-done | bytes 32800 | tf_op jit(solution)/shard_map/ppermute | solution.py:49
  49.8 1.4 %totals.1 = f32[4,4,1,64,128]{4,3,2,1,0:T(8,128)} custom-call(s32[2,2,32]{2,1,0:T(2,128)S(1)} %copy-done.2, bf16[2,64,128]{2,1,0:T(8,128)(2,1)S(1)} %collective-permute-done.3.refs_0_, bf16[2,64,128]{2,1,0:T(8,128)(2,1)S(1)} %collective-permute-done.8.refs_1_), custom_call_target="tpu_custom_call" | custom-call | tf_op jit(solution)/shard_map/totals/pallas_call | solution.py:376
  (2 shorter events, 0.0 us)
Async XLA Ops:
  0.0 14.4 %copy-start.1 = (s32[16,16,2,64]{3,2,1,0:T(2,128)S(1)}, s32[16,16,2,64]{3,2,1,0:T(2,128)}, u32[]{:S(2)}) copy-start(s32[16,16,2,64]{3,2,1,0:T(2,128)} %occupation_ref.1) | copy-start | bytes 393220
  0.0 0.7 %copy-start.2 = (s32[2,2,32]{2,1,0:T(2,128)S(1)}, s32[2,2,32]{2,1,0:T(2,128)}, u32[]{:S(2)}) copy-start(s32[2,2,32]{2,1,0:T(2,128)} %plan_ref.7) | copy-start | bytes 1540
  0.7 14.4 %copy-start = (bf16[1,2,1024,1024]{3,2,1,0:T(8,128)(2,1)S(1)}, bf16[1,2,1024,1024]{3,2,1,0:T(8,128)(2,1)}, u32[]{:S(2)}) copy-start(bf16[1,2,1024,1024]{3,2,1,0:T(8,128)(2,1)} %kernel_ref.9) | copy-start | bytes 12582916
  2.7 12.5 %collective-permute-start = (bf16[1024,128]{1,0:T(8,128)(2,1)S(1)}, bf16[1024,128]{1,0:T(8,128)(2,1)S(1)}, u32[]{:S(2)}, u32[]{:S(2)}) collective-permute-start(bf16[1024,128]{1,0:T(8,128)(2,1)S(1)} %get-tuple-element.16), channel_id=1, source_target_pairs={{0,23},{1,22},{2,17},{3,16},{4,19},{5,18},{6,21},{7,20},{8,31},{9,... | collective-permute-start | bytes 786440 | tf_op jit(solution)/shard_map/ppermute | solution.py:49
  8.2 12.4 %collective-permute-start.1 = (bf16[1024,128]{1,0:T(8,128)(2,1)S(1)}, bf16[1024,128]{1,0:T(8,128)(2,1)S(1)}, u32[]{:S(2)}, u32[]{:S(2)}) collective-permute-start(bf16[1024,128]{1,0:T(8,128)(2,1)S(1)} %get-tuple-element.18), channel_id=1, source_target_pairs={{0,22},{1,23},{2,16},{3,17},{4,18},{5,19},{6,20},{7,21},{8,30},{9,... | collective-permute-start | bytes 786440 | tf_op jit(solution)/shard_map/ppermute | solution.py:49
  10.5 25.4 %collective-permute-start.5 = (bf16[512,128]{1,0:T(8,128)(2,1)S(1)}, bf16[512,128]{1,0:T(8,128)(2,1)S(1)}, u32[]{:S(2)}, u32[]{:S(2)}) collective-permute-start(bf16[512,128]{1,0:T(8,128)(2,1)S(1)} %get-tuple-element.23), channel_id=1, source_target_pairs={{0,11},{1,10},{2,13},{3,12},{4,15},{5,14},{6,9},{7,8},{8,19},{9,18... | collective-permute-start | bytes 393224 | tf_op jit(solution)/shard_map/ppermute | solution.py:49
  12.8 25.0 %collective-permute-start.6 = (bf16[512,128]{1,0:T(8,128)(2,1)S(1)}, bf16[512,128]{1,0:T(8,128)(2,1)S(1)}, u32[]{:S(2)}, u32[]{:S(2)}) collective-permute-start(bf16[512,128]{1,0:T(8,128)(2,1)S(1)} %get-tuple-element.24), channel_id=1, source_target_pairs={{0,11},{1,10},{2,13},{3,12},{4,15},{5,14},{6,9},{7,8},{8,19},{9,18... | collective-permute-start | bytes 393224 | tf_op jit(solution)/shard_map/ppermute | solution.py:49
  12.9 20.6 %collective-permute-start.4 = (bf16[1024,128]{1,0:T(8,128)(2,1)S(1)}, bf16[1024,128]{1,0:T(8,128)(2,1)S(1)}, u32[]{:S(2)}, u32[]{:S(2)}) collective-permute-start(bf16[1024,128]{1,0:T(8,128)(2,1)S(1)} %get-tuple-element.21), channel_id=1, source_target_pairs={{0,10},{1,11},{2,12},{3,13},{4,14},{5,15},{6,8},{7,9},{8,18},{9,19... | collective-permute-start | bytes 786440 | tf_op jit(solution)/shard_map/ppermute | solution.py:49
  25.8 16.3 %collective-permute-start.2 = (bf16[64,128]{1,0:T(8,128)(2,1)S(1)}, bf16[64,128]{1,0:T(8,128)(2,1)S(1)}, u32[]{:S(2)}, u32[]{:S(2)}) collective-permute-start(bf16[64,128]{1,0:T(8,128)(2,1)S(1)} %shard_map.49), channel_id=1, source_target_pairs={{0,1},{1,0},{2,3},{3,2},{4,5},{5,4},{6,7},{7,6},{8,9},{9,8},{10,11... | collective-permute-start | bytes 49160 | tf_op jit(solution)/shard_map/ppermute | solution.py:49
  39.1 5.8 %collective-permute-start.7 = (bf16[64,128]{1,0:T(8,128)(2,1)S(1)}, bf16[64,128]{1,0:T(8,128)(2,1)S(1)}, u32[]{:S(2)}, u32[]{:S(2)}) collective-permute-start(bf16[64,128]{1,0:T(8,128)(2,1)S(1)} %shard_map.55), channel_id=1, source_target_pairs={{0,1},{1,0},{2,3},{3,2},{4,5},{5,4},{6,7},{7,6},{8,9},{9,8},{10,11... | collective-permute-start | bytes 49160 | tf_op jit(solution)/shard_map/ppermute | solution.py:49
  42.2 6.1 %collective-permute-start.3 = (bf16[2,64,128]{2,1,0:T(8,128)(2,1)S(1)}, bf16[2,64,128]{2,1,0:T(8,128)(2,1)S(1)}, u32[]{:S(2)}, u32[]{:S(2)}) collective-permute-start(bf16[2,64,128]{2,1,0:T(8,128)(2,1)S(1)} %pad_maximum_fusion), channel_id=1, source_target_pairs={{0,19},{1,18},{2,21},{3,20},{4,23},{5,22},{6,17},{7,16},{8,27},{9,... | collective-permute-start | bytes 98312 | tf_op jit(solution)/shard_map/ppermute | solution.py:49
  44.9 4.9 %collective-permute-start.8 = (bf16[2,64,128]{2,1,0:T(8,128)(2,1)S(1)}, bf16[2,64,128]{2,1,0:T(8,128)(2,1)S(1)}, u32[]{:S(2)}, u32[]{:S(2)}) collective-permute-start(bf16[2,64,128]{2,1,0:T(8,128)(2,1)S(1)} %pad_maximum_fusion.1), channel_id=1, source_target_pairs={{0,30},{1,31},{2,24},{3,25},{4,26},{5,27},{6,28},{7,29},{8,6},{9,7... | collective-permute-start | bytes 98312 | tf_op jit(solution)/shard_map/ppermute | solution.py:49

commit v3 on v2

--- a/solution.py
+++ b/solution.py
@@ -12,6 +12,12 @@
 SMALL_GRANT = 4 << 20
 PICK_GRANT = 52 << 20
 PAIR_GRANT = 24 << 20
+WIDEN_GRANT = 24 << 20
+WEIGH_ROWS = 4
+WEIGH_COLS = 4
+SECOND_TALL = 4
+SECOND_ROWS = 4
+SECOND_COLS = 4
 CONTRACT_LAST = (((1,), (1,)), ((), ()))
 CONTRACT_FIRST = (((0,), (0,)), ((), ()))
 
@@ -156,7 +162,9 @@
 
 def quarter_turn(block):
     bands = block.shape[1] // 2
-    return jnp.concatenate([-block[:, bands:], block[:, :bands]], axis=1)
+    wide = pltpu.roll(block.astype(jnp.float32), bands, 1)
+    lane = lax.broadcasted_iota(jnp.int32, (1, block.shape[1]), 1)
+    return (wide * jnp.where(lane < bands, -1.0, 1.0)).astype(block.dtype)
 
 
 def folded(gram):
@@ -169,40 +177,47 @@
     return lax.dot_general(left, right, dims, preferred_element_type=jnp.float32)
 
 
-def unturned(block):
-    bands = block.shape[1] // 2
-    return jnp.concatenate([block[:, bands:], -block[:, :bands]], axis=1)
-
-
-def both_parts(rows_of, mask):
-    masked = rows_of * mask
-    return jnp.concatenate([masked, unturned(masked)], axis=0)
-
-
 def steps(low, high, size):
     return [(start, min(start + size, high)) for start in range(low, high, size)]
 
 
 def weigh_kernel(turn_number, mask_ref, kernel_ref, second_ref, weighed_ref, wide_ref):
     points = second_ref.shape[0]
-    size = points // 4
     wide_ref[:points] = second_ref[...]
     wide_ref[points:] = quarter_turn(second_ref[...])
     entry = 2 * turn_number + 1
     mask = mask_ref[entry : entry + 1, :].astype(second_ref.dtype)
-    for low, high in steps(0, points, size):
-        left = both_parts(second_ref[low:high], mask)
-        for start, stop in steps(0, points, size):
-            density = dot32(left, second_ref[start:stop], CONTRACT_LAST)
-            real, imag = density[: high - low], density[high - low :]
-            weight_real = kernel_ref[0, 0, low:high, start:stop].astype(jnp.float32)
-            weight_imag = kernel_ref[0, 1, low:high, start:stop].astype(jnp.float32)
+    for start, stop in steps(0, points, points // WEIGH_COLS):
+        right = second_ref[start:stop]
+        for low, high in steps(0, points, points // WEIGH_ROWS):
+            real = dot32(second_ref[low:high] * mask, right, CONTRACT_LAST)
+            imag = dot32(wide_ref[points + low : points + high] * -mask, right, CONTRACT_LAST)
+            weight_real = kernel_ref[0, low:high, start:stop]
+            weight_imag = kernel_ref[1, low:high, start:stop]
             weighed_ref[low:high, start:stop] = (weight_real * real - weight_imag * imag).astype(
                 jnp.bfloat16
             )
             weighed_ref[low:high, points + start : points + stop] = (
                 weight_real * imag + weight_imag * real
             ).astype(jnp.bfloat16)
+
+
+def widen_kernel(kernel_ref, out_ref):
+    out_ref[...] = kernel_ref[0].astype(jnp.float32)
+
+
+def widened(kernel):
+    parts, rows, columns = kernel.shape[1:]
+    size = rows // 4
+    return pl.pallas_call(
+        widen_kernel,
+        grid=(rows // size,),
+        out_shape=jax.ShapeDtypeStruct((parts, rows, columns), jnp.float32),
+        in_specs=[pl.BlockSpec((1, parts, size, columns), lambda step: (0, 0, step, 0))],
+        out_specs=pl.BlockSpec((parts, size, columns), lambda step: (0, step, 0)),
+        compiler_params=pltpu.CompilerParams(vmem_limit_bytes=WIDEN_GRANT),
+        name="widen",
+    )(kernel)
 
 
 def pair_call(body, out_shape, scratch, flops, operands, aliases=None):
@@ -290,7 +305,6 @@
     held_ref, out_ref = refs[-1], refs[-3] if last else refs[-2]
     mixed_ref = refs[-2] if last else out_ref
     points = wide_ref.shape[0] // 2
-    size = points // 4
     plain = (((1,), (0,)), ((), ()))
     entry = 2 * turn_number
     mask = mask_ref[entry : entry + 1, :].astype(wide_ref.dtype)
@@ -299,37 +313,39 @@
         column_pieces = range(stage + 1) if number == stage else range(stage, stage + 1)
         column_low = bounds[column_pieces[0]]
         span = high - column_low
-        for start, stop in steps(0, rows_ref.shape[0], size):
-            row_low, row_high = bounds[number] + start, bounds[number] + stop
-            count = stop - start
-            left = both_parts(rows_ref[start:stop], mask)
+        if column_low or high < points:
+            right = jnp.concatenate(
+                [wide_ref[column_low:high], wide_ref[points + column_low : points + high]], axis=0
+            )
+        else:
+            right = wide_ref[...]
+        for start, stop in steps(0, rows_ref.shape[0], points // SECOND_TALL):
+            turned = quarter_turn(rows_ref[start:stop]) * -mask
+            kept = rows_ref[start:stop] * mask
             for column in column_pieces:
-                for begin, end in steps(0, pieces[column].shape[0], size):
-                    density = dot32(left, pieces[column][begin:end], CONTRACT_LAST)
-                    real, imag = density[:count], density[count:]
+                for begin, end in steps(0, pieces[column].shape[0], points // SECOND_COLS):
+                    across = pieces[column][begin:end]
                     columns = slice(bounds[column] + begin, bounds[column] + end)
                     at = bounds[column] + begin - column_low
-                    weight_real = kernel_ref[0, 0, row_low:row_high, columns].astype(jnp.float32)
-                    weight_imag = kernel_ref[0, 1, row_low:row_high, columns].astype(jnp.float32)
-                    held_ref[slot, :count, at : at + end - begin] = (
-                        weight_real * real + weight_imag * imag
-                    ).astype(jnp.bfloat16)
-                    held_ref[slot, :count, span + at : span + at + end - begin] = (
-                        weight_real * imag - weight_imag * real
-                    ).astype(jnp.bfloat16)
-            if column_low:
-                right = jnp.concatenate(
-                    [wide_ref[column_low:high], wide_ref[points + column_low : points + high]], axis=0
-                )
-                part = dot32(held_ref[slot, :count, : 2 * span], right, plain)
-            elif high == points:
-                part = dot32(held_ref[slot, :count], wide_ref[...], plain)
-            else:
-                right = jnp.concatenate([wide_ref[:high], wide_ref[points : points + high]], axis=0)
-                part = dot32(held_ref[slot, :count, : 2 * span], right, plain)
+                    for top, bottom in steps(0, stop - start, points // SECOND_ROWS):
+                        real = dot32(kept[top:bottom], across, CONTRACT_LAST)
+                        imag = dot32(turned[top:bottom], across, CONTRACT_LAST)
+                        rows = slice(
+                            bounds[number] + start + top, bounds[number] + start + bottom
+                        )
+                        weight_real = kernel_ref[0, rows, columns]
+                        weight_imag = kernel_ref[1, rows, columns]
+                        held_ref[slot, top:bottom, at : at + end - begin] = (
+                            weight_real * real + weight_imag * imag
+                        ).astype(jnp.bfloat16)
+                        held_ref[slot, top:bottom, span + at : span + at + end - begin] = (
+                            weight_real * imag - weight_imag * real
+                        ).astype(jnp.bfloat16)
+            part = dot32(held_ref[slot, : stop - start, : 2 * span], right, plain)
+            rows = slice(bounds[number] + start, bounds[number] + stop)
             if number < stage:
-                part = part + earlier_ref[row_low:row_high]
-            mixed_ref[row_low:row_high] = part.astype(mixed_ref.dtype)
+                part = part + earlier_ref[rows]
+            mixed_ref[rows] = part.astype(mixed_ref.dtype)
             slot = 1 - slot
     if last:
         out_ref[...] = folded(dot32(wide_ref[:points], mixed_ref[...], CONTRACT_FIRST)).astype(
@@ -347,7 +363,7 @@
         operands += (earlier,)
     shape = (width // 2, width) if last else (high, width)
     out = jax.ShapeDtypeStruct(shape, jnp.bfloat16 if last else jnp.float32)
-    scratch = [pltpu.VMEM((2, points // 4, 2 * high), jnp.bfloat16)]
+    scratch = [pltpu.VMEM((2, points // SECOND_TALL, 2 * high), jnp.bfloat16)]
     if last:
         scratch = [pltpu.VMEM((points, width), jnp.bfloat16)] + scratch
     return pair_call(
@@ -391,12 +407,13 @@
     half = (0, 0, mesh_counts[2] // 2)
     order = tuple(reversed(range(turns)))
     bounds_of = {turn_number: (0, points) for turn_number in order}
-    bounds_of[order[-1]] = (0, points // 2, points)
+    bounds_of[order[-1]] = (0, points // 2, points * 3 // 4, points)
     sends = {
         turn_number: picked(turn_number, mesh_counts, bounds_of[turn_number], plan, orbitals)
         for turn_number in order
     }
     masks = masks_of(mesh_counts, cell_counts, plan, occupation)
+    kernel = widened(after(kernel, masks))
     returned = {}
     done_before = ()
     for turn_number in order:

time: 51.4 us -> 50 us (0.973)
  starting transfers between devices: 15.3 us -> 18.6 us
  waiting for transfers between devices: 13.1 us -> 10.1 us
  Pallas kernels: 21.9 us -> 20.2 us
    ppermute x9 -> x10, starting transfers between devices: 15.3 us -> 18.6 us  [moved(): return lax.ppermute(block, AXES, route)]
    pallas_call x8 -> x10, Pallas kernels: 16.2 us -> 13 us  [pair_call(): pl.pallas_call(body, out_shape=out_shape, in_specs=[whole(pltpu.VMEM)] *...]
    ppermute x9 -> x10, waiting for transfers between devices: 13.1 us -> 10.1 us  [moved(): return lax.ppermute(block, AXES, route)]
    pallas_call x0 -> x1, Pallas kernels: none -> 1.45 us  [widened(): pl.pallas_call(widen_kernel, grid=(rows // size,), out_shape=jax.ShapeDty...]
  transfers between devices with their start and end apart: 9 -> 10, of which waited for: 4 -> 3; matrix products, arithmetic and copies ran while one was open for 0% -> 0% of each run, Pallas kernels for 36% -> 34%
where the time goes in v3:
time: 50 us; the launch traced here: 49.9 us
  Pallas kernels  20.2 us (40%)
  starting transfers between devices  18.6 us (37%)
  waiting for transfers between devices  10.1 us (20%)
  local copies, waits for them, and re-layouts  0.73 us (1%)
    ppermute x10, starting transfers between devices, moved(): return lax.ppermute(block, AXES, route)  18.6 us
    pallas_call x10, Pallas kernels, pair_call(): pl.pallas_call(body, out_shape=out_shape, in_specs=[whole(pltpu.VMEM)] *...  13 us
    ppermute x10, waiting for transfers between devices, moved(): return lax.ppermute(block, AXES, route)  10.1 us
    pallas_call x2, Pallas kernels, picked(): pl.pallas_call(functools.partial(pick_kernel, turn_number, mesh_counts, b...  3.56 us
    pallas_call x1, Pallas kernels, widened(): pl.pallas_call(widen_kernel, grid=(rows // size,), out_shape=jax.ShapeDty...  1.45 us
    pallas_call x1, Pallas kernels, totalled(): pl.pallas_call(functools.partial(total_kernel, mesh_counts), out_shape=ja...  1.41 us
  transfers between devices with their start and end apart: 10, of which 3 were waited for; matrix products, arithmetic and copies ran while one was open for 0% of the time, Pallas kernels for 34%

profile of v3, /device:TPU:0, one launch (start us, length us, event | category | flops | bytes accessed | tf_op | source)
XLA Modules:
  0.0 49.9 jit_solution(13565192667663168584)
XLA Ops:
  0.0 0.0 copy-start.1
  0.0 0.0 copy-start.2
  0.0 0.7 %copy-done.2 = s32[2,2,32]{2,1,0:T(2,128)S(1)} copy-done((s32[2,2,32]{2,1,0:T(2,128)S(1)}, s32[2,2,32]{2,1,0:T(2,128)}, u32[]{:S(2)}) %copy-start.2) | copy-done | bytes 536
  0.7 0.0 copy-start
  0.7 1.9 %shard_map.46 = (bf16[1024,128]{1,0:T(8,128)(2,1)S(1)}, bf16[1024,128]{1,0:T(8,128)(2,1)S(1)}) custom-call(s32[2,2,32]{2,1,0:T(2,128)S(1)} %copy-done.2, bf16[4,4,1,1024,128]{4,3,2,1,0:T(8,128)(2,1)} %orbitals_ref.3), custom_call_target="tpu_custom_call" | custom-call | tf_op jit(solution)/shard_map/pallas_call | solution.py:108
  2.7 5.5 %collective-permute-start = (bf16[1024,128]{1,0:T(8,128)(2,1)S(1)}, bf16[1024,128]{1,0:T(8,128)(2,1)S(1)}, u32[]{:S(2)}, u32[]{:S(2)}) collective-permute-start(bf16[1024,128]{1,0:T(8,128)(2,1)S(1)} %get-tuple-element.20), channel_id=1, source_target_pairs={{0,23},{1,22},{2,17},{3,16},{4,19},{5,18},{6,21},{7,20},{8,31},{9,... | collective-permute-start | bytes 786440 | tf_op jit(solution)/shard_map/ppermute | solution.py:55
  8.2 0.6 %collective-permute-start.1 = (bf16[1024,128]{1,0:T(8,128)(2,1)S(1)}, bf16[1024,128]{1,0:T(8,128)(2,1)S(1)}, u32[]{:S(2)}, u32[]{:S(2)}) collective-permute-start(bf16[1024,128]{1,0:T(8,128)(2,1)S(1)} %get-tuple-element.22), channel_id=1, source_target_pairs={{0,22},{1,23},{2,16},{3,17},{4,18},{5,19},{6,20},{7,21},{8,30},{9,... | collective-permute-start | bytes 786440 | tf_op jit(solution)/shard_map/ppermute | solution.py:55
  8.8 1.6 %shard_map.50 = (bf16[1024,128]{1,0:T(8,128)(2,1)S(1)}, bf16[512,128]{1,0:T(8,128)(2,1)S(1)}, bf16[256,128]{1,0:T(8,128)(2,1)S(1)}, bf16[256,128]{1,0:T(8,128)(2,1)S(1)}) custom-call(s32[2,2,32]{2,1,0:T(2,128)S(1)} %copy-done.2, bf16[4,4,1,1024,128]{4,3,2,1,0:T(8,128)(2,1)} %orbitals_ref.3), custom_call_target="tpu_custom_call" | custom-call | tf_op jit(solution)/shard_map/pallas_call | solution.py:108
  10.5 2.3 %collective-permute-start.6 = (bf16[256,128]{1,0:T(8,128)(2,1)S(1)}, bf16[256,128]{1,0:T(8,128)(2,1)S(1)}, u32[]{:S(2)}, u32[]{:S(2)}) collective-permute-start(bf16[256,128]{1,0:T(8,128)(2,1)S(1)} %get-tuple-element.28), channel_id=1, source_target_pairs={{0,11},{1,10},{2,13},{3,12},{4,15},{5,14},{6,9},{7,8},{8,19},{9,18... | collective-permute-start | bytes 196616 | tf_op jit(solution)/shard_map/ppermute | solution.py:55
  12.8 0.1 collective-permute-start.7
  12.9 1.5 %collective-permute-start.5 = (bf16[512,128]{1,0:T(8,128)(2,1)S(1)}, bf16[512,128]{1,0:T(8,128)(2,1)S(1)}, u32[]{:S(2)}, u32[]{:S(2)}) collective-permute-start(bf16[512,128]{1,0:T(8,128)(2,1)S(1)} %get-tuple-element.27), channel_id=1, source_target_pairs={{0,11},{1,10},{2,13},{3,12},{4,15},{5,14},{6,9},{7,8},{8,19},{9,18... | collective-permute-start | bytes 393224 | tf_op jit(solution)/shard_map/ppermute | solution.py:55
  14.4 0.0 copy-done.1
  14.4 0.8 %masks.1.mask_ref = f32[4,128]{1,0:T(4,128)S(1)} custom-call(s32[2,2,32]{2,1,0:T(2,128)S(1)} %copy-done.2, s32[16,16,2,64]{3,2,1,0:T(2,128)S(1)} %copy-done.1), custom_call_target="tpu_custom_call" | custom-call | tf_op jit(solution)/shard_map/masks/pallas_call | solution.py:149
  15.1 0.0 copy-done
  15.1 1.5 %widen.1.kernel_ref = f32[2,1024,1024]{2,1,0:T(8,128)S(1)} custom-call(bf16[1,2,1024,1024]{3,2,1,0:T(8,128)(2,1)S(1)} %copy-done), custom_call_target="tpu_custom_call" | custom-call | tf_op jit(solution)/shard_map/widen/pallas_call | solution.py:212
  16.6 0.0 collective-permute-done.second_ref
  16.6 3.3 %collective-permute-start.4 = (bf16[1024,128]{1,0:T(8,128)(2,1)S(1)}, bf16[1024,128]{1,0:T(8,128)(2,1)S(1)}, u32[]{:S(2)}, u32[]{:S(2)}) collective-permute-start(bf16[1024,128]{1,0:T(8,128)(2,1)S(1)} %get-tuple-element.25), channel_id=1, source_target_pairs={{0,10},{1,11},{2,12},{3,13},{4,14},{5,15},{6,8},{7,9},{8,18},{9,19... | collective-permute-start | bytes 786440 | tf_op jit(solution)/shard_map/ppermute | solution.py:55
  20.0 1.5 %shard_map.47 = (bf16[1024,2048]{1,0:T(8,128)(2,1)S(1)}, bf16[2048,128]{1,0:T(8,128)(2,1)S(1)}) custom-call(f32[4,128]{1,0:T(4,128)S(1)} %masks.1.mask_ref, f32[2,1024,1024]{2,1,0:T(8,128)S(1)} %widen.1.kernel_ref, bf16[1024,128]{1,0:T(8,128)(2,1)S(1)} %collective-permute-done.second_ref), custom_call_target="tpu_custom_call" | custom-call | flops 536870912 | tf_op jit(solution)/shard_map/pallas_call | solution.py:224
  21.5 0.0 collective-permute-done.1.refs_0_.refs_1_
  21.5 2.8 %shard_map.48 = bf16[64,128]{1,0:T(8,128)(2,1)S(1)} custom-call(f32[4,128]{1,0:T(4,128)S(1)} %masks.1.mask_ref, f32[2,1024,1024]{2,1,0:T(8,128)S(1)} %widen.1.kernel_ref, bf16[2048,128]{1,0:T(8,128)(2,1)S(1)} %get-tuple-element.21.wide_ref, bf16[1024,128]{1,0:T(8,128)(2,1)S(1)} %collective-permute-done.1.refs_0_.refs_1_), custom_call_target="tpu_custom_call" | custom-call | flops 1610612736 | tf_op jit(solution)/shard_map/pallas_call | solution.py:224
  24.3 1.5 %shard_map.49 = bf16[64,128]{1,0:T(8,128)(2,1)S(1)} custom-call(bf16[1024,2048]{1,0:T(8,128)(2,1)S(1)} %get-tuple-element.23.refs_0_, bf16[1024,128]{1,0:T(8,128)(2,1)S(1)} %collective-permute-done.1.refs_0_.refs_1_), custom_call_target="tpu_custom_call" | custom-call | flops 1073741824 | tf_op jit(solution)/shard_map/pallas_call | solution.py:224
  25.8 0.1 collective-permute-start.2
  26.0 7.5 %collective-permute-done.4.second_ref = bf16[1024,128]{1,0:T(8,128)(2,1)S(1)} collective-permute-done((bf16[1024,128]{1,0:T(8,128)(2,1)S(1)}, bf16[1024,128]{1,0:T(8,128)(2,1)S(1)}, u32[]{:S(2)}, u32[]{:S(2)}) %collective-permute-start.4) | collective-permute-done | bytes 262176 | tf_op jit(solution)/shard_map/ppermute | solution.py:55
  33.5 1.6 %shard_map.51 = (bf16[1024,2048]{1,0:T(8,128)(2,1)S(1)}, bf16[2048,128]{1,0:T(8,128)(2,1)S(1)}) custom-call(f32[4,128]{1,0:T(4,128)S(1)} %masks.1.mask_ref, f32[2,1024,1024]{2,1,0:T(8,128)S(1)} %widen.1.kernel_ref, bf16[1024,128]{1,0:T(8,128)(2,1)S(1)} %collective-permute-done.4.second_ref), custom_call_target="tpu_custom_call" | custom-call | flops 536870912 | tf_op jit(solution)/shard_map/pallas_call | solution.py:224
  35.1 0.0 collective-permute-done.5.refs_0_.refs_1_
  35.1 0.9 %shard_map.52.refs_2_ = f32[512,128]{1,0:T(8,128)S(1)} custom-call(f32[4,128]{1,0:T(4,128)S(1)} %masks.1.mask_ref, f32[2,1024,1024]{2,1,0:T(8,128)S(1)} %widen.1.kernel_ref, bf16[2048,128]{1,0:T(8,128)(2,1)S(1)} %get-tuple-element.26.wide_ref, bf16[512,128]{1,0:T(8,128)(2,1)S(1)} %collective-permute-done.5.refs_0_.refs_1_), custom_call_target="tpu_custom_call" | custom-call | flops 402653184 | tf_op jit(solution)/shard_map/pallas_call | solution.py:224
  36.0 0.0 collective-permute-done.6.refs_1_.refs_2_
  36.0 1.1 %shard_map.53.refs_3_ = f32[768,128]{1,0:T(8,128)S(1)} custom-call(f32[4,128]{1,0:T(4,128)S(1)} %masks.1.mask_ref, f32[2,1024,1024]{2,1,0:T(8,128)S(1)} %widen.1.kernel_ref, bf16[2048,128]{1,0:T(8,128)(2,1)S(1)} %get-tuple-element.26.wide_ref, bf16[512,128]{1,0:T(8,128)(2,1)S(1)} %collective-permute-done.5.refs_0_.refs_1_, ...), custom_call_target="tpu_custom_call" | custom-call | flops 503316480 | tf_op jit(solution)/shard_map/pallas_call | solution.py:224
  37.1 0.7 %shard_map.55.refs_2_ = f32[1024,128]{1,0:T(8,128)S(1)} custom-call(bf16[1024,2048]{1,0:T(8,128)(2,1)S(1)} %get-tuple-element.32.refs_0_, bf16[512,128]{1,0:T(8,128)(2,1)S(1)} %collective-permute-done.5.refs_0_.refs_1_), custom_call_target="tpu_custom_call" | custom-call | flops 536870912 | tf_op jit(solution)/shard_map/pallas_call | solution.py:224
  37.8 0.5 %shard_map.56.refs_4_ = f32[1024,128]{1,0:T(8,128)S(1)} custom-call(bf16[1024,2048]{1,0:T(8,128)(2,1)S(1)} %get-tuple-element.32.refs_0_, bf16[256,128]{1,0:T(8,128)(2,1)S(1)} %collective-permute-done.6.refs_1_.refs_2_, f32[1024,128]{1,0:T(8,128)S(1)} %shard_map.55.refs_2_), custom_call_target="tpu_custom_call", output_to_operand_aliasing={{}: (2, {})} | custom-call | flops 268435456 | tf_op jit(solution)/shard_map/pallas_call | solution.py:224
  38.3 0.0 collective-permute-done.7.refs_2_.refs_3_
  38.3 0.7 %shard_map.57 = bf16[64,128]{1,0:T(8,128)(2,1)S(1)} custom-call(bf16[1024,2048]{1,0:T(8,128)(2,1)S(1)} %get-tuple-element.32.refs_0_, bf16[512,128]{1,0:T(8,128)(2,1)S(1)} %collective-permute-done.5.refs_0_.refs_1_, bf16[256,128]{1,0:T(8,128)(2,1)S(1)} %collective-permute-done.6.refs_1_.refs_2_, bf16[256,128]{1,0:T(8,128)(2,1)S(1)} %collective-permute-done.7.refs_2_.refs_3_, ...), custom_call_target="tpu_custom_call" | custom-call | flops 268435456 | tf_op jit(solution)/shard_map/pallas_call | solution.py:224
  39.1 0.1 collective-permute-start.8
  39.2 1.7 %shard_map.54 = bf16[64,128]{1,0:T(8,128)(2,1)S(1)} custom-call(f32[4,128]{1,0:T(4,128)S(1)} %masks.1.mask_ref, f32[2,1024,1024]{2,1,0:T(8,128)S(1)} %widen.1.kernel_ref, bf16[2048,128]{1,0:T(8,128)(2,1)S(1)} %get-tuple-element.26.wide_ref, bf16[512,128]{1,0:T(8,128)(2,1)S(1)} %collective-permute-done.5.refs_0_.refs_1_, ...), custom_call_target="tpu_custom_call" | custom-call | flops 704643072 | tf_op jit(solution)/shard_map/pallas_call | solution.py:224
  40.8 0.0 collective-permute-done.2
  40.9 2.7 %collective-permute-start.3 = (bf16[2,64,128]{2,1,0:T(8,128)(2,1)S(1)}, bf16[2,64,128]{2,1,0:T(8,128)(2,1)S(1)}, u32[]{:S(2)}, u32[]{:S(2)}) collective-permute-start(bf16[2,64,128]{2,1,0:T(8,128)(2,1)S(1)} %pad_maximum_fusion), channel_id=1, source_target_pairs={{0,19},{1,18},{2,21},{3,20},{4,23},{5,22},{6,17},{7,16},{8,27},{9,... | collective-permute-start | bytes 98312 | tf_op jit(solution)/shard_map/ppermute | solution.py:55
  43.6 0.0 collective-permute-done.8
  43.6 2.3 %collective-permute-start.9 = (bf16[2,64,128]{2,1,0:T(8,128)(2,1)S(1)}, bf16[2,64,128]{2,1,0:T(8,128)(2,1)S(1)}, u32[]{:S(2)}, u32[]{:S(2)}) collective-permute-start(bf16[2,64,128]{2,1,0:T(8,128)(2,1)S(1)} %pad_maximum_fusion.1), channel_id=1, source_target_pairs={{0,30},{1,31},{2,24},{3,25},{4,26},{5,27},{6,28},{7,29},{8,6},{9,7... | collective-permute-start | bytes 98312 | tf_op jit(solution)/shard_map/ppermute | solution.py:55
  45.9 1.1 %collective-permute-done.3.refs_0_ = bf16[2,64,128]{2,1,0:T(8,128)(2,1)S(1)} collective-permute-done((bf16[2,64,128]{2,1,0:T(8,128)(2,1)S(1)}, bf16[2,64,128]{2,1,0:T(8,128)(2,1)S(1)}, u32[]{:S(2)}, u32[]{:S(2)}) %collective-permute-start.3) | collective-permute-done | bytes 32800 | tf_op jit(solution)/shard_map/ppermute | solution.py:55
  47.0 1.5 %collective-permute-done.9.refs_1_ = bf16[2,64,128]{2,1,0:T(8,128)(2,1)S(1)} collective-permute-done((bf16[2,64,128]{2,1,0:T(8,128)(2,1)S(1)}, bf16[2,64,128]{2,1,0:T(8,128)(2,1)S(1)}, u32[]{:S(2)}, u32[]{:S(2)}) %collective-permute-start.9) | collective-permute-done | bytes 32800 | tf_op jit(solution)/shard_map/ppermute | solution.py:55
  48.5 1.4 %totals.1 = f32[4,4,1,64,128]{4,3,2,1,0:T(8,128)} custom-call(s32[2,2,32]{2,1,0:T(2,128)S(1)} %copy-done.2, bf16[2,64,128]{2,1,0:T(8,128)(2,1)S(1)} %collective-permute-done.3.refs_0_, bf16[2,64,128]{2,1,0:T(8,128)(2,1)S(1)} %collective-permute-done.9.refs_1_), custom_call_target="tpu_custom_call" | custom-call | tf_op jit(solution)/shard_map/totals/pallas_call | solution.py:392
  (2 shorter events, 0.0 us)
Async XLA Ops:
  0.0 14.4 %copy-start.1 = (s32[16,16,2,64]{3,2,1,0:T(2,128)S(1)}, s32[16,16,2,64]{3,2,1,0:T(2,128)}, u32[]{:S(2)}) copy-start(s32[16,16,2,64]{3,2,1,0:T(2,128)} %occupation_ref.1) | copy-start | bytes 393220
  0.0 0.7 %copy-start.2 = (s32[2,2,32]{2,1,0:T(2,128)S(1)}, s32[2,2,32]{2,1,0:T(2,128)}, u32[]{:S(2)}) copy-start(s32[2,2,32]{2,1,0:T(2,128)} %plan_ref.7) | copy-start | bytes 1540
  0.7 14.4 %copy-start = (bf16[1,2,1024,1024]{3,2,1,0:T(8,128)(2,1)S(1)}, bf16[1,2,1024,1024]{3,2,1,0:T(8,128)(2,1)}, u32[]{:S(2)}) copy-start(bf16[1,2,1024,1024]{3,2,1,0:T(8,128)(2,1)} %kernel_ref) | copy-start | bytes 12582916
  2.7 13.9 %collective-permute-start = (bf16[1024,128]{1,0:T(8,128)(2,1)S(1)}, bf16[1024,128]{1,0:T(8,128)(2,1)S(1)}, u32[]{:S(2)}, u32[]{:S(2)}) collective-permute-start(bf16[1024,128]{1,0:T(8,128)(2,1)S(1)} %get-tuple-element.20), channel_id=1, source_target_pairs={{0,23},{1,22},{2,17},{3,16},{4,19},{5,18},{6,21},{7,20},{8,31},{9,... | collective-permute-start | bytes 786440 | tf_op jit(solution)/shard_map/ppermute | solution.py:55
  8.2 13.3 %collective-permute-start.1 = (bf16[1024,128]{1,0:T(8,128)(2,1)S(1)}, bf16[1024,128]{1,0:T(8,128)(2,1)S(1)}, u32[]{:S(2)}, u32[]{:S(2)}) collective-permute-start(bf16[1024,128]{1,0:T(8,128)(2,1)S(1)} %get-tuple-element.22), channel_id=1, source_target_pairs={{0,22},{1,23},{2,16},{3,17},{4,18},{5,19},{6,20},{7,21},{8,30},{9,... | collective-permute-start | bytes 786440 | tf_op jit(solution)/shard_map/ppermute | solution.py:55
  10.5 25.6 %collective-permute-start.6 = (bf16[256,128]{1,0:T(8,128)(2,1)S(1)}, bf16[256,128]{1,0:T(8,128)(2,1)S(1)}, u32[]{:S(2)}, u32[]{:S(2)}) collective-permute-start(bf16[256,128]{1,0:T(8,128)(2,1)S(1)} %get-tuple-element.28), channel_id=1, source_target_pairs={{0,11},{1,10},{2,13},{3,12},{4,15},{5,14},{6,9},{7,8},{8,19},{9,18... | collective-permute-start | bytes 196616 | tf_op jit(solution)/shard_map/ppermute | solution.py:55
  12.8 25.6 %collective-permute-start.7 = (bf16[256,128]{1,0:T(8,128)(2,1)S(1)}, bf16[256,128]{1,0:T(8,128)(2,1)S(1)}, u32[]{:S(2)}, u32[]{:S(2)}) collective-permute-start(bf16[256,128]{1,0:T(8,128)(2,1)S(1)} %get-tuple-element.29), channel_id=1, source_target_pairs={{0,11},{1,10},{2,13},{3,12},{4,15},{5,14},{6,9},{7,8},{8,19},{9,18... | collective-permute-start | bytes 196616 | tf_op jit(solution)/shard_map/ppermute | solution.py:55
  12.9 22.2 %collective-permute-start.5 = (bf16[512,128]{1,0:T(8,128)(2,1)S(1)}, bf16[512,128]{1,0:T(8,128)(2,1)S(1)}, u32[]{:S(2)}, u32[]{:S(2)}) collective-permute-start(bf16[512,128]{1,0:T(8,128)(2,1)S(1)} %get-tuple-element.27), channel_id=1, source_target_pairs={{0,11},{1,10},{2,13},{3,12},{4,15},{5,14},{6,9},{7,8},{8,19},{9,18... | collective-permute-start | bytes 393224 | tf_op jit(solution)/shard_map/ppermute | solution.py:55
  16.6 16.9 %collective-permute-start.4 = (bf16[1024,128]{1,0:T(8,128)(2,1)S(1)}, bf16[1024,128]{1,0:T(8,128)(2,1)S(1)}, u32[]{:S(2)}, u32[]{:S(2)}) collective-permute-start(bf16[1024,128]{1,0:T(8,128)(2,1)S(1)} %get-tuple-element.25), channel_id=1, source_target_pairs={{0,10},{1,11},{2,12},{3,13},{4,14},{5,15},{6,8},{7,9},{8,18},{9,19... | collective-permute-start | bytes 786440 | tf_op jit(solution)/shard_map/ppermute | solution.py:55
  25.8 15.0 %collective-permute-start.2 = (bf16[64,128]{1,0:T(8,128)(2,1)S(1)}, bf16[64,128]{1,0:T(8,128)(2,1)S(1)}, u32[]{:S(2)}, u32[]{:S(2)}) collective-permute-start(bf16[64,128]{1,0:T(8,128)(2,1)S(1)} %shard_map.49), channel_id=1, source_target_pairs={{0,1},{1,0},{2,3},{3,2},{4,5},{5,4},{6,7},{7,6},{8,9},{9,8},{10,11... | collective-permute-start | bytes 49160 | tf_op jit(solution)/shard_map/ppermute | solution.py:55
  39.1 4.5 %collective-permute-start.8 = (bf16[64,128]{1,0:T(8,128)(2,1)S(1)}, bf16[64,128]{1,0:T(8,128)(2,1)S(1)}, u32[]{:S(2)}, u32[]{:S(2)}) collective-permute-start(bf16[64,128]{1,0:T(8,128)(2,1)S(1)} %shard_map.57), channel_id=1, source_target_pairs={{0,1},{1,0},{2,3},{3,2},{4,5},{5,4},{6,7},{7,6},{8,9},{9,8},{10,11... | collective-permute-start | bytes 49160 | tf_op jit(solution)/shard_map/ppermute | solution.py:55
  40.9 6.1 %collective-permute-start.3 = (bf16[2,64,128]{2,1,0:T(8,128)(2,1)S(1)}, bf16[2,64,128]{2,1,0:T(8,128)(2,1)S(1)}, u32[]{:S(2)}, u32[]{:S(2)}) collective-permute-start(bf16[2,64,128]{2,1,0:T(8,128)(2,1)S(1)} %pad_maximum_fusion), channel_id=1, source_target_pairs={{0,19},{1,18},{2,21},{3,20},{4,23},{5,22},{6,17},{7,16},{8,27},{9,... | collective-permute-start | bytes 98312 | tf_op jit(solution)/shard_map/ppermute | solution.py:55
  43.6 4.9 %collective-permute-start.9 = (bf16[2,64,128]{2,1,0:T(8,128)(2,1)S(1)}, bf16[2,64,128]{2,1,0:T(8,128)(2,1)S(1)}, u32[]{:S(2)}, u32[]{:S(2)}) collective-permute-start(bf16[2,64,128]{2,1,0:T(8,128)(2,1)S(1)} %pad_maximum_fusion.1), channel_id=1, source_target_pairs={{0,30},{1,31},{2,24},{3,25},{4,26},{5,27},{6,28},{7,29},{8,6},{9,7... | collective-permute-start | bytes 98312 | tf_op jit(solution)/shard_map/ppermute | solution.py:55

commit v4 on v3

--- a/solution.py
+++ b/solution.py
@@ -79,6 +79,12 @@
     return jnp.where(value < 0, value + count, value)
 
 
+def slot_of(plan_ref, turn_number, column, device):
+    row = plan_ref[turn_number, column : column + 1, :]
+    lane = lax.broadcasted_iota(jnp.int32, row.shape, 1)
+    return jnp.sum(jnp.where(lane == device, row, 0))
+
+
 def whole(space):
     return pl.BlockSpec(memory_space=space)
 
@@ -86,10 +92,11 @@
 def pick_kernel(turn_number, mesh_counts, bounds, plan_ref, orbitals_ref, *refs):
     sems = refs[-1]
     own = linear_of(own_places(), mesh_counts)
+    slots = [slot_of(plan_ref, turn_number, column, own) for column in range(2)]
     copies = []
     for number, out_ref in enumerate(refs[:-1]):
         column = 1 if number == 0 else 0
-        cell = cell_of(plan_ref[turn_number, column, own], orbitals_ref.shape[:3])
+        cell = cell_of(slots[column], orbitals_ref.shape[:3])
         low = 0 if number == 0 else bounds[number - 1]
         copy = pltpu.make_async_copy(
             orbitals_ref.at[cell[0], cell[1], cell[2], pl.ds(low, out_ref.shape[0])],
@@ -108,7 +115,7 @@
     return pl.pallas_call(
         functools.partial(pick_kernel, turn_number, mesh_counts, bounds),
         out_shape=tuple(jax.ShapeDtypeStruct((rows, width), orbitals.dtype) for rows in lengths),
-        in_specs=[whole(pltpu.SMEM), whole(pl.ANY)],
+        in_specs=[whole(pltpu.VMEM), whole(pl.ANY)],
         out_specs=(whole(pltpu.VMEM),) * len(lengths),
         scratch_shapes=[pltpu.SemaphoreType.DMA((len(lengths),))],
         compiler_params=pltpu.CompilerParams(vmem_limit_bytes=PICK_GRANT),
@@ -383,7 +390,7 @@
     for number, pair_ref in enumerate(refs[:-1]):
         turn_number = plan_ref.shape[0] - 1 - number
         for column in range(2):
-            cell = cell_of(plan_ref[turn_number, 1 - column, own], out_ref.shape[:3])
+            cell = cell_of(slot_of(plan_ref, turn_number, 1 - column, own), out_ref.shape[:3])
             held = out_ref[cell[0], cell[1], cell[2]]
             out_ref[cell[0], cell[1], cell[2]] = held + pair_ref[column].astype(out_ref.dtype)
 
@@ -392,7 +399,7 @@
     return pl.pallas_call(
         functools.partial(total_kernel, mesh_counts),
         out_shape=jax.ShapeDtypeStruct((*cell_counts, *pairs[0].shape[1:]), jnp.float32),
-        in_specs=[whole(pltpu.SMEM)] + [whole(pltpu.VMEM)] * len(pairs),
+        in_specs=[whole(pltpu.VMEM)] * (1 + len(pairs)),
         out_specs=whole(pltpu.VMEM),
         compiler_params=pltpu.CompilerParams(vmem_limit_bytes=SMALL_GRANT),
         name="totals",

time: 50 us -> 49 us (0.980)
  Pallas kernels: 20.2 us -> 18.7 us
  waiting for transfers between devices: 10.1 us -> 10.6 us
    pallas_call x2, Pallas kernels: 3.56 us -> 2.51 us  [picked(): pl.pallas_call(functools.partial(pick_kernel, turn_number, mesh_counts, b...]
where the time goes in v4:
time: 49 us; the launch traced here: 48.8 us
  Pallas kernels  18.7 us (38%)
  starting transfers between devices  18.6 us (38%)
  waiting for transfers between devices  10.6 us (22%)
  local copies, waits for them, and re-layouts  0.73 us (1%)
    ppermute x10, starting transfers between devices, moved(): return lax.ppermute(block, AXES, route)  18.6 us
    pallas_call x10, Pallas kernels, pair_call(): pl.pallas_call(body, out_shape=out_shape, in_specs=[whole(pltpu.VMEM)] *...  13 us
    ppermute x10, waiting for transfers between devices, moved(): return lax.ppermute(block, AXES, route)  10.6 us
    pallas_call x2, Pallas kernels, picked(): pl.pallas_call(functools.partial(pick_kernel, turn_number, mesh_counts, b...  2.51 us
    pallas_call x1, Pallas kernels, widened(): pl.pallas_call(widen_kernel, grid=(rows // size,), out_shape=jax.ShapeDty...  1.45 us
  transfers between devices with their start and end apart: 10, of which 3 were waited for; matrix products, arithmetic and copies ran while one was open for 0% of the time, Pallas kernels for 34%

profile of v4, /device:TPU:0, one launch (start us, length us, event | category | flops | bytes accessed | tf_op | source)
XLA Modules:
  0.0 48.8 jit_solution(9502996641278630370)
XLA Ops:
  0.0 0.0 copy-start.1
  0.0 0.0 copy-start.2
  0.0 0.7 %copy-done.2 = s32[2,2,32]{2,1,0:T(2,128)S(1)} copy-done((s32[2,2,32]{2,1,0:T(2,128)S(1)}, s32[2,2,32]{2,1,0:T(2,128)}, u32[]{:S(2)}) %copy-start.2) | copy-done | bytes 536
  0.7 0.0 copy-start
  0.7 1.3 %shard_map.46 = (bf16[1024,128]{1,0:T(8,128)(2,1)S(1)}, bf16[1024,128]{1,0:T(8,128)(2,1)S(1)}) custom-call(s32[2,2,32]{2,1,0:T(2,128)S(1)} %copy-done.2, bf16[4,4,1,1024,128]{4,3,2,1,0:T(8,128)(2,1)} %orbitals_ref.3), custom_call_target="tpu_custom_call" | custom-call | tf_op jit(solution)/shard_map/pallas_call | solution.py:115
  2.1 5.5 %collective-permute-start = (bf16[1024,128]{1,0:T(8,128)(2,1)S(1)}, bf16[1024,128]{1,0:T(8,128)(2,1)S(1)}, u32[]{:S(2)}, u32[]{:S(2)}) collective-permute-start(bf16[1024,128]{1,0:T(8,128)(2,1)S(1)} %get-tuple-element.20), channel_id=1, source_target_pairs={{0,23},{1,22},{2,17},{3,16},{4,19},{5,18},{6,21},{7,20},{8,31},{9,... | collective-permute-start | bytes 786440 | tf_op jit(solution)/shard_map/ppermute | solution.py:55
  7.6 0.6 %collective-permute-start.1 = (bf16[1024,128]{1,0:T(8,128)(2,1)S(1)}, bf16[1024,128]{1,0:T(8,128)(2,1)S(1)}, u32[]{:S(2)}, u32[]{:S(2)}) collective-permute-start(bf16[1024,128]{1,0:T(8,128)(2,1)S(1)} %get-tuple-element.22), channel_id=1, source_target_pairs={{0,22},{1,23},{2,16},{3,17},{4,18},{5,19},{6,20},{7,21},{8,30},{9,... | collective-permute-start | bytes 786440 | tf_op jit(solution)/shard_map/ppermute | solution.py:55
  8.2 1.2 %shard_map.50 = (bf16[1024,128]{1,0:T(8,128)(2,1)S(1)}, bf16[512,128]{1,0:T(8,128)(2,1)S(1)}, bf16[256,128]{1,0:T(8,128)(2,1)S(1)}, bf16[256,128]{1,0:T(8,128)(2,1)S(1)}) custom-call(s32[2,2,32]{2,1,0:T(2,128)S(1)} %copy-done.2, bf16[4,4,1,1024,128]{4,3,2,1,0:T(8,128)(2,1)} %orbitals_ref.3), custom_call_target="tpu_custom_call" | custom-call | tf_op jit(solution)/shard_map/pallas_call | solution.py:115
  9.4 2.3 %collective-permute-start.6 = (bf16[256,128]{1,0:T(8,128)(2,1)S(1)}, bf16[256,128]{1,0:T(8,128)(2,1)S(1)}, u32[]{:S(2)}, u32[]{:S(2)}) collective-permute-start(bf16[256,128]{1,0:T(8,128)(2,1)S(1)} %get-tuple-element.28), channel_id=1, source_target_pairs={{0,11},{1,10},{2,13},{3,12},{4,15},{5,14},{6,9},{7,8},{8,19},{9,18... | collective-permute-start | bytes 196616 | tf_op jit(solution)/shard_map/ppermute | solution.py:55
  11.7 0.1 collective-permute-start.7
  11.8 1.5 %collective-permute-start.5 = (bf16[512,128]{1,0:T(8,128)(2,1)S(1)}, bf16[512,128]{1,0:T(8,128)(2,1)S(1)}, u32[]{:S(2)}, u32[]{:S(2)}) collective-permute-start(bf16[512,128]{1,0:T(8,128)(2,1)S(1)} %get-tuple-element.27), channel_id=1, source_target_pairs={{0,11},{1,10},{2,13},{3,12},{4,15},{5,14},{6,9},{7,8},{8,19},{9,18... | collective-permute-start | bytes 393224 | tf_op jit(solution)/shard_map/ppermute | solution.py:55
  13.3 0.0 copy-done.1
  13.3 0.8 %masks.1.mask_ref = f32[4,128]{1,0:T(4,128)S(1)} custom-call(s32[2,2,32]{2,1,0:T(2,128)S(1)} %copy-done.2, s32[16,16,2,64]{3,2,1,0:T(2,128)S(1)} %copy-done.1), custom_call_target="tpu_custom_call" | custom-call | tf_op jit(solution)/shard_map/masks/pallas_call | solution.py:156
  14.1 0.0 copy-done
  14.1 1.5 %widen.1.kernel_ref = f32[2,1024,1024]{2,1,0:T(8,128)S(1)} custom-call(bf16[1,2,1024,1024]{3,2,1,0:T(8,128)(2,1)S(1)} %copy-done), custom_call_target="tpu_custom_call" | custom-call | tf_op jit(solution)/shard_map/widen/pallas_call | solution.py:219
  15.5 0.0 collective-permute-done.second_ref
  15.6 3.3 %collective-permute-start.4 = (bf16[1024,128]{1,0:T(8,128)(2,1)S(1)}, bf16[1024,128]{1,0:T(8,128)(2,1)S(1)}, u32[]{:S(2)}, u32[]{:S(2)}) collective-permute-start(bf16[1024,128]{1,0:T(8,128)(2,1)S(1)} %get-tuple-element.25), channel_id=1, source_target_pairs={{0,10},{1,11},{2,12},{3,13},{4,14},{5,15},{6,8},{7,9},{8,18},{9,19... | collective-permute-start | bytes 786440 | tf_op jit(solution)/shard_map/ppermute | solution.py:55
  18.9 1.5 %shard_map.47 = (bf16[1024,2048]{1,0:T(8,128)(2,1)S(1)}, bf16[2048,128]{1,0:T(8,128)(2,1)S(1)}) custom-call(f32[4,128]{1,0:T(4,128)S(1)} %masks.1.mask_ref, f32[2,1024,1024]{2,1,0:T(8,128)S(1)} %widen.1.kernel_ref, bf16[1024,128]{1,0:T(8,128)(2,1)S(1)} %collective-permute-done.second_ref), custom_call_target="tpu_custom_call" | custom-call | flops 536870912 | tf_op jit(solution)/shard_map/pallas_call | solution.py:231
  20.4 0.0 collective-permute-done.1.refs_0_.refs_1_
  20.4 2.8 %shard_map.48 = bf16[64,128]{1,0:T(8,128)(2,1)S(1)} custom-call(f32[4,128]{1,0:T(4,128)S(1)} %masks.1.mask_ref, f32[2,1024,1024]{2,1,0:T(8,128)S(1)} %widen.1.kernel_ref, bf16[2048,128]{1,0:T(8,128)(2,1)S(1)} %get-tuple-element.21.wide_ref, bf16[1024,128]{1,0:T(8,128)(2,1)S(1)} %collective-permute-done.1.refs_0_.refs_1_), custom_call_target="tpu_custom_call" | custom-call | flops 1610612736 | tf_op jit(solution)/shard_map/pallas_call | solution.py:231
  23.3 1.5 %shard_map.49 = bf16[64,128]{1,0:T(8,128)(2,1)S(1)} custom-call(bf16[1024,2048]{1,0:T(8,128)(2,1)S(1)} %get-tuple-element.23.refs_0_, bf16[1024,128]{1,0:T(8,128)(2,1)S(1)} %collective-permute-done.1.refs_0_.refs_1_), custom_call_target="tpu_custom_call" | custom-call | flops 1073741824 | tf_op jit(solution)/shard_map/pallas_call | solution.py:231
  24.8 0.1 collective-permute-start.2
  24.9 8.0 %collective-permute-done.4.second_ref = bf16[1024,128]{1,0:T(8,128)(2,1)S(1)} collective-permute-done((bf16[1024,128]{1,0:T(8,128)(2,1)S(1)}, bf16[1024,128]{1,0:T(8,128)(2,1)S(1)}, u32[]{:S(2)}, u32[]{:S(2)}) %collective-permute-start.4) | collective-permute-done | bytes 262176 | tf_op jit(solution)/shard_map/ppermute | solution.py:55
  32.9 1.6 %shard_map.51 = (bf16[1024,2048]{1,0:T(8,128)(2,1)S(1)}, bf16[2048,128]{1,0:T(8,128)(2,1)S(1)}) custom-call(f32[4,128]{1,0:T(4,128)S(1)} %masks.1.mask_ref, f32[2,1024,1024]{2,1,0:T(8,128)S(1)} %widen.1.kernel_ref, bf16[1024,128]{1,0:T(8,128)(2,1)S(1)} %collective-permute-done.4.second_ref), custom_call_target="tpu_custom_call" | custom-call | flops 536870912 | tf_op jit(solution)/shard_map/pallas_call | solution.py:231
  34.5 0.0 collective-permute-done.5.refs_0_.refs_1_
  34.5 0.9 %shard_map.52.refs_2_ = f32[512,128]{1,0:T(8,128)S(1)} custom-call(f32[4,128]{1,0:T(4,128)S(1)} %masks.1.mask_ref, f32[2,1024,1024]{2,1,0:T(8,128)S(1)} %widen.1.kernel_ref, bf16[2048,128]{1,0:T(8,128)(2,1)S(1)} %get-tuple-element.26.wide_ref, bf16[512,128]{1,0:T(8,128)(2,1)S(1)} %collective-permute-done.5.refs_0_.refs_1_), custom_call_target="tpu_custom_call" | custom-call | flops 402653184 | tf_op jit(solution)/shard_map/pallas_call | solution.py:231
  35.4 0.0 collective-permute-done.6.refs_1_.refs_2_
  35.4 1.1 %shard_map.53.refs_3_ = f32[768,128]{1,0:T(8,128)S(1)} custom-call(f32[4,128]{1,0:T(4,128)S(1)} %masks.1.mask_ref, f32[2,1024,1024]{2,1,0:T(8,128)S(1)} %widen.1.kernel_ref, bf16[2048,128]{1,0:T(8,128)(2,1)S(1)} %get-tuple-element.26.wide_ref, bf16[512,128]{1,0:T(8,128)(2,1)S(1)} %collective-permute-done.5.refs_0_.refs_1_, ...), custom_call_target="tpu_custom_call" | custom-call | flops 503316480 | tf_op jit(solution)/shard_map/pallas_call | solution.py:231
  36.5 0.7 %shard_map.55.refs_2_ = f32[1024,128]{1,0:T(8,128)S(1)} custom-call(bf16[1024,2048]{1,0:T(8,128)(2,1)S(1)} %get-tuple-element.32.refs_0_, bf16[512,128]{1,0:T(8,128)(2,1)S(1)} %collective-permute-done.5.refs_0_.refs_1_), custom_call_target="tpu_custom_call" | custom-call | flops 536870912 | tf_op jit(solution)/shard_map/pallas_call | solution.py:231
  37.2 0.5 %shard_map.56.refs_4_ = f32[1024,128]{1,0:T(8,128)S(1)} custom-call(bf16[1024,2048]{1,0:T(8,128)(2,1)S(1)} %get-tuple-element.32.refs_0_, bf16[256,128]{1,0:T(8,128)(2,1)S(1)} %collective-permute-done.6.refs_1_.refs_2_, f32[1024,128]{1,0:T(8,128)S(1)} %shard_map.55.refs_2_), custom_call_target="tpu_custom_call", output_to_operand_aliasing={{}: (2, {})} | custom-call | flops 268435456 | tf_op jit(solution)/shard_map/pallas_call | solution.py:231
  37.7 0.0 collective-permute-done.7.refs_2_.refs_3_
  37.7 0.7 %shard_map.57 = bf16[64,128]{1,0:T(8,128)(2,1)S(1)} custom-call(bf16[1024,2048]{1,0:T(8,128)(2,1)S(1)} %get-tuple-element.32.refs_0_, bf16[512,128]{1,0:T(8,128)(2,1)S(1)} %collective-permute-done.5.refs_0_.refs_1_, bf16[256,128]{1,0:T(8,128)(2,1)S(1)} %collective-permute-done.6.refs_1_.refs_2_, bf16[256,128]{1,0:T(8,128)(2,1)S(1)} %collective-permute-done.7.refs_2_.refs_3_, ...), custom_call_target="tpu_custom_call" | custom-call | flops 268435456 | tf_op jit(solution)/shard_map/pallas_call | solution.py:231
  38.5 0.1 collective-permute-start.8
  38.6 1.7 %shard_map.54 = bf16[64,128]{1,0:T(8,128)(2,1)S(1)} custom-call(f32[4,128]{1,0:T(4,128)S(1)} %masks.1.mask_ref, f32[2,1024,1024]{2,1,0:T(8,128)S(1)} %widen.1.kernel_ref, bf16[2048,128]{1,0:T(8,128)(2,1)S(1)} %get-tuple-element.26.wide_ref, bf16[512,128]{1,0:T(8,128)(2,1)S(1)} %collective-permute-done.5.refs_0_.refs_1_, ...), custom_call_target="tpu_custom_call" | custom-call | flops 704643072 | tf_op jit(solution)/shard_map/pallas_call | solution.py:231
  40.2 0.0 collective-permute-done.2
  40.3 2.7 %collective-permute-start.3 = (bf16[2,64,128]{2,1,0:T(8,128)(2,1)S(1)}, bf16[2,64,128]{2,1,0:T(8,128)(2,1)S(1)}, u32[]{:S(2)}, u32[]{:S(2)}) collective-permute-start(bf16[2,64,128]{2,1,0:T(8,128)(2,1)S(1)} %pad_maximum_fusion), channel_id=1, source_target_pairs={{0,19},{1,18},{2,21},{3,20},{4,23},{5,22},{6,17},{7,16},{8,27},{9,... | collective-permute-start | bytes 98312 | tf_op jit(solution)/shard_map/ppermute | solution.py:55
  43.0 0.0 collective-permute-done.8
  43.0 2.3 %collective-permute-start.9 = (bf16[2,64,128]{2,1,0:T(8,128)(2,1)S(1)}, bf16[2,64,128]{2,1,0:T(8,128)(2,1)S(1)}, u32[]{:S(2)}, u32[]{:S(2)}) collective-permute-start(bf16[2,64,128]{2,1,0:T(8,128)(2,1)S(1)} %pad_maximum_fusion.1), channel_id=1, source_target_pairs={{0,30},{1,31},{2,24},{3,25},{4,26},{5,27},{6,28},{7,29},{8,6},{9,7... | collective-permute-start | bytes 98312 | tf_op jit(solution)/shard_map/ppermute | solution.py:55
  45.3 1.1 %collective-permute-done.3.refs_0_ = bf16[2,64,128]{2,1,0:T(8,128)(2,1)S(1)} collective-permute-done((bf16[2,64,128]{2,1,0:T(8,128)(2,1)S(1)}, bf16[2,64,128]{2,1,0:T(8,128)(2,1)S(1)}, u32[]{:S(2)}, u32[]{:S(2)}) %collective-permute-start.3) | collective-permute-done | bytes 32800 | tf_op jit(solution)/shard_map/ppermute | solution.py:55
  46.4 1.5 %collective-permute-done.9.refs_1_ = bf16[2,64,128]{2,1,0:T(8,128)(2,1)S(1)} collective-permute-done((bf16[2,64,128]{2,1,0:T(8,128)(2,1)S(1)}, bf16[2,64,128]{2,1,0:T(8,128)(2,1)S(1)}, u32[]{:S(2)}, u32[]{:S(2)}) %collective-permute-start.9) | collective-permute-done | bytes 32800 | tf_op jit(solution)/shard_map/ppermute | solution.py:55
  47.9 1.0 %totals.1 = f32[4,4,1,64,128]{4,3,2,1,0:T(8,128)} custom-call(s32[2,2,32]{2,1,0:T(2,128)S(1)} %copy-done.2, bf16[2,64,128]{2,1,0:T(8,128)(2,1)S(1)} %collective-permute-done.3.refs_0_, bf16[2,64,128]{2,1,0:T(8,128)(2,1)S(1)} %collective-permute-done.9.refs_1_), custom_call_target="tpu_custom_call" | custom-call | tf_op jit(solution)/shard_map/totals/pallas_call | solution.py:399
  (2 shorter events, 0.0 us)
Async XLA Ops:
  0.0 13.3 %copy-start.1 = (s32[16,16,2,64]{3,2,1,0:T(2,128)S(1)}, s32[16,16,2,64]{3,2,1,0:T(2,128)}, u32[]{:S(2)}) copy-start(s32[16,16,2,64]{3,2,1,0:T(2,128)} %occupation_ref.1) | copy-start | bytes 393220
  0.0 0.7 %copy-start.2 = (s32[2,2,32]{2,1,0:T(2,128)S(1)}, s32[2,2,32]{2,1,0:T(2,128)}, u32[]{:S(2)}) copy-start(s32[2,2,32]{2,1,0:T(2,128)} %plan_ref.7) | copy-start | bytes 1540
  0.7 13.3 %copy-start = (bf16[1,2,1024,1024]{3,2,1,0:T(8,128)(2,1)S(1)}, bf16[1,2,1024,1024]{3,2,1,0:T(8,128)(2,1)}, u32[]{:S(2)}) copy-start(bf16[1,2,1024,1024]{3,2,1,0:T(8,128)(2,1)} %kernel_ref) | copy-start | bytes 12582916
  2.1 13.5 %collective-permute-start = (bf16[1024,128]{1,0:T(8,128)(2,1)S(1)}, bf16[1024,128]{1,0:T(8,128)(2,1)S(1)}, u32[]{:S(2)}, u32[]{:S(2)}) collective-permute-start(bf16[1024,128]{1,0:T(8,128)(2,1)S(1)} %get-tuple-element.20), channel_id=1, source_target_pairs={{0,23},{1,22},{2,17},{3,16},{4,19},{5,18},{6,21},{7,20},{8,31},{9,... | collective-permute-start | bytes 786440 | tf_op jit(solution)/shard_map/ppermute | solution.py:55
  7.6 12.8 %collective-permute-start.1 = (bf16[1024,128]{1,0:T(8,128)(2,1)S(1)}, bf16[1024,128]{1,0:T(8,128)(2,1)S(1)}, u32[]{:S(2)}, u32[]{:S(2)}) collective-permute-start(bf16[1024,128]{1,0:T(8,128)(2,1)S(1)} %get-tuple-element.22), channel_id=1, source_target_pairs={{0,22},{1,23},{2,16},{3,17},{4,18},{5,19},{6,20},{7,21},{8,30},{9,... | collective-permute-start | bytes 786440 | tf_op jit(solution)/shard_map/ppermute | solution.py:55
  9.4 26.0 %collective-permute-start.6 = (bf16[256,128]{1,0:T(8,128)(2,1)S(1)}, bf16[256,128]{1,0:T(8,128)(2,1)S(1)}, u32[]{:S(2)}, u32[]{:S(2)}) collective-permute-start(bf16[256,128]{1,0:T(8,128)(2,1)S(1)} %get-tuple-element.28), channel_id=1, source_target_pairs={{0,11},{1,10},{2,13},{3,12},{4,15},{5,14},{6,9},{7,8},{8,19},{9,18... | collective-permute-start | bytes 196616 | tf_op jit(solution)/shard_map/ppermute | solution.py:55
  11.7 26.0 %collective-permute-start.7 = (bf16[256,128]{1,0:T(8,128)(2,1)S(1)}, bf16[256,128]{1,0:T(8,128)(2,1)S(1)}, u32[]{:S(2)}, u32[]{:S(2)}) collective-permute-start(bf16[256,128]{1,0:T(8,128)(2,1)S(1)} %get-tuple-element.29), channel_id=1, source_target_pairs={{0,11},{1,10},{2,13},{3,12},{4,15},{5,14},{6,9},{7,8},{8,19},{9,18... | collective-permute-start | bytes 196616 | tf_op jit(solution)/shard_map/ppermute | solution.py:55
  11.8 22.7 %collective-permute-start.5 = (bf16[512,128]{1,0:T(8,128)(2,1)S(1)}, bf16[512,128]{1,0:T(8,128)(2,1)S(1)}, u32[]{:S(2)}, u32[]{:S(2)}) collective-permute-start(bf16[512,128]{1,0:T(8,128)(2,1)S(1)} %get-tuple-element.27), channel_id=1, source_target_pairs={{0,11},{1,10},{2,13},{3,12},{4,15},{5,14},{6,9},{7,8},{8,19},{9,18... | collective-permute-start | bytes 393224 | tf_op jit(solution)/shard_map/ppermute | solution.py:55
  15.6 17.3 %collective-permute-start.4 = (bf16[1024,128]{1,0:T(8,128)(2,1)S(1)}, bf16[1024,128]{1,0:T(8,128)(2,1)S(1)}, u32[]{:S(2)}, u32[]{:S(2)}) collective-permute-start(bf16[1024,128]{1,0:T(8,128)(2,1)S(1)} %get-tuple-element.25), channel_id=1, source_target_pairs={{0,10},{1,11},{2,12},{3,13},{4,14},{5,15},{6,8},{7,9},{8,18},{9,19... | collective-permute-start | bytes 786440 | tf_op jit(solution)/shard_map/ppermute | solution.py:55
  24.8 15.5 %collective-permute-start.2 = (bf16[64,128]{1,0:T(8,128)(2,1)S(1)}, bf16[64,128]{1,0:T(8,128)(2,1)S(1)}, u32[]{:S(2)}, u32[]{:S(2)}) collective-permute-start(bf16[64,128]{1,0:T(8,128)(2,1)S(1)} %shard_map.49), channel_id=1, source_target_pairs={{0,1},{1,0},{2,3},{3,2},{4,5},{5,4},{6,7},{7,6},{8,9},{9,8},{10,11... | collective-permute-start | bytes 49160 | tf_op jit(solution)/shard_map/ppermute | solution.py:55
  38.5 4.5 %collective-permute-start.8 = (bf16[64,128]{1,0:T(8,128)(2,1)S(1)}, bf16[64,128]{1,0:T(8,128)(2,1)S(1)}, u32[]{:S(2)}, u32[]{:S(2)}) collective-permute-start(bf16[64,128]{1,0:T(8,128)(2,1)S(1)} %shard_map.57), channel_id=1, source_target_pairs={{0,1},{1,0},{2,3},{3,2},{4,5},{5,4},{6,7},{7,6},{8,9},{9,8},{10,11... | collective-permute-start | bytes 49160 | tf_op jit(solution)/shard_map/ppermute | solution.py:55
  40.3 6.1 %collective-permute-start.3 = (bf16[2,64,128]{2,1,0:T(8,128)(2,1)S(1)}, bf16[2,64,128]{2,1,0:T(8,128)(2,1)S(1)}, u32[]{:S(2)}, u32[]{:S(2)}) collective-permute-start(bf16[2,64,128]{2,1,0:T(8,128)(2,1)S(1)} %pad_maximum_fusion), channel_id=1, source_target_pairs={{0,19},{1,18},{2,21},{3,20},{4,23},{5,22},{6,17},{7,16},{8,27},{9,... | collective-permute-start | bytes 98312 | tf_op jit(solution)/shard_map/ppermute | solution.py:55
  43.0 4.9 %collective-permute-start.9 = (bf16[2,64,128]{2,1,0:T(8,128)(2,1)S(1)}, bf16[2,64,128]{2,1,0:T(8,128)(2,1)S(1)}, u32[]{:S(2)}, u32[]{:S(2)}) collective-permute-start(bf16[2,64,128]{2,1,0:T(8,128)(2,1)S(1)} %pad_maximum_fusion.1), channel_id=1, source_target_pairs={{0,30},{1,31},{2,24},{3,25},{4,26},{5,27},{6,28},{7,29},{8,6},{9,7... | collective-permute-start | bytes 98312 | tf_op jit(solution)/shard_map/ppermute | solution.py:55

commit v5 on v4

--- a/solution.py
+++ b/solution.py
@@ -89,18 +89,18 @@
     return pl.BlockSpec(memory_space=space)
 
 
-def pick_kernel(turn_number, mesh_counts, bounds, plan_ref, orbitals_ref, *refs):
+def pick_kernel(jobs, mesh_counts, plan_ref, orbitals_ref, *refs):
     sems = refs[-1]
     own = linear_of(own_places(), mesh_counts)
-    slots = [slot_of(plan_ref, turn_number, column, own) for column in range(2)]
+    slots = {}
     copies = []
-    for number, out_ref in enumerate(refs[:-1]):
-        column = 1 if number == 0 else 0
-        cell = cell_of(slots[column], orbitals_ref.shape[:3])
-        low = 0 if number == 0 else bounds[number - 1]
+    for number, (turn_number, column, low) in enumerate(jobs):
+        if (turn_number, column) not in slots:
+            slots[turn_number, column] = slot_of(plan_ref, turn_number, column, own)
+        cell = cell_of(slots[turn_number, column], orbitals_ref.shape[:3])
         copy = pltpu.make_async_copy(
-            orbitals_ref.at[cell[0], cell[1], cell[2], pl.ds(low, out_ref.shape[0])],
-            out_ref,
+            orbitals_ref.at[cell[0], cell[1], cell[2], pl.ds(low, refs[number].shape[0])],
+            refs[number],
             sems.at[number],
         )
         copy.start()
@@ -109,17 +109,27 @@
         copy.wait()
 
 
-def picked(turn_number, mesh_counts, bounds, plan, orbitals):
+def picked(bounds_of, mesh_counts, plan, orbitals):
     points, width = orbitals.shape[3:]
-    lengths = [points] + [high - low for low, high in zip(bounds, bounds[1:])]
-    return pl.pallas_call(
-        functools.partial(pick_kernel, turn_number, mesh_counts, bounds),
+    jobs, lengths = [], []
+    for turn_number, bounds in bounds_of.items():
+        jobs.append((turn_number, 1, 0))
+        lengths.append(points)
+        jobs += [(turn_number, 0, low) for low in bounds[:-1]]
+        lengths += [high - low for low, high in zip(bounds, bounds[1:])]
+    blocks = pl.pallas_call(
+        functools.partial(pick_kernel, tuple(jobs), mesh_counts),
         out_shape=tuple(jax.ShapeDtypeStruct((rows, width), orbitals.dtype) for rows in lengths),
         in_specs=[whole(pltpu.VMEM), whole(pl.ANY)],
         out_specs=(whole(pltpu.VMEM),) * len(lengths),
         scratch_shapes=[pltpu.SemaphoreType.DMA((len(lengths),))],
         compiler_params=pltpu.CompilerParams(vmem_limit_bytes=PICK_GRANT),
+        name="pick",
     )(plan, orbitals)
+    sends = {turn_number: [] for turn_number in bounds_of}
+    for job, block in zip(jobs, blocks):
+        sends[job[0]].append(block)
+    return sends
 
 
 def mask_kernel(mesh_counts, cell_counts, plan_ref, occupation_ref, out_ref, rows, sem):
@@ -383,27 +393,68 @@
     )
 
 
-def total_kernel(mesh_counts, plan_ref, *refs):
-    out_ref = refs[-1]
+def base_kernel(mesh_counts, plan_ref, *refs):
+    pairs, (out_ref, held_ref) = refs[:-2], refs[-2:]
     own = linear_of(own_places(), mesh_counts)
     out_ref[...] = jnp.zeros_like(out_ref)
-    for number, pair_ref in enumerate(refs[:-1]):
-        turn_number = plan_ref.shape[0] - 1 - number
+    for number, pair_ref in enumerate(pairs):
+        turn_number = number + 1
         for column in range(2):
             cell = cell_of(slot_of(plan_ref, turn_number, 1 - column, own), out_ref.shape[:3])
             held = out_ref[cell[0], cell[1], cell[2]]
             out_ref[cell[0], cell[1], cell[2]] = held + pair_ref[column].astype(out_ref.dtype)
-
-
-def totalled(mesh_counts, cell_counts, plan, pairs):
+    for column in range(2):
+        cell = cell_of(slot_of(plan_ref, 0, 1 - column, own), out_ref.shape[:3])
+        held_ref[column] = out_ref[cell[0], cell[1], cell[2]]
+
+
+def based(mesh_counts, cell_counts, plan, pairs):
+    block = pairs[0].shape[1:]
+    return pl.pallas_call(
+        functools.partial(base_kernel, mesh_counts),
+        out_shape=(
+            jax.ShapeDtypeStruct((*cell_counts, *block), jnp.float32),
+            jax.ShapeDtypeStruct((2, *block), jnp.float32),
+        ),
+        in_specs=[whole(pltpu.VMEM)] * (1 + len(pairs)),
+        out_specs=(whole(pltpu.VMEM), whole(pltpu.VMEM)),
+        compiler_params=pltpu.CompilerParams(vmem_limit_bytes=SMALL_GRANT),
+        name="base",
+    )(plan, *pairs)
+
+
+def total_kernel(mesh_counts, plan_ref, held_ref, pair_ref, base_ref, out_ref, sums, sems):
+    own = linear_of(own_places(), mesh_counts)
+    slots = [slot_of(plan_ref, 0, 1 - column, own) for column in range(2)]
+    apart = slots[0] != slots[1]
+    share = jnp.where(apart, 0.0, 1.0)
+    blocks = [pair_ref[column].astype(out_ref.dtype) for column in range(2)]
+    copies = []
+    for column in range(2):
+        sums[column] = held_ref[column] + (blocks[column] + share * blocks[1 - column])
+        cell = cell_of(slots[column], out_ref.shape[:3])
+        copies.append(
+            pltpu.make_async_copy(
+                sums.at[column], out_ref.at[cell[0], cell[1], cell[2]], sems.at[column]
+            )
+        )
+    copies[0].start()
+    pl.when(apart)(copies[1].start)
+    copies[0].wait()
+    pl.when(apart)(copies[1].wait)
+
+
+def totalled(mesh_counts, plan, held, pair, base):
     return pl.pallas_call(
         functools.partial(total_kernel, mesh_counts),
-        out_shape=jax.ShapeDtypeStruct((*cell_counts, *pairs[0].shape[1:]), jnp.float32),
-        in_specs=[whole(pltpu.VMEM)] * (1 + len(pairs)),
-        out_specs=whole(pltpu.VMEM),
+        out_shape=jax.ShapeDtypeStruct(base.shape, base.dtype),
+        in_specs=[whole(pltpu.VMEM)] * 3 + [whole(pl.ANY)],
+        out_specs=whole(pl.ANY),
+        scratch_shapes=[pltpu.VMEM(held.shape, held.dtype), pltpu.SemaphoreType.DMA((2,))],
+        input_output_aliases={3: 0},
         compiler_params=pltpu.CompilerParams(vmem_limit_bytes=SMALL_GRANT),
         name="totals",
-    )(plan, *pairs)
+    )(plan, held, pair, base)
 
 
 def on_device(orbitals, kernel, plan, occupation):
@@ -415,10 +466,7 @@
     order = tuple(reversed(range(turns)))
     bounds_of = {turn_number: (0, points) for turn_number in order}
     bounds_of[order[-1]] = (0, points // 2, points * 3 // 4, points)
-    sends = {
-        turn_number: picked(turn_number, mesh_counts, bounds_of[turn_number], plan, orbitals)
-        for turn_number in order
-    }
+    sends = picked(bounds_of, mesh_counts, plan, orbitals)
     masks = masks_of(mesh_counts, cell_counts, plan, occupation)
     kernel = widened(after(kernel, masks))
     returned = {}
@@ -448,8 +496,10 @@
         returned[turn_number] = moved(
             jnp.stack([second_block, crossed]), negated(partner), mesh_counts
         )
-    blocks = [returned[turn_number] for turn_number in reversed(range(turns))]
-    return totalled(mesh_counts, cell_counts, plan, blocks)
+    base, held = based(
+        mesh_counts, cell_counts, plan, [returned[turn_number] for turn_number in range(1, turns)]
+    )
+    return totalled(mesh_counts, plan, held, returned[0], base)
 
 
 def solution(mesh):

time: 49 us -> 49 us (level)
  waiting for transfers between devices: 10.6 us -> 11.4 us
  starting transfers between devices: 18.6 us -> 17.9 us
    ppermute x10, waiting for transfers between devices: 10.6 us -> 11.4 us  [moved(): return lax.ppermute(block, AXES, route)]
    ppermute x10, starting transfers between devices: 18.6 us -> 17.9 us  [moved(): return lax.ppermute(block, AXES, route)]
  transfers between devices with their start and end apart: 10 -> 10, of which waited for: 3 -> 5; matrix products, arithmetic and copies ran while one was open for 0% -> 0% of each run, Pallas kernels for 34% -> 33%
where the time goes in v5:
time: 49 us; the launch traced here: 48.8 us
  Pallas kernels  18.5 us (38%)
  starting transfers between devices  17.9 us (37%)
  waiting for transfers between devices  11.4 us (23%)
  local copies, waits for them, and re-layouts  0.73 us (1%)
    ppermute x10, starting transfers between devices, moved(): return lax.ppermute(block, AXES, route)  17.9 us
    pallas_call x10, Pallas kernels, pair_call(): pl.pallas_call(body, out_shape=out_shape, in_specs=[whole(pltpu.VMEM)] *...  13.1 us
    ppermute x10, waiting for transfers between devices, moved(): return lax.ppermute(block, AXES, route)  11.4 us
    pallas_call x1, Pallas kernels, picked(): pl.pallas_call(functools.partial(pick_kernel, tuple(jobs), mesh_counts),...  1.48 us
    pallas_call x1, Pallas kernels, widened(): pl.pallas_call(widen_kernel, grid=(rows // size,), out_shape=jax.ShapeDty...  1.45 us
  transfers between devices with their start and end apart: 10, of which 5 were waited for; matrix products, arithmetic and copies ran while one was open for 0% of the time, Pallas kernels for 33%

profile of v5, /device:TPU:0, one launch (start us, length us, event | category | flops | bytes accessed | tf_op | source)
XLA Modules:
  0.0 48.8 jit_solution(9644489078398446785)
XLA Ops:
  0.0 0.0 copy-start.1
  0.0 0.0 copy-start.2
  0.0 0.7 %copy-done.2 = s32[2,2,32]{2,1,0:T(2,128)S(1)} copy-done((s32[2,2,32]{2,1,0:T(2,128)S(1)}, s32[2,2,32]{2,1,0:T(2,128)}, u32[]{:S(2)}) %copy-start.2) | copy-done | bytes 536
  0.7 0.0 copy-start
  0.7 1.5 %pick.1 = (bf16[1024,128]{1,0:T(8,128)(2,1)S(1)}, bf16[1024,128]{1,0:T(8,128)(2,1)S(1)}, bf16[1024,128]{1,0:T(8,128)(2,1)S(1)}, bf16[512,128]{1,0:T(8,128)(2,1)S...) custom-call(s32[2,2,32]{2,1,0:T(2,128)S(1)} %copy-done.2, bf16[4,4,1,1024,128]{4,3,2,1,0:T(8,128)(2,1)} %orbitals_ref.1), custom_call_target="tpu_custom_call" | custom-call | tf_op jit(solution)/shard_map/pick/pallas_call | solution.py:120
  2.2 5.5 %collective-permute-start = (bf16[1024,128]{1,0:T(8,128)(2,1)S(1)}, bf16[1024,128]{1,0:T(8,128)(2,1)S(1)}, u32[]{:S(2)}, u32[]{:S(2)}) collective-permute-start(bf16[1024,128]{1,0:T(8,128)(2,1)S(1)} %get-tuple-element.22), channel_id=1, source_target_pairs={{0,23},{1,22},{2,17},{3,16},{4,19},{5,18},{6,21},{7,20},{8,31},{9,... | collective-permute-start | bytes 786440 | tf_op jit(solution)/shard_map/ppermute | solution.py:55
  7.7 0.6 %collective-permute-start.1 = (bf16[1024,128]{1,0:T(8,128)(2,1)S(1)}, bf16[1024,128]{1,0:T(8,128)(2,1)S(1)}, u32[]{:S(2)}, u32[]{:S(2)}) collective-permute-start(bf16[1024,128]{1,0:T(8,128)(2,1)S(1)} %get-tuple-element.24), channel_id=1, source_target_pairs={{0,22},{1,23},{2,16},{3,17},{4,18},{5,19},{6,20},{7,21},{8,30},{9,... | collective-permute-start | bytes 786440 | tf_op jit(solution)/shard_map/ppermute | solution.py:55
  8.4 2.3 %collective-permute-start.6 = (bf16[256,128]{1,0:T(8,128)(2,1)S(1)}, bf16[256,128]{1,0:T(8,128)(2,1)S(1)}, u32[]{:S(2)}, u32[]{:S(2)}) collective-permute-start(bf16[256,128]{1,0:T(8,128)(2,1)S(1)} %get-tuple-element.31), channel_id=1, source_target_pairs={{0,11},{1,10},{2,13},{3,12},{4,15},{5,14},{6,9},{7,8},{8,19},{9,18... | collective-permute-start | bytes 196616 | tf_op jit(solution)/shard_map/ppermute | solution.py:55
  10.6 0.0 collective-permute-start.7
  10.7 1.5 %collective-permute-start.5 = (bf16[512,128]{1,0:T(8,128)(2,1)S(1)}, bf16[512,128]{1,0:T(8,128)(2,1)S(1)}, u32[]{:S(2)}, u32[]{:S(2)}) collective-permute-start(bf16[512,128]{1,0:T(8,128)(2,1)S(1)} %get-tuple-element.30), channel_id=1, source_target_pairs={{0,11},{1,10},{2,13},{3,12},{4,15},{5,14},{6,9},{7,8},{8,19},{9,18... | collective-permute-start | bytes 393224 | tf_op jit(solution)/shard_map/ppermute | solution.py:55
  12.2 0.0 copy-done.1
  12.2 0.8 %masks.1.mask_ref = f32[4,128]{1,0:T(4,128)S(1)} custom-call(s32[2,2,32]{2,1,0:T(2,128)S(1)} %copy-done.2, s32[16,16,2,64]{3,2,1,0:T(2,128)S(1)} %copy-done.1), custom_call_target="tpu_custom_call" | custom-call | tf_op jit(solution)/shard_map/masks/pallas_call | solution.py:166
  13.0 0.0 copy-done
  13.0 1.5 %widen.1.kernel_ref = f32[2,1024,1024]{2,1,0:T(8,128)S(1)} custom-call(bf16[1,2,1024,1024]{3,2,1,0:T(8,128)(2,1)S(1)} %copy-done), custom_call_target="tpu_custom_call" | custom-call | tf_op jit(solution)/shard_map/widen/pallas_call | solution.py:229
  14.5 0.6 %collective-permute-done.second_ref = bf16[1024,128]{1,0:T(8,128)(2,1)S(1)} collective-permute-done((bf16[1024,128]{1,0:T(8,128)(2,1)S(1)}, bf16[1024,128]{1,0:T(8,128)(2,1)S(1)}, u32[]{:S(2)}, u32[]{:S(2)}) %collective-permute-start) | collective-permute-done | bytes 262176 | tf_op jit(solution)/shard_map/ppermute | solution.py:55
  15.1 2.7 %collective-permute-start.4 = (bf16[1024,128]{1,0:T(8,128)(2,1)S(1)}, bf16[1024,128]{1,0:T(8,128)(2,1)S(1)}, u32[]{:S(2)}, u32[]{:S(2)}) collective-permute-start(bf16[1024,128]{1,0:T(8,128)(2,1)S(1)} %get-tuple-element.28), channel_id=1, source_target_pairs={{0,10},{1,11},{2,12},{3,13},{4,14},{5,15},{6,8},{7,9},{8,18},{9,19... | collective-permute-start | bytes 786440 | tf_op jit(solution)/shard_map/ppermute | solution.py:55
  17.8 1.5 %shard_map.46 = (bf16[1024,2048]{1,0:T(8,128)(2,1)S(1)}, bf16[2048,128]{1,0:T(8,128)(2,1)S(1)}) custom-call(f32[4,128]{1,0:T(4,128)S(1)} %masks.1.mask_ref, f32[2,1024,1024]{2,1,0:T(8,128)S(1)} %widen.1.kernel_ref, bf16[1024,128]{1,0:T(8,128)(2,1)S(1)} %collective-permute-done.second_ref), custom_call_target="tpu_custom_call" | custom-call | flops 536870912 | tf_op jit(solution)/shard_map/pallas_call | solution.py:241
  19.4 1.3 %collective-permute-done.1.refs_0_.refs_1_ = bf16[1024,128]{1,0:T(8,128)(2,1)S(1)} collective-permute-done((bf16[1024,128]{1,0:T(8,128)(2,1)S(1)}, bf16[1024,128]{1,0:T(8,128)(2,1)S(1)}, u32[]{:S(2)}, u32[]{:S(2)}) %collective-permute-start.1) | collective-permute-done | bytes 262176 | tf_op jit(solution)/shard_map/ppermute | solution.py:55
  20.7 2.8 %shard_map.47 = bf16[64,128]{1,0:T(8,128)(2,1)S(1)} custom-call(f32[4,128]{1,0:T(4,128)S(1)} %masks.1.mask_ref, f32[2,1024,1024]{2,1,0:T(8,128)S(1)} %widen.1.kernel_ref, bf16[2048,128]{1,0:T(8,128)(2,1)S(1)} %get-tuple-element.23.wide_ref, bf16[1024,128]{1,0:T(8,128)(2,1)S(1)} %collective-permute-done.1.refs_0_.refs_1_), custom_call_target="tpu_custom_call" | custom-call | flops 1610612736 | tf_op jit(solution)/shard_map/pallas_call | solution.py:241
  23.5 1.5 %shard_map.48 = bf16[64,128]{1,0:T(8,128)(2,1)S(1)} custom-call(bf16[1024,2048]{1,0:T(8,128)(2,1)S(1)} %get-tuple-element.25.refs_0_, bf16[1024,128]{1,0:T(8,128)(2,1)S(1)} %collective-permute-done.1.refs_0_.refs_1_), custom_call_target="tpu_custom_call" | custom-call | flops 1073741824 | tf_op jit(solution)/shard_map/pallas_call | solution.py:241
  25.1 0.2 collective-permute-start.2
  25.2 7.8 %collective-permute-done.4.second_ref = bf16[1024,128]{1,0:T(8,128)(2,1)S(1)} collective-permute-done((bf16[1024,128]{1,0:T(8,128)(2,1)S(1)}, bf16[1024,128]{1,0:T(8,128)(2,1)S(1)}, u32[]{:S(2)}, u32[]{:S(2)}) %collective-permute-start.4) | collective-permute-done | bytes 262176 | tf_op jit(solution)/shard_map/ppermute | solution.py:55
  33.1 1.6 %shard_map.49 = (bf16[1024,2048]{1,0:T(8,128)(2,1)S(1)}, bf16[2048,128]{1,0:T(8,128)(2,1)S(1)}) custom-call(f32[4,128]{1,0:T(4,128)S(1)} %masks.1.mask_ref, f32[2,1024,1024]{2,1,0:T(8,128)S(1)} %widen.1.kernel_ref, bf16[1024,128]{1,0:T(8,128)(2,1)S(1)} %collective-permute-done.4.second_ref), custom_call_target="tpu_custom_call" | custom-call | flops 536870912 | tf_op jit(solution)/shard_map/pallas_call | solution.py:241
  34.7 0.0 collective-permute-done.5.refs_0_.refs_1_
  34.7 0.9 %shard_map.50.refs_2_ = f32[512,128]{1,0:T(8,128)S(1)} custom-call(f32[4,128]{1,0:T(4,128)S(1)} %masks.1.mask_ref, f32[2,1024,1024]{2,1,0:T(8,128)S(1)} %widen.1.kernel_ref, bf16[2048,128]{1,0:T(8,128)(2,1)S(1)} %get-tuple-element.29.wide_ref, bf16[512,128]{1,0:T(8,128)(2,1)S(1)} %collective-permute-done.5.refs_0_.refs_1_), custom_call_target="tpu_custom_call" | custom-call | flops 402653184 | tf_op jit(solution)/shard_map/pallas_call | solution.py:241
  35.6 0.0 collective-permute-done.6.refs_1_.refs_2_
  35.6 1.1 %shard_map.51.refs_3_ = f32[768,128]{1,0:T(8,128)S(1)} custom-call(f32[4,128]{1,0:T(4,128)S(1)} %masks.1.mask_ref, f32[2,1024,1024]{2,1,0:T(8,128)S(1)} %widen.1.kernel_ref, bf16[2048,128]{1,0:T(8,128)(2,1)S(1)} %get-tuple-element.29.wide_ref, bf16[512,128]{1,0:T(8,128)(2,1)S(1)} %collective-permute-done.5.refs_0_.refs_1_, ...), custom_call_target="tpu_custom_call" | custom-call | flops 503316480 | tf_op jit(solution)/shard_map/pallas_call | solution.py:241
  36.6 0.7 %shard_map.53.refs_2_ = f32[1024,128]{1,0:T(8,128)S(1)} custom-call(bf16[1024,2048]{1,0:T(8,128)(2,1)S(1)} %get-tuple-element.35.refs_0_, bf16[512,128]{1,0:T(8,128)(2,1)S(1)} %collective-permute-done.5.refs_0_.refs_1_), custom_call_target="tpu_custom_call" | custom-call | flops 536870912 | tf_op jit(solution)/shard_map/pallas_call | solution.py:241
  37.4 0.5 %shard_map.54.refs_4_ = f32[1024,128]{1,0:T(8,128)S(1)} custom-call(bf16[1024,2048]{1,0:T(8,128)(2,1)S(1)} %get-tuple-element.35.refs_0_, bf16[256,128]{1,0:T(8,128)(2,1)S(1)} %collective-permute-done.6.refs_1_.refs_2_, f32[1024,128]{1,0:T(8,128)S(1)} %shard_map.53.refs_2_), custom_call_target="tpu_custom_call", output_to_operand_aliasing={{}: (2, {})} | custom-call | flops 268435456 | tf_op jit(solution)/shard_map/pallas_call | solution.py:241
  37.9 0.0 collective-permute-done.7.refs_2_.refs_3_
  37.9 0.7 %shard_map.55 = bf16[64,128]{1,0:T(8,128)(2,1)S(1)} custom-call(bf16[1024,2048]{1,0:T(8,128)(2,1)S(1)} %get-tuple-element.35.refs_0_, bf16[512,128]{1,0:T(8,128)(2,1)S(1)} %collective-permute-done.5.refs_0_.refs_1_, bf16[256,128]{1,0:T(8,128)(2,1)S(1)} %collective-permute-done.6.refs_1_.refs_2_, bf16[256,128]{1,0:T(8,128)(2,1)S(1)} %collective-permute-done.7.refs_2_.refs_3_, ...), custom_call_target="tpu_custom_call" | custom-call | flops 268435456 | tf_op jit(solution)/shard_map/pallas_call | solution.py:241
  38.7 0.1 collective-permute-start.8
  38.7 1.7 %shard_map.52 = bf16[64,128]{1,0:T(8,128)(2,1)S(1)} custom-call(f32[4,128]{1,0:T(4,128)S(1)} %masks.1.mask_ref, f32[2,1024,1024]{2,1,0:T(8,128)S(1)} %widen.1.kernel_ref, bf16[2048,128]{1,0:T(8,128)(2,1)S(1)} %get-tuple-element.29.wide_ref, bf16[512,128]{1,0:T(8,128)(2,1)S(1)} %collective-permute-done.5.refs_0_.refs_1_, ...), custom_call_target="tpu_custom_call" | custom-call | flops 704643072 | tf_op jit(solution)/shard_map/pallas_call | solution.py:241
  40.4 0.0 collective-permute-done.2
  40.4 2.7 %collective-permute-start.3 = (bf16[2,64,128]{2,1,0:T(8,128)(2,1)S(1)}, bf16[2,64,128]{2,1,0:T(8,128)(2,1)S(1)}, u32[]{:S(2)}, u32[]{:S(2)}) collective-permute-start(bf16[2,64,128]{2,1,0:T(8,128)(2,1)S(1)} %pad_maximum_fusion), channel_id=1, source_target_pairs={{0,19},{1,18},{2,21},{3,20},{4,23},{5,22},{6,17},{7,16},{8,27},{9,... | collective-permute-start | bytes 98312 | tf_op jit(solution)/shard_map/ppermute | solution.py:55
  43.2 0.0 collective-permute-done.8
  43.2 2.3 %collective-permute-start.9 = (bf16[2,64,128]{2,1,0:T(8,128)(2,1)S(1)}, bf16[2,64,128]{2,1,0:T(8,128)(2,1)S(1)}, u32[]{:S(2)}, u32[]{:S(2)}) collective-permute-start(bf16[2,64,128]{2,1,0:T(8,128)(2,1)S(1)} %pad_maximum_fusion.1), channel_id=1, source_target_pairs={{0,30},{1,31},{2,24},{3,25},{4,26},{5,27},{6,28},{7,29},{8,6},{9,7... | collective-permute-start | bytes 98312 | tf_op jit(solution)/shard_map/ppermute | solution.py:55
  45.4 1.2 %collective-permute-done.3.refs_0_ = bf16[2,64,128]{2,1,0:T(8,128)(2,1)S(1)} collective-permute-done((bf16[2,64,128]{2,1,0:T(8,128)(2,1)S(1)}, bf16[2,64,128]{2,1,0:T(8,128)(2,1)S(1)}, u32[]{:S(2)}, u32[]{:S(2)}) %collective-permute-start.3) | collective-permute-done | bytes 32800 | tf_op jit(solution)/shard_map/ppermute | solution.py:55
  46.6 1.0 %base.1 = (f32[4,4,1,64,128]{4,3,2,1,0:T(8,128)}, f32[2,64,128]{2,1,0:T(8,128)S(1)}) custom-call(s32[2,2,32]{2,1,0:T(2,128)S(1)} %copy-done.2, bf16[2,64,128]{2,1,0:T(8,128)(2,1)S(1)} %collective-permute-done.3.refs_0_), custom_call_target="tpu_custom_call" | custom-call | tf_op jit(solution)/shard_map/base/pallas_call | solution.py:413
  47.6 0.4 collective-permute-done.9.pair_ref
  48.0 0.8 %totals.1 = f32[4,4,1,64,128]{4,3,2,1,0:T(8,128)} custom-call(s32[2,2,32]{2,1,0:T(2,128)S(1)} %copy-done.2, f32[2,64,128]{2,1,0:T(8,128)S(1)} %get-tuple-element.26.held_ref, bf16[2,64,128]{2,1,0:T(8,128)(2,1)S(1)} %collective-permute-done.9.pair_ref, f32[4,4,1,64,128]{4,3,2,1,0:T(8,128)} %get-tuple-element.36.base_ref), custom_call_target="tpu_custom_call", output_to_operand_aliasing={{}: (3, {})} | custom-call | tf_op jit(solution)/shard_map/totals/pallas_call | solution.py:448
  (2 shorter events, 0.0 us)
Async XLA Ops:
  0.0 12.2 %copy-start.1 = (s32[16,16,2,64]{3,2,1,0:T(2,128)S(1)}, s32[16,16,2,64]{3,2,1,0:T(2,128)}, u32[]{:S(2)}) copy-start(s32[16,16,2,64]{3,2,1,0:T(2,128)} %occupation_ref.1) | copy-start | bytes 393220
  0.0 0.7 %copy-start.2 = (s32[2,2,32]{2,1,0:T(2,128)S(1)}, s32[2,2,32]{2,1,0:T(2,128)}, u32[]{:S(2)}) copy-start(s32[2,2,32]{2,1,0:T(2,128)} %plan_ref.7) | copy-start | bytes 1540
  0.7 12.3 %copy-start = (bf16[1,2,1024,1024]{3,2,1,0:T(8,128)(2,1)S(1)}, bf16[1,2,1024,1024]{3,2,1,0:T(8,128)(2,1)}, u32[]{:S(2)}) copy-start(bf16[1,2,1024,1024]{3,2,1,0:T(8,128)(2,1)} %kernel_ref) | copy-start | bytes 12582916
  2.2 12.9 %collective-permute-start = (bf16[1024,128]{1,0:T(8,128)(2,1)S(1)}, bf16[1024,128]{1,0:T(8,128)(2,1)S(1)}, u32[]{:S(2)}, u32[]{:S(2)}) collective-permute-start(bf16[1024,128]{1,0:T(8,128)(2,1)S(1)} %get-tuple-element.22), channel_id=1, source_target_pairs={{0,23},{1,22},{2,17},{3,16},{4,19},{5,18},{6,21},{7,20},{8,31},{9,... | collective-permute-start | bytes 786440 | tf_op jit(solution)/shard_map/ppermute | solution.py:55
  7.7 12.9 %collective-permute-start.1 = (bf16[1024,128]{1,0:T(8,128)(2,1)S(1)}, bf16[1024,128]{1,0:T(8,128)(2,1)S(1)}, u32[]{:S(2)}, u32[]{:S(2)}) collective-permute-start(bf16[1024,128]{1,0:T(8,128)(2,1)S(1)} %get-tuple-element.24), channel_id=1, source_target_pairs={{0,22},{1,23},{2,16},{3,17},{4,18},{5,19},{6,20},{7,21},{8,30},{9,... | collective-permute-start | bytes 786440 | tf_op jit(solution)/shard_map/ppermute | solution.py:55
  8.4 27.2 %collective-permute-start.6 = (bf16[256,128]{1,0:T(8,128)(2,1)S(1)}, bf16[256,128]{1,0:T(8,128)(2,1)S(1)}, u32[]{:S(2)}, u32[]{:S(2)}) collective-permute-start(bf16[256,128]{1,0:T(8,128)(2,1)S(1)} %get-tuple-element.31), channel_id=1, source_target_pairs={{0,11},{1,10},{2,13},{3,12},{4,15},{5,14},{6,9},{7,8},{8,19},{9,18... | collective-permute-start | bytes 196616 | tf_op jit(solution)/shard_map/ppermute | solution.py:55
  10.6 27.3 %collective-permute-start.7 = (bf16[256,128]{1,0:T(8,128)(2,1)S(1)}, bf16[256,128]{1,0:T(8,128)(2,1)S(1)}, u32[]{:S(2)}, u32[]{:S(2)}) collective-permute-start(bf16[256,128]{1,0:T(8,128)(2,1)S(1)} %get-tuple-element.32), channel_id=1, source_target_pairs={{0,11},{1,10},{2,13},{3,12},{4,15},{5,14},{6,9},{7,8},{8,19},{9,18... | collective-permute-start | bytes 196616 | tf_op jit(solution)/shard_map/ppermute | solution.py:55
  10.7 24.0 %collective-permute-start.5 = (bf16[512,128]{1,0:T(8,128)(2,1)S(1)}, bf16[512,128]{1,0:T(8,128)(2,1)S(1)}, u32[]{:S(2)}, u32[]{:S(2)}) collective-permute-start(bf16[512,128]{1,0:T(8,128)(2,1)S(1)} %get-tuple-element.30), channel_id=1, source_target_pairs={{0,11},{1,10},{2,13},{3,12},{4,15},{5,14},{6,9},{7,8},{8,19},{9,18... | collective-permute-start | bytes 393224 | tf_op jit(solution)/shard_map/ppermute | solution.py:55
  15.1 18.0 %collective-permute-start.4 = (bf16[1024,128]{1,0:T(8,128)(2,1)S(1)}, bf16[1024,128]{1,0:T(8,128)(2,1)S(1)}, u32[]{:S(2)}, u32[]{:S(2)}) collective-permute-start(bf16[1024,128]{1,0:T(8,128)(2,1)S(1)} %get-tuple-element.28), channel_id=1, source_target_pairs={{0,10},{1,11},{2,12},{3,13},{4,14},{5,15},{6,8},{7,9},{8,18},{9,19... | collective-permute-start | bytes 786440 | tf_op jit(solution)/shard_map/ppermute | solution.py:55
  25.1 15.4 %collective-permute-start.2 = (bf16[64,128]{1,0:T(8,128)(2,1)S(1)}, bf16[64,128]{1,0:T(8,128)(2,1)S(1)}, u32[]{:S(2)}, u32[]{:S(2)}) collective-permute-start(bf16[64,128]{1,0:T(8,128)(2,1)S(1)} %shard_map.48), channel_id=1, source_target_pairs={{0,1},{1,0},{2,3},{3,2},{4,5},{5,4},{6,7},{7,6},{8,9},{9,8},{10,11... | collective-permute-start | bytes 49160 | tf_op jit(solution)/shard_map/ppermute | solution.py:55
  38.7 4.5 %collective-permute-start.8 = (bf16[64,128]{1,0:T(8,128)(2,1)S(1)}, bf16[64,128]{1,0:T(8,128)(2,1)S(1)}, u32[]{:S(2)}, u32[]{:S(2)}) collective-permute-start(bf16[64,128]{1,0:T(8,128)(2,1)S(1)} %shard_map.55), channel_id=1, source_target_pairs={{0,1},{1,0},{2,3},{3,2},{4,5},{5,4},{6,7},{7,6},{8,9},{9,8},{10,11... | collective-permute-start | bytes 49160 | tf_op jit(solution)/shard_map/ppermute | solution.py:55
  40.4 6.2 %collective-permute-start.3 = (bf16[2,64,128]{2,1,0:T(8,128)(2,1)S(1)}, bf16[2,64,128]{2,1,0:T(8,128)(2,1)S(1)}, u32[]{:S(2)}, u32[]{:S(2)}) collective-permute-start(bf16[2,64,128]{2,1,0:T(8,128)(2,1)S(1)} %pad_maximum_fusion), channel_id=1, source_target_pairs={{0,19},{1,18},{2,21},{3,20},{4,23},{5,22},{6,17},{7,16},{8,27},{9,... | collective-permute-start | bytes 98312 | tf_op jit(solution)/shard_map/ppermute | solution.py:55
  43.2 4.9 %collective-permute-start.9 = (bf16[2,64,128]{2,1,0:T(8,128)(2,1)S(1)}, bf16[2,64,128]{2,1,0:T(8,128)(2,1)S(1)}, u32[]{:S(2)}, u32[]{:S(2)}) collective-permute-start(bf16[2,64,128]{2,1,0:T(8,128)(2,1)S(1)} %pad_maximum_fusion.1), channel_id=1, source_target_pairs={{0,30},{1,31},{2,24},{3,25},{4,26},{5,27},{6,28},{7,29},{8,6},{9,7... | collective-permute-start | bytes 98312 | tf_op jit(solution)/shard_map/ppermute | solution.py:55
